TPU v7x, 32 devices: a whole 2x2x4 slice. The times are simulated.
32 devices in a mesh: groups: 2 (over y), seq: 4 (over z), dp: 2 (over x), mp: 2 (over core).
Axes of the slice: x: 2, y: 2, z: 4, core: 2. Of those that a mesh axis runs over, the one named last changes fastest.
Arguments:
- tiles: bfloat16 [160, 8, 8, 768], P(('groups', 'seq', 'dp')), parts along dimension 0, may hold values from -6 to 6
- token_grad: bfloat16 [160, 8, 8, 768], P(('groups', 'seq', 'dp')), parts along dimension 0, may hold values from -1.5 to 1.5
- embed_grad: bfloat16 [2, 80, 768], P('dp', 'groups', 'seq'), parts along dimension 1, may hold values from -48 to 48
- live_tiles: int32 [16], P(('groups', 'seq', 'dp')), parts along dimension 0, may hold values from 1 to 10, 60 in all
- dw_kernel: float32 [7, 7, 768], replicated, may hold values from -0.875 to 0.875
- dw_bias: float32 [768], replicated, may hold values from -3 to 3
- ln_gain: float32 [768], replicated, may hold values from 0.1 to 1.9
- ln_bias: float32 [768], replicated, may hold values from -2 to 2
- w_up: bfloat16 [768, 2560], P('seq', 'mp'), may hold values from -0.21875 to 0.21875
- b_up: float32 [2560], P('mp'), may hold values from -3 to 3
- w_down: bfloat16 [768, 2560], P('seq', 'mp'), may hold values from -0.125 to 0.125
- layer_scale: float32 [768], replicated, may hold values from 0.3 to 1.5
Outputs:
- tile_grad: bfloat16 [160, 8, 8, 768], P(('groups', 'seq', 'dp')), parts along dimension 0
- grad_up: float32 [1536, 2560], P(('groups', 'seq'), 'mp'), parts along dimension 0
- grad_down: float32 [1536, 2560], P(('groups', 'seq'), 'mp'), parts along dimension 0
There are 2 independent parts, one for each index of `groups`. A program takes and returns all parts, laid end to end along the dimension named above; an argument that names none is the same for every part. Nothing has to cross between parts.
Inputs may be any that keep to these rules, and one draw needn't show every extreme that they name: Each loader's foreground tiles fill its slots 0 to live_tiles - 1 of 10; some loader has all 10.
All inputs are finite; a program needn't handle non-finite values. No bound on the sum of `live_tiles` on one device may be relied on, other than what follows from the above.
Results may differ from a plain program's by a relative error of at most 0.01.
Values may be sent and summed in bfloat16 or wider, within the bound.
No kernel may reach another device: no remote copies, remote signals or barrier semaphores. Data moves between devices by JAX's collectives and lax.ppermute only.
A program may use at most 64 MiB of HBM per device.

v0:
```python
import jax
import jax.numpy as jnp
from jax import lax
from jax.sharding import PartitionSpec as P

sqrt_two_pi = 0.7978845608028654
cubic_coef = 0.044715


def depthwise(values, kernel):
    reach = kernel.shape[0]
    margin = reach // 2
    height = values.shape[1]
    padded = jnp.pad(values, ((0, 0), (margin, margin), (margin, margin), (0, 0)))
    total = jnp.zeros(values.shape, jnp.float32)
    for row_off in range(reach):
        for col_off in range(reach):
            total = (
                total
                + padded[:, row_off : row_off + height, col_off : col_off + height, :]
                * kernel[row_off, col_off]
            )
    return total


def gelu_tanh(values):
    inner = sqrt_two_pi * (values + cubic_coef * values * values * values)
    return 0.5 * values * (1.0 + jnp.tanh(inner))


def gelu_slope(values):
    tangent = jnp.tanh(sqrt_two_pi * (values + cubic_coef * values * values * values))
    return 0.5 * (1.0 + tangent) + 0.5 * values * (1.0 - tangent * tangent) * sqrt_two_pi * (
        1.0 + 3.0 * cubic_coef * values * values
    )


def normalize(values):
    center = jnp.mean(values, axis=-1, keepdims=True)
    shifted = values - center
    spread = jnp.sqrt(jnp.mean(shifted * shifted, axis=-1, keepdims=True) + 1e-06)
    return (shifted / spread, spread)


def norm_backward(normed_grad, normal, spread, ln_gain):
    scaled = normed_grad * ln_gain
    return (
        scaled
        - jnp.mean(scaled, axis=-1, keepdims=True)
        - normal * jnp.mean(scaled * normal, axis=-1, keepdims=True)
    ) / spread


def on_device(
    tiles,
    token_grad,
    embed_grad,
    live_tiles,
    dw_kernel,
    dw_bias,
    ln_gain,
    ln_bias,
    w_up,
    b_up,
    w_down,
    layer_scale,
):
    count = tiles.shape[0]
    height = tiles.shape[1]
    width = tiles.shape[3]
    flipped = dw_kernel[::-1, ::-1, :]
    arrived = lax.all_to_all(embed_grad[0], "seq", split_axis=0, concat_axis=1, tiled=True)
    live = (jnp.arange(count) < live_tiles[0]).astype(jnp.float32)[:, None, None, None]
    pooled = arrived.astype(jnp.float32)[:, None, None, :] * live
    out_grad = live * token_grad.astype(jnp.float32) + pooled / (height * height)
    branch_grad = (layer_scale * out_grad).astype(jnp.bfloat16).reshape(-1, width)
    conv = depthwise(tiles.astype(jnp.float32), dw_kernel) + dw_bias
    normal, spread = normalize(conv)
    normed = (normal * ln_gain + ln_bias).astype(jnp.bfloat16)
    rows = normed.reshape(-1, width)
    full_up, full_down = (
        lax.all_gather(w_up, "seq", axis=0, tiled=True),
        lax.all_gather(w_down, "seq", axis=0, tiled=True),
    )
    hidden = jnp.dot(rows, full_up, preferred_element_type=jnp.float32) + b_up
    act = gelu_tanh(hidden).astype(jnp.bfloat16)
    act_grad = jnp.dot(branch_grad, full_down, preferred_element_type=jnp.float32)
    hidden_grad = (act_grad * gelu_slope(hidden)).astype(jnp.bfloat16)
    normed_part = lax.dot_general(
        hidden_grad, full_up, (((1,), (1,)), ((), ())), preferred_element_type=jnp.float32
    )
    part_down = lax.dot_general(
        branch_grad, act, (((0,), (0,)), ((), ())), preferred_element_type=jnp.float32
    )
    part_up = lax.dot_general(
        rows, hidden_grad, (((0,), (0,)), ((), ())), preferred_element_type=jnp.float32
    )
    up_piece, down_piece = (
        lax.psum_scatter(
            part_up.astype(jnp.bfloat16), "seq", scatter_dimension=0, tiled=True
        ).astype(jnp.float32),
        lax.psum_scatter(
            part_down.astype(jnp.bfloat16), "seq", scatter_dimension=0, tiled=True
        ).astype(jnp.float32),
    )
    grad_up, grad_down = (
        lax.psum(up_piece.astype(jnp.bfloat16), "dp").astype(jnp.float32),
        lax.psum(down_piece.astype(jnp.bfloat16), "dp").astype(jnp.float32),
    )
    normed_grad = lax.psum(normed_part.astype(jnp.bfloat16), "mp").astype(jnp.float32)
    conv_grad = norm_backward(normed_grad.reshape(conv.shape), normal, spread, ln_gain)
    tile_grad = (out_grad + depthwise(conv_grad, flipped)).astype(jnp.bfloat16)
    return (tile_grad, grad_up, grad_down)


def solution(mesh):
    return jax.shard_map(
        on_device,
        mesh=mesh,
        in_specs=(
            P(("groups", "seq", "dp"), None, None, None),
            P(("groups", "seq", "dp"), None, None, None),
            P("dp", "groups", "seq"),
            P(("groups", "seq", "dp")),
            P(),
            P(),
            P(),
            P(),
            P("seq", "mp"),
            P("mp"),
            P("seq", "mp"),
            P(),
        ),
        out_specs=(
            P(("groups", "seq", "dp"), None, None, None),
            P(("groups", "seq"), "mp"),
            P(("groups", "seq"), "mp"),
        ),
        check_vma=False,
    )
```

profile of v0, /device:TPU:0, one launch (start us, length us, event | category | flops | bytes accessed | tf_op | source)
XLA Modules:
  0.0 267.0 jit_solution(10190657379910288535)
XLA Ops:
  7.2 0.0 all-gather.5.cloned.1.call-start
  7.2 0.7 all-gather.5.cloned.1.call-update
  7.9 0.7 all_to_all.10
  8.7 0.7 reshape.223
  9.4 6.5 %all-to-all-start = ((bf16[4,2,960]{2,1,0:T(2,128)(2,1)}), bf16[4,2,960]{2,1,0:T(2,128)(2,1)S(1)}, u32[]{:S(2)}, u32[]{:S(2)}) async-start(bf16[4,2,960]{2,1,0:T(2,128)(2,1)} %reshape.223), calls=%async_computation | async-start | bytes 32768 | tf_op jit(solution)/shard_map/all_to_all | solution.py:72
  15.8 0.0 all-gather.3.cloned.1.call-start
  15.8 0.7 all-gather.3.cloned.1.call-update
  16.6 0.0 all-reduce.6.cloned.1.call-start
  16.6 1.1 slice_reduce_fusion.46
  17.7 1.4 slice_reduce_fusion.48
  19.1 1.4 slice_reduce_fusion.47
  20.5 0.2 convert_element_type.70
  20.7 13.0 %fusion.209 = (f32[10,8,8]{2,1,0:T(8,128)S(1)}, f32[10,8,8,768]{3,2,1,0:T(8,128)S(1)}) fusion(f32[768]{0:T(1024)S(1)} %copy-done.5, f32[768]{0:T(1024)S(1)} %get-tuple-element.50, f32[768]{0:T(1024)S(1)} %get-tuple-element.51, f32[768]{0:T(1024)S(1)} %get-tuple-element.4, f32[768]{0:T(1024)S(1)} %get-tuple-element.5, f32[768]{0:T(1024)S(1)} %get-tuple-element.6, ...), kind=kLoop, calls=%fused_computation.377 | loop fusion | flops 48659840 | bytes 4088320 | tf_op jit(solution)/shard_map/reduce_sum | solution.py:39
  34.4 0.3 multiply_reduce_fusion.2
  34.7 0.0 copy-start
  34.7 0.0 copy-start.4
  34.8 1.3 add_convert_fusion
  36.1 0.0 all-to-all-done
  36.1 0.1 reshape.224
  36.3 0.1 reshape.173
  36.4 0.1 multiply_multiply_fusion.1
  36.4 1.3 multiply_convert_fusion.1
  37.7 18.1 %all-gather.5.cloned.1.call-done = bf16[768,1280]{1,0:T(8,128)(2,1)} async-done(((bf16[192,1280]{1,0:T(8,128)(2,1)}), bf16[768,1280]{1,0:T(8,128)(2,1)}) %all-gather.5.cloned.1.call-update) | async-done | bytes 1966096 | tf_op jit(solution)/shard_map/all_gather | solution.py:82
  55.9 5.0 %convolution_add_fusion = f32[640,1280]{1,0:T(8,128)} fusion(bf16[640,768]{1,0:T(8,128)(2,1)} %bitcast.18, bf16[768,1280]{1,0:T(8,128)(2,1)} %all-gather.5.cloned.1.call-done, f32[1280]{0:T(1024)S(1)} %copy-done.7), kind=kOutput, calls=%fused_computation.99 | convolution fusion | flops 1259110400 | bytes 6231040 | tf_op jit(solution)/shard_map/dot_general | solution.py:85
  60.9 39.0 %all-gather.3.cloned.1.call-done = bf16[768,1280]{1,0:T(8,128)(2,1)} async-done(((bf16[192,1280]{1,0:T(8,128)(2,1)}), bf16[768,1280]{1,0:T(8,128)(2,1)}) %all-gather.3.cloned.1.call-update) | async-done | bytes 1966096 | tf_op jit(solution)/shard_map/all_gather | solution.py:83
  99.9 5.7 %fusion.5 = bf16[640,1280]{1,0:T(8,128)(2,1)S(1)} fusion(f32[640,1280]{1,0:T(8,128)} %convolution_add_fusion, bf16[640,768]{1,0:T(8,128)(2,1)} %bitcast.20, bf16[768,1280]{1,0:T(8,128)(2,1)} %all-gather.3.cloned.1.call-done), kind=kOutput, calls=%fused_computation.108 | convolution fusion | flops 1273856000 | bytes 7864320 | tf_op jit(solution)/shard_map/dot_general | solution.py:87
  105.6 1.2 copy-done.8
  106.8 2.4 convolution_convert_fusion.2
  109.2 0.0 all-reduce.6.cloned.1.call-update
  109.2 0.0 reduce-scatter.3.cloned.1.call-start
  109.3 4.8 %convolution_convert_fusion.1 = bf16[768,1280]{1,0:T(8,128)(2,1)} fusion(bf16[640,768]{1,0:T(8,128)(2,1)} %bitcast.19, bf16[640,1280]{1,0:T(8,128)(2,1)} %copy-done.8), kind=kOutput, calls=%fused_computation.101 | convolution fusion | flops 1259274240 | bytes 4587520 | tf_op jit(solution)/shard_map/dot_general | solution.py:95
  114.1 0.0 reduce-scatter.3.cloned.1.call-update
  114.1 0.2 reduce-scatter.5.cloned.1.call-start
  114.3 5.5 %convolution_convert_fusion = bf16[768,1280]{1,0:T(8,128)(2,1)} fusion(bf16[640,768]{1,0:T(8,128)(2,1)} %bitcast.21, f32[640,1280]{1,0:T(8,128)} %convolution_add_fusion), kind=kOutput, calls=%fused_computation.100 | convolution fusion | flops 1266647040 | bytes 6225920 | tf_op jit(solution)/shard_map/dot_general | solution.py:92
  119.9 0.0 reduce-scatter.5.cloned.1.call-update
  119.9 0.0 all-reduce.8.cloned.1.call-start
  119.9 7.8 %all-reduce.6.cloned.1.call-done = bf16[640,768]{1,0:T(8,128)(2,1)} async-done(((bf16[640,768]{1,0:T(8,128)(2,1)}), bf16[640,768]{1,0:T(8,128)(2,1)}) %all-reduce.6.cloned.1.call-update) | async-done | bytes 983056 | tf_op jit(solution)/shard_map/psum | solution.py:110
  127.7 1.5 multiply_reduce_fusion.1
  129.2 0.1 div.41
  129.3 1.8 multiply_reduce_fusion
  131.1 1.9 subtract_divide_fusion
  133.0 39.7 %reduce-scatter.3.cloned.1.call-done = bf16[192,1280]{1,0:T(8,128)(2,1)} async-done(((bf16[768,1280]{1,0:T(8,128)(2,1)}), bf16[192,1280]{1,0:T(8,128)(2,1)}) %reduce-scatter.3.cloned.1.call-update) | async-done | bytes 491536 | tf_op jit(solution)/shard_map/reduce_scatter | solution.py:99
  172.7 43.0 %reduce-scatter.5.cloned.1.call-done = bf16[192,1280]{1,0:T(8,128)(2,1)} async-done(((bf16[768,1280]{1,0:T(8,128)(2,1)}), bf16[192,1280]{1,0:T(8,128)(2,1)}) %reduce-scatter.5.cloned.1.call-update) | async-done | bytes 491536 | tf_op jit(solution)/shard_map/reduce_scatter | solution.py:102
  215.6 0.0 all-reduce.8.cloned.1.call-update
  215.7 38.3 %fusion.200 = bf16[10,8,8,768]{3,2,1,0:T(8,128)(2,1)} fusion(f32[10,8,8,768]{3,2,1,0:T(8,128)} %subtract_divide_fusion, bf16[10,8,8,768]{3,2,1,0:T(8,128)(2,1)S(1)} %copy-done, f32[768]{0:T(1024)S(1)} %get-tuple-element.50, f32[768]{0:T(1024)S(1)} %get-tuple-element.51, f32[768]{0:T(1024)S(1)} %get-tuple-element.4, f32[768]{0:T(1024)S(1)} %get-tuple-element.5, ...), kind=kLoop, calls=%fused_computation.310 | loop fusion | flops 50135040 | bytes 4113448 | tf_op jit(solution)/shard_map/convert_element_type | solution.py:112
  254.0 2.1 all-reduce.8.cloned.1.call-done
  256.1 2.0 convert_element_type.77
  258.1 2.0 convert_element_type.80
  (22 shorter events, 0.1 us)
Async XLA Ops:
  7.2 13.3 %copy-start.1 = (bf16[10,8,8,768]{3,2,1,0:T(8,128)(2,1)S(1)}, bf16[10,8,8,768]{3,2,1,0:T(8,128)(2,1)}, u32[]{:S(2)}) copy-start(bf16[10,8,8,768]{3,2,1,0:T(8,128)(2,1)} %param.12) | copy-start | bytes 2949124
  7.2 48.7 %all-gather.5.cloned.1.call-start = ((), (), s32[]{:S(2)}) async-start(), calls=%async_computation.4 | async-start | bytes 2457600 | tf_op jit(solution)/shard_map/all_gather | solution.py:82
  9.4 11.3 %copy-start.5 = (f32[768]{0:T(1024)S(1)}, f32[768]{0:T(1024)}, u32[]{:S(2)}) copy-start(f32[768]{0:T(1024)} %param.17) | copy-start | bytes 9220
  9.4 26.7 %all-to-all-start = ((bf16[4,2,960]{2,1,0:T(2,128)(2,1)}), bf16[4,2,960]{2,1,0:T(2,128)(2,1)S(1)}, u32[]{:S(2)}, u32[]{:S(2)}) async-start(bf16[4,2,960]{2,1,0:T(2,128)(2,1)} %reshape.223), calls=%async_computation | async-start | bytes 32768 | tf_op jit(solution)/shard_map/all_to_all | solution.py:72
  15.8 84.0 %all-gather.3.cloned.1.call-start = ((), (), s32[]{:S(2)}) async-start(), calls=%async_computation.3 | async-start | bytes 2457600 | tf_op jit(solution)/shard_map/all_gather | solution.py:83
  16.6 111.2 %all-reduce.6.cloned.1.call-start = ((), (), s32[]{:S(2)}) async-start(), calls=%async_computation.5 | async-start | bytes 1966080 | tf_op jit(solution)/shard_map/psum | solution.py:110
  33.6 1.1 copy-start.2
  33.7 1.1 copy-start.3
  34.7 1.7 copy-start
  34.7 1.7 copy-start.4
  36.1 19.8 %copy-start.7 = (f32[1280]{0:T(1024)S(1)}, f32[1280]{0:T(1024)}, u32[]{:S(2)}) copy-start(f32[1280]{0:T(1024)} %param.21) | copy-start | bytes 15364
  99.9 6.9 %copy-start.6 = (bf16[768,1280]{1,0:T(8,128)(2,1)S(1)}, bf16[768,1280]{1,0:T(8,128)(2,1)}, u32[]{:S(2)}) copy-start(bf16[768,1280]{1,0:T(8,128)(2,1)} %all-gather.5.cloned.1.call-done) | copy-start | bytes 5898244
  105.5 1.2 copy-start.8
  109.2 63.4 %reduce-scatter.3.cloned.1.call-start = ((), (), s32[]{:S(2)}) async-start(), calls=%async_computation.6 | async-start | bytes 2457600 | tf_op jit(solution)/shard_map/reduce_scatter | solution.py:99
  114.1 101.5 %reduce-scatter.5.cloned.1.call-start = ((), (), s32[]{:S(2)}) async-start(), calls=%async_computation.7 | async-start | bytes 2457600 | tf_op jit(solution)/shard_map/reduce_scatter | solution.py:102
  119.9 136.2 %all-reduce.8.cloned.1.call-start = ((), (), s32[]{:S(2)}) async-start(), calls=%async_computation.8 | async-start | bytes 1966080 | tf_op jit(solution)/shard_map/psum | solution.py:107
Sparse Core Ops, SparseCore 0:
  9.6 46.2 all-gather.4
  57.4 42.3 all-gather.2
  109.3 18.3 all-reduce.5
  130.0 42.6 reduce-scatter.2
  174.9 40.6 reduce-scatter.4
  218.0 38.0 all-reduce.7
where the time goes:
time: 268 us; the launch traced here: 267 us
  waiting for transfers between devices  151 us (56%)
  other arithmetic  63.8 us (24%)
  matrix products  23.4 us (9%)
  between operations  14.9 us (6%)
  local copies, waits for them, and re-layouts  6.86 us (3%)
  starting transfers between devices  6.85 us (3%)
    reduce_scatter x1, waiting for transfers between devices, on_device(): lax.psum_scatter(part_down.astype(jnp.bfloat16), 'seq', scatter_dimension...  43 us
    reduce_scatter x1, waiting for transfers between devices, on_device(): lax.psum_scatter(part_up.astype(jnp.bfloat16), 'seq', scatter_dimension=0...  39.7 us
    all_gather x1, waiting for transfers between devices, on_device(): lax.all_gather(w_down, 'seq', axis=0, tiled=True)  39 us
    convert_element_type x1, other arithmetic, on_device(): tile_grad = (out_grad + depthwise(conv_grad, flipped)).astype(jnp.bfloat16)  38.3 us
    all_gather x1, waiting for transfers between devices, on_device(): lax.all_gather(w_up, 'seq', axis=0, tiled=True)  18.1 us
    reduce_sum x1, other arithmetic, normalize(): center = jnp.mean(values, axis=-1, keepdims=True)  13 us
    psum x1, waiting for transfers between devices, on_device(): lax.psum(normed_part.astype(jnp.bfloat16), 'mp').astype(jnp.float32)  7.78 us
    all_to_all x1, starting transfers between devices, on_device(): lax.all_to_all(embed_grad[0], 'seq', split_axis=0, concat_axis=1, tiled=T...  6.46 us
  transfers between devices with their start and end apart: 7, of which 6 were waited for; matrix products, arithmetic and copies ran while one was open for 30% of the time, Pallas kernels for 0%

commit v1 on v0

v1 whole, which is shorter than its diff:
```python
import functools
import jax
import jax.numpy as jnp
from jax import lax
from jax.experimental import pallas as pl
from jax.experimental.pallas import tpu as pltpu
from jax.sharding import PartitionSpec as P

sqrt_two_pi = 0.7978845608028654
cubic_coef = 0.044715
LANES = 128
F32 = jnp.float32
BF16 = jnp.bfloat16
WHOLE = pl.BlockSpec(memory_space=pltpu.VMEM)
SCALARS = pl.BlockSpec(memory_space=pltpu.SMEM)
APART = pl.BlockSpec(memory_space=pl.ANY)


def depthwise_lanes(rows, taps_ref, lanes, reach, flip):
    height, width = len(rows), rows[0].shape[0]
    margin = reach // 2
    place = lax.broadcasted_iota(jnp.int32, rows[0].shape, 0)
    total = [None] * height
    for col in range(reach):
        shift = col - margin
        if shift:
            inside = (place + shift >= 0) & (place + shift < width)
            moved = [jnp.where(inside, pltpu.roll(row, (-shift) % width, 0), 0.0) for row in rows]
        else:
            moved = rows
        for line in range(reach):
            index = line * reach + col
            if flip:
                index = reach * reach - 1 - index
            tap = jnp.broadcast_to(taps_ref[pl.ds(index, 1), lanes], rows[0].shape)
            for u in range(height):
                source = u + line - margin
                if 0 <= source < height:
                    term = moved[source] * tap
                    total[u] = term if total[u] is None else total[u] + term
    return total


def front_kernel(reach, base_ref, tiles_ref, taps_ref, bias_ref, gain_ref, shift_ref, normed_ref, normal_ref, inv_ref, conv_ref):
    height, width = tiles_ref.shape[1:3]
    channels = tiles_ref.shape[3]

    def slab(block, carry):
        lanes = pl.ds(pl.multiple_of(block * LANES, LANES), LANES)
        rows = [tiles_ref[0, u, :, lanes].astype(F32) for u in range(height)]
        total = depthwise_lanes(rows, taps_ref, lanes, reach, False)
        for u in range(height):
            conv_ref[u * width : (u + 1) * width, lanes] = total[u] + bias_ref[:, lanes]
        return carry

    lax.fori_loop(0, channels // LANES, slab, 0)
    conv = conv_ref[...]
    center = jnp.mean(conv, axis=-1, keepdims=True)
    shifted = conv - center
    inv = lax.rsqrt(jnp.mean(shifted * shifted, axis=-1, keepdims=True) + 1e-06)
    normal = shifted * inv
    normal_ref[...] = normal
    inv_ref[...] = jnp.broadcast_to(inv, inv_ref.shape)
    normed_ref[...] = (normal * gain_ref[...] + shift_ref[...]).astype(BF16)


def front(base, tiles, taps, bias, gain, shift, mine, reach):
    _, height, width, channels = tiles.shape
    spots = height * width
    one = lambda i, b: (0, 0)
    return pl.pallas_call(
        functools.partial(front_kernel, reach),
        name="conv_norm",
        out_shape=(
            jax.ShapeDtypeStruct((mine * spots, channels), BF16),
            jax.ShapeDtypeStruct((mine * spots, channels), F32),
            jax.ShapeDtypeStruct((mine * spots, LANES), F32),
        ),
        grid_spec=pltpu.PrefetchScalarGridSpec(
            num_scalar_prefetch=1,
            grid=(mine,),
            in_specs=[
                pl.BlockSpec((1, height, width, channels), lambda i, b: (b[0] + i, 0, 0, 0)),
                pl.BlockSpec(taps.shape, one),
                pl.BlockSpec((1, channels), one),
                pl.BlockSpec((1, channels), one),
                pl.BlockSpec((1, channels), one),
            ],
            out_specs=[
                pl.BlockSpec((spots, channels), lambda i, b: (i, 0)),
                pl.BlockSpec((spots, channels), lambda i, b: (i, 0)),
                pl.BlockSpec((spots, LANES), lambda i, b: (i, 0)),
            ],
            scratch_shapes=[pltpu.VMEM((spots, channels), F32)],
        ),
    )(base, tiles, taps, bias, gain, shift)


def gather_rows(at_ref, pieces, whole_ref, sems):
    rows = pieces[0].shape[0]
    copies = [
        pltpu.make_async_copy(piece, whole_ref.at[pl.ds(pl.multiple_of(at_ref[k], 16), rows)], sems.at[k])
        for k, piece in enumerate(pieces)
    ]
    for copy in copies:
        copy.start()
    for copy in copies:
        copy.wait()


def across_rows(left, right):
    return lax.dot_general(left, right, (((0,), (0,)), ((), ())), preferred_element_type=F32)


ROWS = 32


def up_kernel(count, at_ref, own_n, other_n, own_b, other_b, bias_ref, *rest):
    pieces, (slope_ref, down_ref, weight_ref, hidden_ref, act_ref, sems) = rest[:count], rest[count:]
    gather_rows(at_ref, pieces, weight_ref, sems)
    rows = own_n.shape[0]
    for half, normed in enumerate((own_n, other_n)):
        hidden_ref[...] = jnp.dot(normed[...], weight_ref[...], preferred_element_type=F32)

        def block(i, carry):
            here = pl.ds(pl.multiple_of(i * ROWS, ROWS), ROWS)
            value = hidden_ref[here, :] + bias_ref[...]
            square = value * value
            tangent = jnp.tanh(value * (sqrt_two_pi + (sqrt_two_pi * cubic_coef) * square))
            upper = 0.5 + 0.5 * tangent
            act_ref[half, here, :] = (value * upper).astype(BF16)
            bend = (0.5 * value) * (1.0 - tangent * tangent)
            slope = upper + bend * (sqrt_two_pi + (3.0 * sqrt_two_pi * cubic_coef) * square)
            slope_ref[half, here, :] = slope
            return carry

        lax.fori_loop(0, rows // ROWS, block, 0)
    down_ref[...] = (across_rows(own_b[...], act_ref[0]) + across_rows(other_b[...], act_ref[1])).astype(BF16)


def up(at, own_n, other_n, own_b, other_b, bias, pieces):
    rows, channels = own_n.shape
    columns = pieces[0].shape[1]
    return pl.pallas_call(
        functools.partial(up_kernel, len(pieces)),
        name="up_and_down_grad",
        out_shape=(
            jax.ShapeDtypeStruct((2, rows, columns), F32),
            jax.ShapeDtypeStruct((channels, columns), BF16),
            jax.ShapeDtypeStruct((channels, columns), BF16),
        ),
        in_specs=[SCALARS] + [WHOLE] * 5 + [APART] * len(pieces),
        out_specs=[WHOLE] * 3,
        scratch_shapes=[
            pltpu.VMEM((rows, columns), F32),
            pltpu.VMEM((2, rows, columns), BF16),
            pltpu.SemaphoreType.DMA((len(pieces),)),
        ],
        compiler_params=pltpu.CompilerParams(vmem_limit_bytes=40 << 20),
    )(at, own_n, other_n, own_b, other_b, bias, *pieces)


def down_kernel(count, at_ref, own_n, other_n, own_b, other_b, slope_ref, *rest):
    pieces, (grad_ref, up_ref, weight_ref, acted_ref, sems) = rest[:count], rest[count:]
    gather_rows(at_ref, pieces, weight_ref, sems)
    rows = own_n.shape[0]
    for half, branch in enumerate((own_b, other_b)):
        acted_ref[...] = jnp.dot(branch[...], weight_ref[...], preferred_element_type=F32)

        def block(i, carry):
            here = pl.ds(pl.multiple_of(i * ROWS, ROWS), ROWS)
            grad_ref[half, here, :] = (acted_ref[here, :] * slope_ref[half, here, :]).astype(BF16)
            return carry

        lax.fori_loop(0, rows // ROWS, block, 0)
    up_ref[...] = (across_rows(own_n[...], grad_ref[0]) + across_rows(other_n[...], grad_ref[1])).astype(BF16)


def down(at, own_n, other_n, own_b, other_b, slope, pieces):
    rows, channels = own_n.shape
    columns = pieces[0].shape[1]
    return pl.pallas_call(
        functools.partial(down_kernel, len(pieces)),
        name="hidden_and_up_grad",
        out_shape=(
            jax.ShapeDtypeStruct((2, rows, columns), BF16),
            jax.ShapeDtypeStruct((channels, columns), BF16),
        ),
        in_specs=[SCALARS] + [WHOLE] * 5 + [APART] * len(pieces),
        out_specs=[WHOLE] * 2,
        scratch_shapes=[
            pltpu.VMEM((channels, columns), BF16),
            pltpu.VMEM((rows, columns), F32),
            pltpu.SemaphoreType.DMA((len(pieces),)),
        ],
        compiler_params=pltpu.CompilerParams(vmem_limit_bytes=40 << 20),
    )(at, own_n, other_n, own_b, other_b, slope, *pieces)


def back_kernel(core_ref, grad_ref, weight_ref, keep_ref, send_ref):
    rows = grad_ref.shape[1] // 2
    core = core_ref[0]
    for half in range(2):
        for target, side in ((keep_ref, core), (send_ref, 1 - core)):
            here = pl.ds(pl.multiple_of(side * rows, rows), rows)
            target[half] = lax.dot_general(
                grad_ref[half, here, :], weight_ref[...], (((1,), (1,)), ((), ())), preferred_element_type=F32
            ).astype(BF16)


def back(core, grad, weight):
    half = jax.ShapeDtypeStruct((2, grad.shape[1] // 2, weight.shape[0]), BF16)
    return pl.pallas_call(
        back_kernel,
        name="normed_grad",
        out_shape=(half, half),
        in_specs=[SCALARS, WHOLE, WHOLE],
        out_specs=[WHOLE] * 2,
        compiler_params=pltpu.CompilerParams(vmem_limit_bytes=40 << 20),
    )(core, grad, weight)


def tail_kernel(
    reach, base_ref, live_ref, near_ref, core_ref, far_ref, normal_ref, inv_ref, token_ref, pooled_ref, taps_ref, gain_ref, out_ref, conv_ref
):
    height, width, channels = token_ref.shape[1:]
    tile = base_ref[0] + pl.program_id(0)
    live = (tile < live_ref[0]).astype(F32)
    total = near_ref[0].astype(F32) + core_ref[0].astype(F32) + far_ref[...].astype(F32)
    scaled = total * gain_ref[...]
    normal = normal_ref[...]
    center = jnp.mean(scaled, axis=-1, keepdims=True)
    along = jnp.mean(scaled * normal, axis=-1, keepdims=True)
    conv_ref[...] = (scaled - center - normal * along) * inv_ref[:, :1]

    def slab(block, carry):
        lanes = pl.ds(pl.multiple_of(block * LANES, LANES), LANES)
        rows = [conv_ref[u * width : (u + 1) * width, lanes] for u in range(height)]
        total = depthwise_lanes(rows, taps_ref, lanes, reach, True)
        pooled = pooled_ref[0, :, lanes]
        for u in range(height):
            out_grad = live * token_ref[0, u, :, lanes].astype(F32) + pooled
            out_ref[0, u, :, lanes] = (out_grad + total[u]).astype(BF16)
        return carry

    lax.fori_loop(0, channels // LANES, slab, 0)


def tail(base, live, keep, core, far, normal, inv, token, pooled, taps, gain, reach):
    _, height, width, channels = token.shape
    spots = height * width
    mine = normal.shape[0] // spots
    one = lambda i, b, n: (0, 0)
    rows = lambda i, b, n: (i, 0)
    first = lambda i, b, n: (0, i, 0)
    return pl.pallas_call(
        functools.partial(tail_kernel, reach),
        name="norm_conv_back",
        out_shape=jax.ShapeDtypeStruct((mine, height, width, channels), BF16),
        grid_spec=pltpu.PrefetchScalarGridSpec(
            num_scalar_prefetch=2,
            grid=(mine,),
            in_specs=[
                pl.BlockSpec((1, spots, channels), first),
                pl.BlockSpec((1, spots, channels), first),
                pl.BlockSpec((spots, channels), rows),
                pl.BlockSpec((spots, channels), rows),
                pl.BlockSpec((spots, LANES), rows),
                pl.BlockSpec((1, height, width, channels), lambda i, b, n: (b[0] + i, 0, 0, 0)),
                pl.BlockSpec((1, 1, channels), lambda i, b, n: (b[0] + i, 0, 0)),
                pl.BlockSpec(taps.shape, one),
                pl.BlockSpec((1, channels), one),
            ],
            out_specs=pl.BlockSpec((1, height, width, channels), lambda i, b, n: (i, 0, 0, 0)),
            scratch_shapes=[pltpu.VMEM((spots, channels), F32)],
        ),
    )(base, live, keep, core, far, normal, inv, token, pooled[:, None, :], taps, gain)


def on_device(
    sizes,
    tiles,
    token_grad,
    embed_grad,
    live_tiles,
    dw_kernel,
    dw_bias,
    ln_gain,
    ln_bias,
    w_up,
    b_up,
    w_down,
    layer_scale,
):
    n_seq, n_dp = sizes
    count, height, width, channels = tiles.shape
    reach = dw_kernel.shape[0]
    mine = count // 2
    spots = height * width
    shard, columns = w_up.shape
    part = columns // 2
    seq, dp, core = lax.axis_index("seq"), lax.axis_index("dp"), lax.axis_index("mp")
    pair = [(i, i ^ 1) for i in range(n_dp)]
    ring = [(i, (i + 1) % n_seq) for i in range(n_seq)]
    side = (dp % 2) * part

    def over_ring(value):
        return lax.ppermute(value, "seq", ring)

    def over_pair(value):
        return lax.ppermute(value, "dp", pair)

    def over_cores(value):
        return lax.ppermute(value, "mp", [(0, 1), (1, 0)])

    def round_ring(weight):
        pieces = [lax.dynamic_slice_in_dim(weight, side, part, 1)]
        for _ in range(n_seq - 1):
            pieces.append(over_ring(pieces[-1]))
        return pieces

    def reduce_ring(partial):
        chunks = partial.reshape(n_seq, shard, part)

        def chunk(back):
            return lax.dynamic_index_in_dim(chunks, lax.rem(seq + (n_seq - back), n_seq), 0, keepdims=False)

        moving = chunk(1 % n_seq)
        for step in range(1, n_seq):
            moving = over_ring(moving).astype(F32) + chunk((step + 1) % n_seq).astype(F32)
            moving = moving.astype(BF16)
        return moving

    def both_sides(piece):
        if n_dp == 2:
            theirs = over_pair(piece)
            low = jnp.where(dp == 0, piece, theirs)
            high = jnp.where(dp == 0, theirs, piece)
            return jnp.concatenate([low, high], axis=1).astype(F32)
        spread = lax.dynamic_update_slice_in_dim(jnp.zeros((shard, columns), F32), piece.astype(F32), side, 1)
        return lax.psum(spread.astype(BF16), "dp").astype(F32)

    at = (lax.rem(seq + n_seq - jnp.arange(n_seq, dtype=jnp.int32), n_seq) * shard).astype(jnp.int32)
    base = (core * mine).astype(jnp.int32)[None]
    taps = dw_kernel.reshape(reach * reach, channels)
    row = lambda vector: vector.reshape(1, -1)

    up_pieces = round_ring(w_up)
    own_half, normal, inv = front(base, tiles, taps, row(dw_bias), row(ln_gain), row(ln_bias), mine, reach)
    other_half = over_pair(own_half)
    own_n = lax.all_gather(own_half, "mp", axis=0, tiled=True)
    arrived = lax.all_to_all(embed_grad[0], "seq", split_axis=0, concat_axis=1, tiled=True)
    live = (jnp.arange(count) < live_tiles[0]).astype(F32)
    pooled = arrived.astype(F32) * live[:, None] / spots
    out_grad = live[:, None, None, None] * token_grad.astype(F32) + pooled[:, None, None, :]
    own_b = (layer_scale * out_grad).astype(BF16).reshape(count * spots, channels)
    other_b = over_pair(lax.dynamic_slice_in_dim(own_b, core * (mine * spots), mine * spots, 0))
    down_pieces = round_ring(w_down)
    other_n = lax.all_gather(other_half, "mp", axis=0, tiled=True)
    other_b = lax.all_gather(other_b, "mp", axis=0, tiled=True)
    bias = row(lax.dynamic_slice_in_dim(b_up, side, part, 0))
    slope, part_down, whole_up = up(at, own_n, other_n, own_b, other_b, bias, up_pieces)
    down_sum = reduce_ring(part_down)
    hidden_grad, part_up = down(at, own_n, other_n, own_b, other_b, slope, down_pieces)
    up_sum = reduce_ring(part_up)
    keep, send = back(core.astype(jnp.int32)[None], hidden_grad, whole_up)
    from_core = over_cores(send)
    far = over_pair((keep[1].astype(F32) + from_core[1].astype(F32)).astype(BF16))
    grad_half = tail(base, live_tiles, keep, from_core, far, normal, inv, token_grad, pooled, taps, row(ln_gain), reach)
    tile_grad = lax.all_gather(grad_half, "mp", axis=0, tiled=True)
    return (tile_grad, both_sides(up_sum), both_sides(down_sum))


def solution(mesh):
    sizes = (mesh.shape["seq"], mesh.shape["dp"])
    return jax.shard_map(
        functools.partial(on_device, sizes),
        mesh=mesh,
        in_specs=(
            P(("groups", "seq", "dp"), None, None, None),
            P(("groups", "seq", "dp"), None, None, None),
            P("dp", "groups", "seq"),
            P(("groups", "seq", "dp")),
            P(),
            P(),
            P(),
            P(),
            P("seq", "mp"),
            P("mp"),
            P("seq", "mp"),
            P(),
        ),
        out_specs=(
            P(("groups", "seq", "dp"), None, None, None),
            P(("groups", "seq"), "mp"),
            P(("groups", "seq"), "mp"),
        ),
        check_vma=False,
    )
```

time: 268 us -> 133 us (0.50)
  waiting for transfers between devices: 151 us -> 47.9 us
  other arithmetic: 63.8 us -> 8.41 us
  Pallas kernels: 0 us -> 30 us
  matrix products: 23.4 us -> 0 us
  between operations: 14.9 us -> 1.6 us
  starting transfers between devices: 6.85 us -> 19.5 us
  blocking collectives: 0 us -> 10.4 us
  local copies, waits for them, and re-layouts: 6.86 us -> 14.1 us
    reduce_scatter x2 -> x0, waiting for transfers between devices: 82.7 us -> none  [the longest x1 43 us: on_device(): lax.psum_scatter(part_down.astype(jnp.bfloat16), 'seq', scatter_dimension...]
    all_gather x2 -> x0, waiting for transfers between devices: 57.1 us -> none  [the longest x1 39 us: on_device(): lax.all_gather(w_down, 'seq', axis=0, tiled=True)]
    ppermute x0 -> x18, waiting for transfers between devices: none -> 47.9 us  [the longest x12 33.9 us: over_ring(): return lax.ppermute(value, 'seq', ring)]
    convert_element_type x8 -> x12, other arithmetic: 45.2 us -> 7.52 us  [the longest x6 5 us: reduce_ring(): moving = moving.astype(BF16)]
    pallas_call x0 -> x5, Pallas kernels: none -> 30 us  [the longest x1 8.25 us: up(): pl.pallas_call(functools.partial(up_kernel, len(pieces)), name='up_and_do...]
    dot_general x5 -> x0, matrix products: 23.4 us -> none  [the longest x1 5.67 us: on_device(): jnp.dot(branch_grad, full_down, preferred_element_type=jnp.float32)]
    reduce_sum x4 -> x0, other arithmetic: 16.5 us -> none  [the longest x1 13 us: normalize(): center = jnp.mean(values, axis=-1, keepdims=True)]
    ppermute x0 -> x18, starting transfers between devices: none -> 13.2 us  [the longest x12 7.2 us: over_ring(): return lax.ppermute(value, 'seq', ring)]
  transfers between devices with their start and end apart: 7 -> 19, of which waited for: 6 -> 12; matrix products, arithmetic and copies ran while one was open for 30% -> 12% of each run, Pallas kernels for 0% -> 17%
where the time goes in v1:
time: 133 us; the launch traced here: 132 us
  waiting for transfers between devices  47.9 us (36%)
  Pallas kernels  30 us (23%)
  starting transfers between devices  19.5 us (15%)
  local copies, waits for them, and re-layouts  14.1 us (11%)
  blocking collectives  10.4 us (8%)
  other arithmetic  8.41 us (6%)
  between operations  1.6 us (1%)
    ppermute x12, waiting for transfers between devices, over_ring(): return lax.ppermute(value, 'seq', ring)  33.9 us
    ppermute x5, waiting for transfers between devices, over_pair(): return lax.ppermute(value, 'dp', pair)  14 us
    pallas_call x1, Pallas kernels, up(): pl.pallas_call(functools.partial(up_kernel, len(pieces)), name='up_and_do...  8.25 us
    ppermute x12, starting transfers between devices, over_ring(): return lax.ppermute(value, 'seq', ring)  7.2 us
    pallas_call x1, Pallas kernels, tail(): pl.pallas_call(functools.partial(tail_kernel, reach), name='norm_conv_bac...  7 us
    pallas_call x1, Pallas kernels, down(): pl.pallas_call(functools.partial(down_kernel, len(pieces)), name='hidden_...  6.61 us
    pallas_call x1, Pallas kernels, front(): pl.pallas_call(functools.partial(front_kernel, reach), name='conv_norm',...  6.47 us
    all_to_all x1, starting transfers between devices, on_device(): lax.all_to_all(embed_grad[0], 'seq', split_axis=0, concat_axis=1, tiled=T...  6.32 us
  transfers between devices with their start and end apart: 19, of which 12 were waited for; matrix products, arithmetic and copies ran while one was open for 12% of the time, Pallas kernels for 17%

profile of v1, /device:TPU:0, one launch (start us, length us, event | category | flops | bytes accessed | tf_op | source)
XLA Modules:
  0.0 132.0 jit_solution(2611663312729847706)
XLA Ops:
  0.7 0.8 all_to_all.10
  1.5 0.7 reshape.134
  2.2 6.3 %all-to-all-start = ((bf16[4,2,960]{2,1,0:T(2,128)(2,1)}), bf16[4,2,960]{2,1,0:T(2,128)(2,1)S(1)}, u32[]{:S(2)}, u32[]{:S(2)}) async-start(bf16[4,2,960]{2,1,0:T(2,128)(2,1)} %reshape.134), calls=%async_computation | async-start | bytes 32768 | tf_op jit(solution)/shard_map/all_to_all | solution.py:352
  8.6 2.1 %collective-permute-start.5 = (bf16[192,640]{1,0:T(8,128)(2,1)S(1)}, bf16[192,640]{1,0:T(8,128)(2,1)S(1)}, u32[]{:S(2)}, u32[]{:S(2)}) collective-permute-start(bf16[192,640]{1,0:T(8,128)(2,1)S(1)} %constant_dynamic-slice_fusion.rest_0_), channel_id=1, source_target_pairs={{0,4},{4,8},{8,12},{12,0},{1,5},{5,9},{9,13},{13,1},{2,6},{6,10},{... | collective-permute-start | bytes 737288 | tf_op jit(solution)/shard_map/ppermute | solution.py:308
  10.7 1.0 constant_dynamic-slice_fusion.1.rest_0_
  11.6 1.5 %collective-permute-start.2 = (bf16[192,640]{1,0:T(8,128)(2,1)S(1)}, bf16[192,640]{1,0:T(8,128)(2,1)S(1)}, u32[]{:S(2)}, u32[]{:S(2)}) collective-permute-start(bf16[192,640]{1,0:T(8,128)(2,1)S(1)} %constant_dynamic-slice_fusion.1.rest_0_), channel_id=1, source_target_pairs={{0,4},{4,8},{8,12},{12,0},{1,5},{5,9},{9,13},{13,1},{2,6},{6,10},{... | collective-permute-start | bytes 737288 | tf_op jit(solution)/shard_map/ppermute | solution.py:308
  13.1 1.3 reshape.120.gain_ref
  14.4 1.3 reshape.119.bias_ref
  15.7 1.3 reshape.121.shift_ref
  17.0 1.6 %reshape.118.taps_ref = f32[49,768]{1,0:T(8,128)} reshape(f32[7,7,768]{2,1,0:T(8,128)} %param.16) | data formatting | bytes 301056 | tf_op jit(solution)/shard_map/reshape | solution.py:345
  18.6 6.5 %conv_norm.1 = (bf16[320,768]{1,0:T(8,128)(2,1)}, f32[320,768]{1,0:T(8,128)}, f32[320,128]{1,0:T(8,128)}) custom-call(s32[1]{0:T(128)} %bitcast.base_ref, bf16[10,8,8,768]{3,2,1,0:T(8,128)(2,1)} %tiles_ref.1, f32[49,768]{1,0:T(8,128)} %reshape.118.taps_ref, f32[1,768]{1,0:T(1,128)} %reshape.119.bias_ref, f32[1,768]{1,0:T(1,128)} %reshape.120.gain_ref, ...), custom_call_target="tpu_custom_call" | custom-call | tf_op jit(solution)/shard_map/conv_norm/pallas_call | solution.py:71
  25.0 1.6 %collective-permute-start = (bf16[320,768]{1,0:T(8,128)(2,1)}, bf16[320,768]{1,0:T(8,128)(2,1)}, u32[]{:S(2)}, u32[]{:S(2)}) collective-permute-start(bf16[320,768]{1,0:T(8,128)(2,1)} %get-tuple-element.13), channel_id=1, source_target_pairs={{0,2},{2,0},{1,3},{3,1},{4,6},{6,4},{5,7},{7,5},{8,10},{10,8},{9,1... | collective-permute-start | bytes 1474568 | tf_op jit(solution)/shard_map/ppermute | solution.py:311
  28.1 0.6 collective-permute-start.1
  28.7 1.5 %collective-permute-start.6 = (bf16[192,640]{1,0:T(8,128)(2,1)S(1)}, bf16[192,640]{1,0:T(8,128)(2,1)S(1)}, u32[]{:S(2)}, u32[]{:S(2)}) collective-permute-start(bf16[192,640]{1,0:T(8,128)(2,1)S(1)} %collective-permute-done.5.rest_1_), channel_id=1, source_target_pairs={{0,4},{4,8},{8,12},{12,0},{1,5},{5,9},{9,13},{13,1},{2,6},{6,10},{... | collective-permute-start | bytes 737288 | tf_op jit(solution)/shard_map/ppermute | solution.py:308
  30.3 2.5 %all_gather.12.own_n = bf16[640,768]{1,0:T(8,128)(2,1)S(1)} all-gather(bf16[320,768]{1,0:T(8,128)(2,1)S(1)} %copy-done.10), channel_id=1, replica_groups=mesh['groups'=2,'seq'=4,'dp'=2,'mp'=2] {'mp'}, dimensions={0}, use_global_device_ids=true | all-gather | bytes 1474560 | tf_op jit(solution)/shard_map/all_gather | solution.py:351
  32.8 6.7 %collective-permute-done.6.rest_2_ = bf16[192,640]{1,0:T(8,128)(2,1)S(1)} collective-permute-done((bf16[192,640]{1,0:T(8,128)(2,1)S(1)}, bf16[192,640]{1,0:T(8,128)(2,1)S(1)}, u32[]{:S(2)}, u32[]{:S(2)}) %collective-permute-start.6) | collective-permute-done | bytes 245792 | tf_op jit(solution)/shard_map/ppermute | solution.py:308
  39.4 5.3 %collective-permute-done.3.rest_2_ = bf16[192,640]{1,0:T(8,128)(2,1)S(1)} collective-permute-done((bf16[192,640]{1,0:T(8,128)(2,1)S(1)}, bf16[192,640]{1,0:T(8,128)(2,1)S(1)}, u32[]{:S(2)}, u32[]{:S(2)}) %collective-permute-start.3) | collective-permute-done | bytes 245792 | tf_op jit(solution)/shard_map/ppermute | solution.py:308
  44.7 2.7 %all_gather.13.other_n = bf16[640,768]{1,0:T(8,128)(2,1)S(1)} all-gather(bf16[320,768]{1,0:T(8,128)(2,1)} %collective-permute-done), channel_id=1, replica_groups=mesh['groups'=2,'seq'=4,'dp'=2,'mp'=2] {'mp'}, dimensions={0}, use_global_device_ids=true | all-gather | bytes 1474560 | tf_op jit(solution)/shard_map/all_gather | solution.py:359
  47.7 2.5 %all_gather.14.other_b = bf16[640,768]{1,0:T(8,128)(2,1)S(1)} all-gather(bf16[320,768]{1,0:T(8,128)(2,1)S(1)} %collective-permute-done.1), channel_id=1, replica_groups=mesh['groups'=2,'seq'=4,'dp'=2,'mp'=2] {'mp'}, dimensions={0}, use_global_device_ids=true | all-gather | bytes 1474560 | tf_op jit(solution)/shard_map/all_gather | solution.py:360
  50.2 2.5 %collective-permute-done.4.rest_3_ = bf16[192,640]{1,0:T(8,128)(2,1)S(1)} collective-permute-done((bf16[192,640]{1,0:T(8,128)(2,1)S(1)}, bf16[192,640]{1,0:T(8,128)(2,1)S(1)}, u32[]{:S(2)}, u32[]{:S(2)}) %collective-permute-start.4) | collective-permute-done | bytes 245792 | tf_op jit(solution)/shard_map/ppermute | solution.py:308
  52.7 8.2 %up_and_down_grad.1 = (f32[2,640,640]{2,1,0:T(8,128)S(1)}, bf16[768,640]{1,0:T(8,128)(2,1)S(1)}, bf16[768,640]{1,0:T(8,128)(2,1)S(1)}) custom-call(s32[4]{0:T(128)S(1)} %fusion.8.at_ref, bf16[640,768]{1,0:T(8,128)(2,1)S(1)} %all_gather.12.own_n, bf16[640,768]{1,0:T(8,128)(2,1)S(1)} %all_gather.13.other_n, bf16[640,768]{1,0:T(8,128)(2,1)S(1)} %bitcast.34, ...), custom_call_target="tpu_custom_call" | custom-call | tf_op jit(solution)/shard_map/up_and_down_grad/pallas_call | solution.py:144
  61.0 0.9 copy-done.4
  61.9 0.7 dynamic-slice_bitcast_fusion
  62.6 6.6 %hidden_and_up_grad.1 = (bf16[2,640,640]{2,1,0:T(8,128)(2,1)S(1)}, bf16[768,640]{1,0:T(8,128)(2,1)S(1)}) custom-call(s32[4]{0:T(128)S(1)} %fusion.8.at_ref, bf16[640,768]{1,0:T(8,128)(2,1)S(1)} %all_gather.12.own_n, bf16[640,768]{1,0:T(8,128)(2,1)S(1)} %all_gather.13.other_n, bf16[640,768]{1,0:T(8,128)(2,1)S(1)} %bitcast.35, ...), custom_call_target="tpu_custom_call" | custom-call | tf_op jit(solution)/shard_map/hidden_and_up_grad/pallas_call | solution.py:182
  69.3 0.9 copy-done.2
  70.3 0.6 collective-permute-done.14
  70.9 1.7 %fusion.3 = bf16[192,640]{1,0:T(8,128)(2,1)} fusion(bf16[192,640]{1,0:T(8,128)(2,1)} %collective-permute-done.14, bf16[4,192,640]{2,1,0:T(8,128)(2,1)S(1)} %bitcast.37, s32[]{:T(128)S(6)} %select_n.57), kind=kLoop, calls=%fused_computation.10 | loop fusion | flops 491520 | bytes 737284 | tf_op jit(solution)/shard_map/convert_element_type | solution.py:331
  72.6 1.5 %collective-permute-start.15 = (bf16[192,640]{1,0:T(8,128)(2,1)}, bf16[192,640]{1,0:T(8,128)(2,1)}, u32[]{:S(2)}, u32[]{:S(2)}) collective-permute-start(bf16[192,640]{1,0:T(8,128)(2,1)} %fusion.3), channel_id=1, source_target_pairs={{0,4},{4,8},{8,12},{12,0},{1,5},{5,9},{9,13},{13,1},{2,6},{6,10},{... | collective-permute-start | bytes 737288 | tf_op jit(solution)/shard_map/ppermute | solution.py:308
  74.2 6.9 %collective-permute-done.10 = bf16[192,640]{1,0:T(8,128)(2,1)} collective-permute-done((bf16[192,640]{1,0:T(8,128)(2,1)S(1)}, bf16[192,640]{1,0:T(8,128)(2,1)}, u32[]{:S(2)}, u32[]{:S(2)}) %collective-permute-start.10) | collective-permute-done | bytes 245792 | tf_op jit(solution)/shard_map/ppermute | solution.py:308
  81.1 1.1 fusion.6
  82.4 1.3 copy-done.5
  83.7 1.7 %normed_grad.1 = (bf16[2,320,768]{2,1,0:T(8,128)(2,1)S(1)}, bf16[2,320,768]{2,1,0:T(8,128)(2,1)S(1)}) custom-call(s32[1]{0:T(128)} %bitcast.1.core_ref, bf16[2,640,640]{2,1,0:T(8,128)(2,1)S(1)} %get-tuple-element.15.grad_ref, bf16[768,640]{1,0:T(8,128)(2,1)S(1)} %copy-done.5), custom_call_target="tpu_custom_call" | custom-call | tf_op jit(solution)/shard_map/normed_grad/pallas_call | solution.py:213
  85.8 1.0 fusion.2
  87.2 3.2 %collective-permute-done.11 = bf16[192,640]{1,0:T(8,128)(2,1)} collective-permute-done((bf16[192,640]{1,0:T(8,128)(2,1)S(1)}, bf16[192,640]{1,0:T(8,128)(2,1)}, u32[]{:S(2)}, u32[]{:S(2)}) %collective-permute-start.11) | collective-permute-done | bytes 245792 | tf_op jit(solution)/shard_map/ppermute | solution.py:308
  90.4 1.0 fusion.5
  91.4 0.7 multiply_multiply_fusion.1.pooled_ref
  92.1 5.2 %collective-permute-done.16 = bf16[192,640]{1,0:T(8,128)(2,1)S(1)} collective-permute-done((bf16[192,640]{1,0:T(8,128)(2,1)S(1)}, bf16[192,640]{1,0:T(8,128)(2,1)S(1)}, u32[]{:S(2)}, u32[]{:S(2)}) %collective-permute-start.16) | collective-permute-done | bytes 245792 | tf_op jit(solution)/shard_map/ppermute | solution.py:308
  97.5 1.6 %collective-permute-start.17 = (bf16[192,640]{1,0:T(8,128)(2,1)S(1)}, bf16[192,640]{1,0:T(8,128)(2,1)S(1)}, u32[]{:S(2)}, u32[]{:S(2)}) collective-permute-start(bf16[192,640]{1,0:T(8,128)(2,1)S(1)} %fusion.1), channel_id=1, source_target_pairs={{0,2},{2,0},{1,3},{3,1},{4,6},{6,4},{5,7},{7,5},{8,10},{10,8},{9,1... | collective-permute-start | bytes 737288 | tf_op jit(solution)/shard_map/ppermute | solution.py:311
  99.0 3.2 %collective-permute-done.12 = bf16[192,640]{1,0:T(8,128)(2,1)S(1)} collective-permute-done((bf16[192,640]{1,0:T(8,128)(2,1)S(1)}, bf16[192,640]{1,0:T(8,128)(2,1)S(1)}, u32[]{:S(2)}, u32[]{:S(2)}) %collective-permute-start.12) | collective-permute-done | bytes 245792 | tf_op jit(solution)/shard_map/ppermute | solution.py:308
  102.3 1.6 %collective-permute-start.13 = (bf16[192,640]{1,0:T(8,128)(2,1)S(1)}, bf16[192,640]{1,0:T(8,128)(2,1)S(1)}, u32[]{:S(2)}, u32[]{:S(2)}) collective-permute-start(bf16[192,640]{1,0:T(8,128)(2,1)S(1)} %fusion.4), channel_id=1, source_target_pairs={{0,2},{2,0},{1,3},{3,1},{4,6},{6,4},{5,7},{7,5},{8,10},{10,8},{9,1... | collective-permute-start | bytes 737288 | tf_op jit(solution)/shard_map/ppermute | solution.py:311
  104.6 6.6 %collective-permute-done.13 = bf16[192,640]{1,0:T(8,128)(2,1)S(1)} collective-permute-done((bf16[192,640]{1,0:T(8,128)(2,1)S(1)}, bf16[192,640]{1,0:T(8,128)(2,1)S(1)}, u32[]{:S(2)}, u32[]{:S(2)}) %collective-permute-start.13) | collective-permute-done | bytes 245792 | tf_op jit(solution)/shard_map/ppermute | solution.py:311
  111.3 1.0 maximum_convert_fusion
  112.4 1.0 maximum_convert_fusion.1
  113.4 7.1 %collective-permute-done.9.far_ref = bf16[320,768]{1,0:T(8,128)(2,1)S(1)} collective-permute-done((bf16[320,768]{1,0:T(8,128)(2,1)S(1)}, bf16[320,768]{1,0:T(8,128)(2,1)S(1)}, u32[]{:S(2)}, u32[]{:S(2)}) %collective-permute-start.9) | collective-permute-done | bytes 491552 | tf_op jit(solution)/shard_map/ppermute | solution.py:311
  120.5 0.8 copy-done.11
  121.3 7.0 %norm_conv_back.1 = bf16[5,8,8,768]{3,2,1,0:T(8,128)(2,1)} custom-call(s32[1]{0:T(128)} %bitcast.base_ref, s32[1]{0:T(128)} %copy.22.live_ref, bf16[2,320,768]{2,1,0:T(8,128)(2,1)} %copy-done.1, bf16[2,320,768]{2,1,0:T(8,128)(2,1)} %copy-done.9, bf16[320,768]{1,0:T(8,128)(2,1)} %copy-done.11, f32[320,768]{1,0:T(8,128)} %get-tuple-element.19.normal_ref, ...), custom_call_target="tpu_custom_call" | custom-call | tf_op jit(solution)/shard_map/norm_conv_back/pallas_call | solution.py:256
  128.3 2.7 %all_gather.15 = bf16[10,8,8,768]{3,2,1,0:T(8,128)(2,1)S(1)} all-gather(bf16[5,8,8,768]{3,2,1,0:T(8,128)(2,1)} %norm_conv_back.1), channel_id=1, replica_groups=mesh['groups'=2,'seq'=4,'dp'=2,'mp'=2] {'mp'}, dimensions={0}, use_global_device_ids=true | all-gather | bytes 1474560 | tf_op jit(solution)/shard_map/all_gather | solution.py:370
  131.0 0.9 copy.23
  (62 shorter events, 3.2 us)
Async XLA Ops:
  0.6 7.9 %copy-start = (bf16[192,1280]{1,0:T(8,128)(2,1)S(1)}, bf16[192,1280]{1,0:T(8,128)(2,1)}, u32[]{:S(2)}) copy-start(bf16[192,1280]{1,0:T(8,128)(2,1)} %param.22) | copy-start | bytes 1474564
  0.6 26.6 %copy-start.13 = (f32[1280]{0:T(1024)S(1)}, f32[1280]{0:T(1024)}, u32[]{:S(2)}) copy-start(f32[1280]{0:T(1024)} %param.21) | copy-start | bytes 15364
  0.7 27.1 %copy-start.8 = (bf16[10,8,8,768]{3,2,1,0:T(8,128)(2,1)S(1)}, bf16[10,8,8,768]{3,2,1,0:T(8,128)(2,1)}, u32[]{:S(2)}) copy-start(bf16[10,8,8,768]{3,2,1,0:T(8,128)(2,1)} %token_ref.1) | copy-start | bytes 2949124
  0.7 27.0 %copy-start.12 = (f32[768]{0:T(1024)S(1)}, f32[768]{0:T(1024)}, u32[]{:S(2)}) copy-start(f32[768]{0:T(1024)} %param.23) | copy-start | bytes 9220
  2.2 25.1 %all-to-all-start = ((bf16[4,2,960]{2,1,0:T(2,128)(2,1)}), bf16[4,2,960]{2,1,0:T(2,128)(2,1)S(1)}, u32[]{:S(2)}, u32[]{:S(2)}) async-start(bf16[4,2,960]{2,1,0:T(2,128)(2,1)} %reshape.134), calls=%async_computation | async-start | bytes 32768 | tf_op jit(solution)/shard_map/all_to_all | solution.py:352
  8.6 20.2 %collective-permute-start.5 = (bf16[192,640]{1,0:T(8,128)(2,1)S(1)}, bf16[192,640]{1,0:T(8,128)(2,1)S(1)}, u32[]{:S(2)}, u32[]{:S(2)}) collective-permute-start(bf16[192,640]{1,0:T(8,128)(2,1)S(1)} %constant_dynamic-slice_fusion.rest_0_), channel_id=1, source_target_pairs={{0,4},{4,8},{8,12},{12,0},{1,5},{5,9},{9,13},{13,1},{2,6},{6,10},{... | collective-permute-start | bytes 737288 | tf_op jit(solution)/shard_map/ppermute | solution.py:308
  11.6 18.6 %collective-permute-start.2 = (bf16[192,640]{1,0:T(8,128)(2,1)S(1)}, bf16[192,640]{1,0:T(8,128)(2,1)S(1)}, u32[]{:S(2)}, u32[]{:S(2)}) collective-permute-start(bf16[192,640]{1,0:T(8,128)(2,1)S(1)} %constant_dynamic-slice_fusion.1.rest_0_), channel_id=1, source_target_pairs={{0,4},{4,8},{8,12},{12,0},{1,5},{5,9},{9,13},{13,1},{2,6},{6,10},{... | collective-permute-start | bytes 737288 | tf_op jit(solution)/shard_map/ppermute | solution.py:308
  25.0 5.2 %copy-start.10 = (bf16[320,768]{1,0:T(8,128)(2,1)S(1)}, bf16[320,768]{1,0:T(8,128)(2,1)}, u32[]{:S(2)}) copy-start(bf16[320,768]{1,0:T(8,128)(2,1)} %get-tuple-element.13) | copy-start | bytes 1474564
  25.0 19.7 %collective-permute-start = (bf16[320,768]{1,0:T(8,128)(2,1)}, bf16[320,768]{1,0:T(8,128)(2,1)}, u32[]{:S(2)}, u32[]{:S(2)}) collective-permute-start(bf16[320,768]{1,0:T(8,128)(2,1)} %get-tuple-element.13), channel_id=1, source_target_pairs={{0,2},{2,0},{1,3},{3,1},{4,6},{6,4},{5,7},{7,5},{8,10},{10,8},{9,1... | collective-permute-start | bytes 1474568 | tf_op jit(solution)/shard_map/ppermute | solution.py:311
  28.1 19.5 %collective-permute-start.1 = (bf16[320,768]{1,0:T(8,128)(2,1)S(1)}, bf16[320,768]{1,0:T(8,128)(2,1)S(1)}, u32[]{:S(2)}, u32[]{:S(2)}) collective-permute-start(bf16[320,768]{1,0:T(8,128)(2,1)S(1)} %constant_dynamic-slice_fusion.2), channel_id=1, source_target_pairs={{0,2},{2,0},{1,3},{3,1},{4,6},{6,4},{5,7},{7,5},{8,10},{10,8},{9,1... | collective-permute-start | bytes 1474568 | tf_op jit(solution)/shard_map/ppermute | solution.py:311
  28.7 21.4 %copy-start.6 = (bf16[192,640]{1,0:T(8,128)(2,1)}, bf16[192,640]{1,0:T(8,128)(2,1)S(1)}, u32[]{:S(2)}) copy-start(bf16[192,640]{1,0:T(8,128)(2,1)S(1)} %collective-permute-done.5.rest_1_) | copy-start | bytes 737284
  28.7 10.7 %collective-permute-start.6 = (bf16[192,640]{1,0:T(8,128)(2,1)S(1)}, bf16[192,640]{1,0:T(8,128)(2,1)S(1)}, u32[]{:S(2)}, u32[]{:S(2)}) collective-permute-start(bf16[192,640]{1,0:T(8,128)(2,1)S(1)} %collective-permute-done.5.rest_1_), channel_id=1, source_target_pairs={{0,4},{4,8},{8,12},{12,0},{1,5},{5,9},{9,13},{13,1},{2,6},{6,10},{... | collective-permute-start | bytes 737288 | tf_op jit(solution)/shard_map/ppermute | solution.py:308
  30.2 14.5 %collective-permute-start.3 = (bf16[192,640]{1,0:T(8,128)(2,1)S(1)}, bf16[192,640]{1,0:T(8,128)(2,1)S(1)}, u32[]{:S(2)}, u32[]{:S(2)}) collective-permute-start(bf16[192,640]{1,0:T(8,128)(2,1)S(1)} %collective-permute-done.2.rest_1_), channel_id=1, source_target_pairs={{0,4},{4,8},{8,12},{12,0},{1,5},{5,9},{9,13},{13,1},{2,6},{6,10},{... | collective-permute-start | bytes 737288 | tf_op jit(solution)/shard_map/ppermute | solution.py:308
  39.4 23.2 %collective-permute-start.7 = (bf16[192,640]{1,0:T(8,128)(2,1)S(1)}, bf16[192,640]{1,0:T(8,128)(2,1)S(1)}, u32[]{:S(2)}, u32[]{:S(2)}) collective-permute-start(bf16[192,640]{1,0:T(8,128)(2,1)S(1)} %collective-permute-done.6.rest_2_), channel_id=1, source_target_pairs={{0,4},{4,8},{8,12},{12,0},{1,5},{5,9},{9,13},{13,1},{2,6},{6,10},{... | collective-permute-start | bytes 737288 | tf_op jit(solution)/shard_map/ppermute | solution.py:308
  44.7 8.0 %collective-permute-start.4 = (bf16[192,640]{1,0:T(8,128)(2,1)S(1)}, bf16[192,640]{1,0:T(8,128)(2,1)S(1)}, u32[]{:S(2)}, u32[]{:S(2)}) collective-permute-start(bf16[192,640]{1,0:T(8,128)(2,1)S(1)} %collective-permute-done.3.rest_2_), channel_id=1, source_target_pairs={{0,4},{4,8},{8,12},{12,0},{1,5},{5,9},{9,13},{13,1},{2,6},{6,10},{... | collective-permute-start | bytes 737288 | tf_op jit(solution)/shard_map/ppermute | solution.py:308
  52.7 9.9 %copy-start.7 = (bf16[192,640]{1,0:T(8,128)(2,1)S(1)}, bf16[192,640]{1,0:T(8,128)(2,1)}, u32[]{:S(2)}) copy-start(bf16[192,640]{1,0:T(8,128)(2,1)} %copy-done.6) | copy-start | bytes 737284
  61.0 0.9 copy-start.4
  62.6 8.3 %collective-permute-start.14 = (bf16[192,640]{1,0:T(8,128)(2,1)}, bf16[192,640]{1,0:T(8,128)(2,1)}, u32[]{:S(2)}, u32[]{:S(2)}) collective-permute-start(bf16[192,640]{1,0:T(8,128)(2,1)} %dynamic-slice_bitcast_fusion), channel_id=1, source_target_pairs={{0,4},{4,8},{8,12},{12,0},{1,5},{5,9},{9,13},{13,1},{2,6},{6,10},{... | collective-permute-start | bytes 737288 | tf_op jit(solution)/shard_map/ppermute | solution.py:308
  69.3 0.9 copy-start.2
  70.2 10.8 %collective-permute-start.10 = (bf16[192,640]{1,0:T(8,128)(2,1)S(1)}, bf16[192,640]{1,0:T(8,128)(2,1)}, u32[]{:S(2)}, u32[]{:S(2)}) collective-permute-start(bf16[192,640]{1,0:T(8,128)(2,1)S(1)} %dynamic-slice_bitcast_fusion.1), channel_id=1, source_target_pairs={{0,4},{4,8},{8,12},{12,0},{1,5},{5,9},{9,13},{13,1},{2,6},{6,10},{... | collective-permute-start | bytes 737288 | tf_op jit(solution)/shard_map/ppermute | solution.py:308
  72.6 13.1 %collective-permute-start.15 = (bf16[192,640]{1,0:T(8,128)(2,1)}, bf16[192,640]{1,0:T(8,128)(2,1)}, u32[]{:S(2)}, u32[]{:S(2)}) collective-permute-start(bf16[192,640]{1,0:T(8,128)(2,1)} %fusion.3), channel_id=1, source_target_pairs={{0,4},{4,8},{8,12},{12,0},{1,5},{5,9},{9,13},{13,1},{2,6},{6,10},{... | collective-permute-start | bytes 737288 | tf_op jit(solution)/shard_map/ppermute | solution.py:308
  82.2 8.2 %collective-permute-start.11 = (bf16[192,640]{1,0:T(8,128)(2,1)S(1)}, bf16[192,640]{1,0:T(8,128)(2,1)}, u32[]{:S(2)}, u32[]{:S(2)}) collective-permute-start(bf16[192,640]{1,0:T(8,128)(2,1)S(1)} %fusion.6), channel_id=1, source_target_pairs={{0,4},{4,8},{8,12},{12,0},{1,5},{5,9},{9,13},{13,1},{2,6},{6,10},{... | collective-permute-start | bytes 737288 | tf_op jit(solution)/shard_map/ppermute | solution.py:308
  82.4 8.0 %copy-start.3 = (bf16[768,640]{1,0:T(8,128)(2,1)S(1)}, bf16[768,640]{1,0:T(8,128)(2,1)}, u32[]{:S(2)}) copy-start(bf16[768,640]{1,0:T(8,128)(2,1)} %copy-done.2) | copy-start | bytes 2949124
  82.4 1.3 copy-start.5
  85.4 18.6 %copy-start.1 = (bf16[2,320,768]{2,1,0:T(8,128)(2,1)}, bf16[2,320,768]{2,1,0:T(8,128)(2,1)S(1)}, u32[]{:S(2)}) copy-start(bf16[2,320,768]{2,1,0:T(8,128)(2,1)S(1)} %get-tuple-element.17.near_ref) | copy-start | bytes 2949124
  85.4 18.5 %collective-permute-start.8 = (bf16[2,320,768]{2,1,0:T(8,128)(2,1)S(1)}, bf16[2,320,768]{2,1,0:T(8,128)(2,1)S(1)}, u32[]{:S(2)}, u32[]{:S(2)}) collective-permute-start(bf16[2,320,768]{2,1,0:T(8,128)(2,1)S(1)} %get-tuple-element.18), channel_id=1, source_target_pairs={{0,1},{1,0},{2,3},{3,2},{4,5},{5,4},{6,7},{7,6},{8,9},{9,8},{10,11... | collective-permute-start | bytes 2949128 | tf_op jit(solution)/shard_map/ppermute | solution.py:314
  86.8 10.6 %collective-permute-start.16 = (bf16[192,640]{1,0:T(8,128)(2,1)S(1)}, bf16[192,640]{1,0:T(8,128)(2,1)S(1)}, u32[]{:S(2)}, u32[]{:S(2)}) collective-permute-start(bf16[192,640]{1,0:T(8,128)(2,1)S(1)} %fusion.2), channel_id=1, source_target_pairs={{0,4},{4,8},{8,12},{12,0},{1,5},{5,9},{9,13},{13,1},{2,6},{6,10},{... | collective-permute-start | bytes 737288 | tf_op jit(solution)/shard_map/ppermute | solution.py:308
  91.4 10.9 %collective-permute-start.12 = (bf16[192,640]{1,0:T(8,128)(2,1)S(1)}, bf16[192,640]{1,0:T(8,128)(2,1)S(1)}, u32[]{:S(2)}, u32[]{:S(2)}) collective-permute-start(bf16[192,640]{1,0:T(8,128)(2,1)S(1)} %fusion.5), channel_id=1, source_target_pairs={{0,4},{4,8},{8,12},{12,0},{1,5},{5,9},{9,13},{13,1},{2,6},{6,10},{... | collective-permute-start | bytes 737288 | tf_op jit(solution)/shard_map/ppermute | solution.py:308
  97.5 14.9 %collective-permute-start.17 = (bf16[192,640]{1,0:T(8,128)(2,1)S(1)}, bf16[192,640]{1,0:T(8,128)(2,1)S(1)}, u32[]{:S(2)}, u32[]{:S(2)}) collective-permute-start(bf16[192,640]{1,0:T(8,128)(2,1)S(1)} %fusion.1), channel_id=1, source_target_pairs={{0,2},{2,0},{1,3},{3,1},{4,6},{6,4},{5,7},{7,5},{8,10},{10,8},{9,1... | collective-permute-start | bytes 737288 | tf_op jit(solution)/shard_map/ppermute | solution.py:311
  102.3 8.9 %collective-permute-start.13 = (bf16[192,640]{1,0:T(8,128)(2,1)S(1)}, bf16[192,640]{1,0:T(8,128)(2,1)S(1)}, u32[]{:S(2)}, u32[]{:S(2)}) collective-permute-start(bf16[192,640]{1,0:T(8,128)(2,1)S(1)} %fusion.4), channel_id=1, source_target_pairs={{0,2},{2,0},{1,3},{3,1},{4,6},{6,4},{5,7},{7,5},{8,10},{10,8},{9,1... | collective-permute-start | bytes 737288 | tf_op jit(solution)/shard_map/ppermute | solution.py:311
  103.9 8.4 %copy-start.9 = (bf16[2,320,768]{2,1,0:T(8,128)(2,1)}, bf16[2,320,768]{2,1,0:T(8,128)(2,1)S(1)}, u32[]{:S(2)}) copy-start(bf16[2,320,768]{2,1,0:T(8,128)(2,1)S(1)} %collective-permute-done.8.core_ref) | copy-start | bytes 2949124
  104.0 16.5 %collective-permute-start.9 = (bf16[320,768]{1,0:T(8,128)(2,1)S(1)}, bf16[320,768]{1,0:T(8,128)(2,1)S(1)}, u32[]{:S(2)}, u32[]{:S(2)}) collective-permute-start(bf16[320,768]{1,0:T(8,128)(2,1)S(1)} %fusion), channel_id=1, source_target_pairs={{0,2},{2,0},{1,3},{3,1},{4,6},{6,4},{5,7},{7,5},{8,10},{10,8},{9,1... | collective-permute-start | bytes 1474568 | tf_op jit(solution)/shard_map/ppermute | solution.py:311
  120.5 0.8 copy-start.11

commit v2 on v0

v2 whole, which is shorter than its diff:
```python
import functools
import jax
import jax.numpy as jnp
from jax import lax
from jax.experimental import pallas as pl
from jax.experimental.pallas import tpu as pltpu
from jax.sharding import PartitionSpec as P

sqrt_two_pi = 0.7978845608028654
cubic_coef = 0.044715
LANES = 128
F32 = jnp.float32
BF16 = jnp.bfloat16
WHOLE = pl.BlockSpec(memory_space=pltpu.VMEM)
SCALARS = pl.BlockSpec(memory_space=pltpu.SMEM)
APART = pl.BlockSpec(memory_space=pltpu.HBM)


def in_vmem(*values):
    return [pltpu.with_memory_space_constraint(value, pltpu.VMEM) for value in values]


def in_hbm(*values):
    return [pltpu.with_memory_space_constraint(value, pltpu.HBM) for value in values]


ROWS = 32
VMEM_LIMIT = 16 << 20


COST = pl.CostEstimate(flops=10 << 30, transcendentals=0, bytes_accessed=4 << 20)


def depthwise_lanes(rows, taps_ref, lanes, reach, flip):
    height, width = len(rows), rows[0].shape[0]
    margin = reach // 2
    place = lax.broadcasted_iota(jnp.int32, rows[0].shape, 0)
    total = [None] * height
    for col in range(reach):
        shift = col - margin
        if shift:
            inside = (place + shift >= 0) & (place + shift < width)
            moved = [jnp.where(inside, pltpu.roll(row, (-shift) % width, 0), 0.0) for row in rows]
        else:
            moved = rows
        for line in range(reach):
            index = line * reach + col
            if flip:
                index = reach * reach - 1 - index
            tap = jnp.broadcast_to(taps_ref[index // reach, pl.ds(index % reach, 1), lanes], rows[0].shape)
            for u in range(height):
                source = u + line - margin
                if 0 <= source < height:
                    term = moved[source] * tap
                    total[u] = term if total[u] is None else total[u] + term
    return total


def front_kernel(
    base_ref, tiles_ref, taps_ref, bias_ref, gain_ref, shift_ref, normed_out, normal_out, inv_out,
    conv_ref, normed_ref, normal_ref, inv_ref, sems,
):
    height, width, channels = tiles_ref.shape[1:]
    spots = height * width
    mine = normed_ref.shape[0] // spots
    reach = taps_ref.shape[0]
    slabs = channels // LANES

    def saves(tile):
        here = pl.ds(pl.multiple_of(tile * spots, spots), spots)
        return (
            pltpu.make_async_copy(normal_ref.at[here], normal_out.at[here], sems.at[0, tile]),
            pltpu.make_async_copy(inv_ref.at[here], inv_out.at[here], sems.at[1, tile]),
            pltpu.make_async_copy(normed_ref.at[here], normed_out.at[here], sems.at[2, tile]),
        )

    def one_tile(tile, carry):
        def slab(block, carry):
            lanes = pl.ds(pl.multiple_of(block * LANES, LANES), LANES)
            rows = [tiles_ref[base_ref[0] + tile, u, :, lanes].astype(F32) for u in range(height)]
            total = depthwise_lanes(rows, taps_ref, lanes, reach, False)
            for u in range(height):
                conv_ref[u * width : (u + 1) * width, lanes] = total[u] + bias_ref[lanes][None, :]
            return carry

        lax.fori_loop(0, slabs, slab, 0)
        for part in range(spots // ROWS):
            conv = conv_ref[part * ROWS : (part + 1) * ROWS, :]
            here = pl.ds(pl.multiple_of(tile * spots + part * ROWS, ROWS), ROWS)
            center = jnp.mean(conv, axis=-1, keepdims=True)
            shifted = conv - center
            inv = lax.rsqrt(jnp.mean(shifted * shifted, axis=-1, keepdims=True) + 1e-06)
            normal = shifted * inv
            normal_ref[here, :] = normal
            inv_ref[here, :] = jnp.broadcast_to(inv, (ROWS, LANES))
            normed_ref[here, :] = (normal * gain_ref[...][None, :] + shift_ref[...][None, :]).astype(BF16)
        for copy in saves(tile):
            copy.start()
        return carry

    lax.fori_loop(0, mine, one_tile, 0)
    for tile in range(mine):
        for copy in saves(tile):
            copy.wait()


def front(base, tiles, taps, bias, gain, shift, mine):
    _, height, width, channels = tiles.shape
    rows = mine * height * width
    return pl.pallas_call(
        front_kernel,
        name="conv_norm",
        out_shape=(
            pltpu.HBM((rows, channels), BF16),
            pltpu.HBM((rows, channels), F32),
            pltpu.HBM((rows, LANES), F32),
        ),
        in_specs=[SCALARS] + [WHOLE] * 5,
        out_specs=[APART] * 3,
        scratch_shapes=[
            pltpu.VMEM((height * width, channels), F32),
            pltpu.VMEM((rows, channels), BF16),
            pltpu.VMEM((rows, channels), F32),
            pltpu.VMEM((rows, LANES), F32),
            pltpu.SemaphoreType.DMA((3, mine)),
        ],
        compiler_params=pltpu.CompilerParams(vmem_limit_bytes=VMEM_LIMIT),
        cost_estimate=COST,
    )(base, tiles, taps, bias, gain, shift)


def across_rows(left, right):
    return lax.dot_general(left, right, (((0,), (0,)), ((), ())), preferred_element_type=F32)


def up_kernel(hops, apart, place_ref, *rest):
    normed, branch, rest = rest[:4], rest[4:8], rest[8:]
    bias_ref, locals_, near, far = rest[0], rest[1:3], rest[3 : 3 + hops], rest[3 + hops : 3 + 2 * hops]
    slope_ref, down_ref, up_ref, fall_ref, normed_ref, branch_ref, hidden_ref, act_ref, sems = rest[3 + 2 * hops :]
    shard, half, part = locals_[0].shape[0], near[0].shape[1], up_ref.shape[1]
    rows = normed[0].shape[0]
    columns = pl.ds(pl.multiple_of(place_ref[0], LANES), part)
    early, late = [], []
    for which, whole_ref in enumerate((up_ref, fall_ref)):
        target = whole_ref.at[pl.ds(pl.multiple_of(place_ref[3], 16), shard)]
        moves = [(True, locals_[which].at[:, columns], target)]
        for k, (here, there) in enumerate(zip(near, far)):
            for is_far, piece, offset in ((0, here, place_ref[1]), (1, there, place_ref[2])):
                target = whole_ref.at[pl.ds(pl.multiple_of(place_ref[4 + k] + offset, 8), half)]
                moves.append((apart[2 * k + is_far], piece.at[which], target))
        for outside, source, target in moves:
            if outside:
                (late if which else early).append((source, target))
            else:
                target[...] = source[...]
    inputs = [(normed[k], normed_ref.at[k * rows : (k + 1) * rows]) for k in (0, 1)]
    copies = [pltpu.make_async_copy(source, target, sems.at[k]) for k, (source, target) in enumerate(early + inputs + late)]
    for copy in copies:
        copy.start()
    for k in (2, 3):
        normed_ref[k * rows : (k + 1) * rows, :] = normed[k][...]
    for k in range(4):
        branch_ref[k * rows : (k + 1) * rows, :] = branch[k][...]
    for copy in copies[: len(early)]:
        copy.wait()
    for k in (2, 3, 0, 1):
        if k < 2:
            copies[len(early) + k].wait()
        hidden_ref[...] = jnp.dot(normed_ref[k * rows : (k + 1) * rows, :], up_ref[...], preferred_element_type=F32)

        def block(i, carry):
            here = pl.ds(pl.multiple_of(i * ROWS, ROWS), ROWS)
            there = pl.ds(pl.multiple_of(k * rows + i * ROWS, ROWS), ROWS)
            value = hidden_ref[here, :] + bias_ref[...]
            square = value * value
            tangent = jnp.tanh(value * (sqrt_two_pi + (sqrt_two_pi * cubic_coef) * square))
            upper = 0.5 + 0.5 * tangent
            act_ref[there, :] = (value * upper).astype(BF16)
            bend = (0.5 * value) * (1.0 - tangent * tangent)
            slope_ref[there, :] = upper + bend * (sqrt_two_pi + (3.0 * sqrt_two_pi * cubic_coef) * square)
            return carry

        lax.fori_loop(0, rows // ROWS, block, 0)
    down_ref[...] = across_rows(branch_ref[...], act_ref[...]).astype(BF16)
    for copy in copies[len(early) + 2 :]:
        copy.wait()


def up(place, normed, branch, bias, weights, near, far):
    rows, channels = normed[0].shape
    columns = near[0].shape[2]
    hops = len(near)
    apart = [True] * (2 * hops)
    for last in (2 * hops - 1, 2 * hops - 2, 2 * hops - 3):
        apart[last] = False
    near = [(in_hbm if apart[2 * k] else in_vmem)(piece)[0] for k, piece in enumerate(near)]
    far = [(in_hbm if apart[2 * k + 1] else in_vmem)(piece)[0] for k, piece in enumerate(far)]
    pieces = [APART if apart[2 * k] else WHOLE for k in range(hops)] + [APART if apart[2 * k + 1] else WHOLE for k in range(hops)]
    return pl.pallas_call(
        functools.partial(up_kernel, hops, tuple(apart)),
        name="up_and_down_grad",
        out_shape=(
            pltpu.VMEM((4 * rows, columns), F32),
            pltpu.VMEM((channels, columns), BF16),
            pltpu.VMEM((channels, columns), BF16),
            pltpu.VMEM((channels, columns), BF16),
            pltpu.VMEM((4 * rows, channels), BF16),
            pltpu.VMEM((4 * rows, channels), BF16),
        ),
        in_specs=[SCALARS] + [APART] * 2 + [WHOLE] * 7 + [APART] * 2 + pieces,
        out_specs=[WHOLE] * 6,
        scratch_shapes=[
            pltpu.VMEM((rows, columns), F32),
            pltpu.VMEM((4 * rows, columns), BF16),
            pltpu.SemaphoreType.DMA((4 + 4 * hops,)),
        ],
        compiler_params=pltpu.CompilerParams(vmem_limit_bytes=VMEM_LIMIT),
        cost_estimate=COST,
    )(place, *in_hbm(*normed[:2]), *in_vmem(*normed[2:], *branch), bias, *in_hbm(*weights), *near, *far)


def down_kernel(branch_ref, slope_ref, weight_ref, grad_ref, acted_ref):
    rows = acted_ref.shape[0]
    for k in range(4):
        acted_ref[...] = jnp.dot(branch_ref[k * rows : (k + 1) * rows, :], weight_ref[...], preferred_element_type=F32)

        def block(i, carry):
            here = pl.ds(pl.multiple_of(i * ROWS, ROWS), ROWS)
            there = pl.ds(pl.multiple_of(k * rows + i * ROWS, ROWS), ROWS)
            grad_ref[there, :] = (acted_ref[here, :] * slope_ref[there, :]).astype(BF16)
            return carry

        lax.fori_loop(0, rows // ROWS, block, 0)


def down(branch, slope, weight):
    rows, columns = slope.shape
    return pl.pallas_call(
        down_kernel,
        name="hidden_grad",
        out_shape=pltpu.VMEM((rows, columns), BF16),
        in_specs=[WHOLE] * 3,
        out_specs=WHOLE,
        scratch_shapes=[pltpu.VMEM((rows // 4, columns), F32)],
        compiler_params=pltpu.CompilerParams(vmem_limit_bytes=VMEM_LIMIT),
        cost_estimate=COST,
    )(*in_vmem(branch, slope, weight))


def rise_kernel(normed_ref, grad_ref, up_ref):
    up_ref[...] = across_rows(normed_ref[...], grad_ref[...]).astype(BF16)


def rise(normed, grad):
    return pl.pallas_call(
        rise_kernel,
        name="up_grad",
        out_shape=pltpu.VMEM((normed.shape[1], grad.shape[1]), BF16),
        in_specs=[WHOLE] * 2,
        out_specs=WHOLE,
        compiler_params=pltpu.CompilerParams(vmem_limit_bytes=VMEM_LIMIT),
        cost_estimate=COST,
    )(*in_vmem(normed, grad))


def back_kernel(grad_ref, weight_ref, keep_ref, send_ref):
    rows = keep_ref.shape[1]
    for k, (target, slot) in enumerate(((keep_ref, 0), (send_ref, 0), (keep_ref, 1), (send_ref, 1))):
        target[slot] = lax.dot_general(
            grad_ref[k * rows : (k + 1) * rows, :], weight_ref[...], (((1,), (1,)), ((), ())), preferred_element_type=F32
        ).astype(BF16)


def back(grad, weight):
    rows, columns = grad.shape
    half = pltpu.VMEM((2, rows // 4, weight.shape[0]), BF16)
    return pl.pallas_call(
        back_kernel,
        name="normed_grad",
        out_shape=(half, half),
        in_specs=[WHOLE, WHOLE],
        out_specs=[WHOLE] * 2,
        compiler_params=pltpu.CompilerParams(vmem_limit_bytes=VMEM_LIMIT),
        cost_estimate=COST,
    )(*in_vmem(grad, weight))


def tail_kernel(
    base_ref, live_ref, normal_in, inv_in, token_in, near_ref, far_ref, taps_ref, pooled_ref, gain_ref, out_ref,
    normal_ref, inv_ref, token_ref, conv_ref, sems,
):
    mine, height, width, channels = out_ref.shape
    spots = height * width
    reach = taps_ref.shape[0]
    slabs = channels // LANES

    def loads(tile):
        here = pl.ds(pl.multiple_of(tile * spots, spots), spots)
        pairs = [(source.at[here], target.at[here]) for source, target in ((normal_in, normal_ref), (inv_in, inv_ref))]
        pairs.append((token_in.at[base_ref[0] + tile], token_ref.at[tile]))
        return [pltpu.make_async_copy(source, target, sems.at[k, tile]) for k, (source, target) in enumerate(pairs)]

    for tile in range(mine):
        for copy in loads(tile):
            copy.start()

    def one_tile(tile, carry):
        for copy in loads(tile):
            copy.wait()
        for part in range(spots // ROWS):
            here = pl.ds(pl.multiple_of(tile * spots + part * ROWS, ROWS), ROWS)
            scaled = (near_ref[here, :] + far_ref[here, :].astype(F32)) * gain_ref[...][None, :]
            normal = normal_ref[here, :]
            center = jnp.mean(scaled, axis=-1, keepdims=True)
            along = jnp.mean(scaled * normal, axis=-1, keepdims=True)
            conv_ref[part * ROWS : (part + 1) * ROWS, :] = (scaled - center - normal * along) * inv_ref[here, :1]
        live = (base_ref[0] + tile < live_ref[0]).astype(F32)

        def slab(block, carry):
            lanes = pl.ds(pl.multiple_of(block * LANES, LANES), LANES)
            rows = [conv_ref[u * width : (u + 1) * width, lanes] for u in range(height)]
            total = depthwise_lanes(rows, taps_ref, lanes, reach, True)
            pooled = pooled_ref[tile, :, lanes]
            for u in range(height):
                out_grad = live * token_ref[tile, u, :, lanes].astype(F32) + pooled
                out_ref[tile, u, :, lanes] = (out_grad + total[u]).astype(BF16)
            return carry

        lax.fori_loop(0, slabs, slab, 0)
        return carry

    lax.fori_loop(0, mine, one_tile, 0)


def tail(base, live, near, far, normal, inv, token, pooled, taps, gain):
    _, height, width, channels = token.shape
    rows = normal.shape[0]
    mine = rows // (height * width)
    return pl.pallas_call(
        tail_kernel,
        name="norm_conv_back",
        out_shape=jax.ShapeDtypeStruct((mine, height, width, channels), BF16),
        in_specs=[SCALARS] * 2 + [APART] * 3 + [WHOLE] * 5,
        out_specs=WHOLE,
        scratch_shapes=[
            pltpu.VMEM(normal.shape, F32),
            pltpu.VMEM(inv.shape, F32),
            pltpu.VMEM((mine, height, width, channels), BF16),
            pltpu.VMEM((height * width, channels), F32),
            pltpu.SemaphoreType.DMA((3, mine)),
        ],
        compiler_params=pltpu.CompilerParams(vmem_limit_bytes=VMEM_LIMIT),
        cost_estimate=COST,
    )(base, live, *in_hbm(normal, inv, token), *in_vmem(near, far), taps, pooled, gain)


def after(value, *others):
    return lax.optimization_barrier((value,) + others)[0]


def on_device(
    sizes,
    tiles,
    token_grad,
    embed_grad,
    live_tiles,
    dw_kernel,
    dw_bias,
    ln_gain,
    ln_bias,
    w_up,
    b_up,
    w_down,
    layer_scale,
):
    n_seq, n_dp = sizes
    count, height, width, channels = tiles.shape
    mine = count // 2
    spots = height * width
    shard, columns = w_up.shape
    part, half = columns // 2, shard // 2
    group, seq, dp, core = (lax.axis_index(name) for name in ("groups", "seq", "dp", "mp"))
    pair = [(i, i ^ 1) for i in range(n_dp)]
    swap = [(0, 1), (1, 0)]
    ring = [(i, (i + 1) % n_seq) for i in range(n_seq)]
    side = (dp % 2) * part

    def over_ring(value):
        return lax.ppermute(value, "seq", ring)

    def over_pair(value):
        return lax.ppermute(value, "dp", pair)

    def over_cores(value):
        return lax.ppermute(value, "mp", swap)

    def over_groups(value):
        return lax.ppermute(value, "groups", swap)

    def chunk(partial, back):
        chunks = partial.reshape(n_seq, shard, part)
        return lax.dynamic_index_in_dim(chunks, lax.rem(seq + (n_seq - back), n_seq), 0, keepdims=False)

    def hop(moving, partial, step):
        arrived = over_ring(moving).astype(F32) + chunk(partial, (step + 1) % n_seq).astype(F32)
        return arrived.astype(BF16)

    def both_sides(piece):
        if n_dp == 2:
            theirs = over_pair(piece)
            low = jnp.where(dp == 0, piece, theirs)
            high = jnp.where(dp == 0, theirs, piece)
            return jnp.concatenate([low, high], axis=1).astype(F32)
        spread = lax.dynamic_update_slice_in_dim(jnp.zeros((shard, columns), F32), piece.astype(F32), side, 1)
        return lax.psum(spread.astype(BF16), "dp").astype(F32)

    offsets = lax.rem(seq + n_seq - jnp.arange(n_seq, dtype=jnp.int32), n_seq) * shard
    place = jnp.concatenate([jnp.stack([side, group * half, (1 - group) * half]), offsets]).astype(jnp.int32)
    base = (core * mine).astype(jnp.int32)[None]

    moving = jnp.stack([lax.dynamic_slice(w, (group * half, side), (half, part)) for w in (w_up, w_down)])
    near, far = [over_ring(moving)], []
    live = (jnp.arange(count) < live_tiles[0]).astype(BF16)

    def own_tiles(values, which):
        return lax.dynamic_slice_in_dim(values, which * mine, mine, 0)

    own_token = own_tiles(token_grad, core) * own_tiles(live, core)[:, None, None, None]
    next_token = over_pair(own_token)
    base = after(base, moving, own_token)
    own_half, normal, inv = front(base, tiles, dw_kernel, dw_bias, ln_gain, ln_bias, mine)
    next_half = over_pair(own_half)
    core_half = over_cores(own_half)
    near[0] = after(near[0], own_half)
    for step in range(1, n_seq):
        far.append(over_groups(near[-1]))
        if step < n_seq - 1:
            near.append(after(over_ring(near[-1]), *far[: step - 1]))
    embed = lax.all_to_all(after(embed_grad[0], near[min(1, n_seq - 2)]), "seq", split_axis=0, concat_axis=1, tiled=True)
    pooled = after(embed, near[-1]) * live[:, None]
    next_pooled = over_pair(pooled)
    core_token = own_tiles(token_grad, 1 - core) * own_tiles(live, 1 - core)[:, None, None, None]

    def branch_grad(tokens, pools, which):
        own_pools = lax.dynamic_slice_in_dim(pools, which * mine, mine, 0).astype(F32) / spots
        return (layer_scale * (tokens.astype(F32) + own_pools[:, None, None, :])).astype(BF16).reshape(mine * spots, channels)

    branch = (
        branch_grad(own_token, pooled, core),
        branch_grad(core_token, pooled, 1 - core),
        branch_grad(next_token, next_pooled, core),
        branch_grad(over_cores(next_token), next_pooled, 1 - core),
    )
    bias = lax.dynamic_slice_in_dim(b_up, side, part, 0)[None, :]
    normed = (own_half, core_half, next_half, over_cores(next_half))
    slope, part_down, whole_up, whole_down, normed, branch = up(place, normed, branch, bias, (w_up, w_down), near, far)
    fall = hop(chunk(part_down, 1 % n_seq), part_down, 1)
    hidden_grad = down(branch, slope, whole_down)
    part_up = rise(normed, after(hidden_grad, fall))
    climb = chunk(part_up, 1 % n_seq)
    keep, send = back(after(hidden_grad, climb), whole_up)
    from_core = over_cores(send)
    from_pair = over_pair((keep[1].astype(F32) + from_core[1].astype(F32)).astype(BF16))
    near_grad = keep[0].astype(F32) + from_core[0].astype(F32)
    for step in range(1, n_seq):
        climb = hop(climb, part_up, step)
        if step < n_seq - 1:
            fall = hop(fall, part_down, step + 1)
        if step == 1:
            from_pair, climb, fall = lax.optimization_barrier((from_pair, climb, fall))
    own_pooled = lax.dynamic_slice_in_dim(pooled, core * mine, mine, 0).astype(F32)[:, None, :] / spots
    grad_half = tail(base, live_tiles, near_grad, from_pair, normal, inv, token_grad, own_pooled, dw_kernel, ln_gain)
    tile_grad = lax.all_gather(grad_half, "mp", axis=0, tiled=True)
    return (tile_grad, both_sides(climb), both_sides(fall))


def solution(mesh):
    sizes = (mesh.shape["seq"], mesh.shape["dp"])
    return jax.shard_map(
        functools.partial(on_device, sizes),
        mesh=mesh,
        in_specs=(
            P(("groups", "seq", "dp"), None, None, None),
            P(("groups", "seq", "dp"), None, None, None),
            P("dp", "groups", "seq"),
            P(("groups", "seq", "dp")),
            P(),
            P(),
            P(),
            P(),
            P("seq", "mp"),
            P("mp"),
            P("seq", "mp"),
            P(),
        ),
        out_specs=(
            P(("groups", "seq", "dp"), None, None, None),
            P(("groups", "seq"), "mp"),
            P(("groups", "seq"), "mp"),
        ),
        check_vma=False,
    )
```

time: 268 us -> 117 us (0.44)
  waiting for transfers between devices: 151 us -> 53 us
  other arithmetic: 63.8 us -> 9.12 us
  Pallas kernels: 0 us -> 25.9 us
  matrix products: 23.4 us -> 0 us
  between operations: 14.9 us -> 1.69 us
  starting transfers between devices: 6.85 us -> 19.3 us
    reduce_scatter x2 -> x0, waiting for transfers between devices: 82.7 us -> none  [the longest x1 43 us: on_device(): lax.psum_scatter(part_down.astype(jnp.bfloat16), 'seq', scatter_dimension...]
    all_gather x2 -> x0, waiting for transfers between devices: 57.1 us -> none  [the longest x1 39 us: on_device(): lax.all_gather(w_down, 'seq', axis=0, tiled=True)]
    ppermute x0 -> x22, waiting for transfers between devices: none -> 47.7 us  [the longest x9 30.7 us: over_ring(): return lax.ppermute(value, 'seq', ring)]
    convert_element_type x8 -> x11, other arithmetic: 45.2 us -> 7.66 us  [the longest x6 2.99 us: hop(): return arrived.astype(BF16)]
    pallas_call x0 -> x6, Pallas kernels: none -> 25.9 us  [the longest x1 8.44 us: up(): pl.pallas_call(functools.partial(up_kernel, hops, tuple(apart)), name='up...]
    dot_general x5 -> x0, matrix products: 23.4 us -> none  [the longest x1 5.67 us: on_device(): jnp.dot(branch_grad, full_down, preferred_element_type=jnp.float32)]
    reduce_sum x4 -> x0, other arithmetic: 16.5 us -> none  [the longest x1 13 us: normalize(): center = jnp.mean(values, axis=-1, keepdims=True)]
    ppermute x0 -> x22, starting transfers between devices: none -> 14.3 us  [the longest x9 5.54 us: over_ring(): return lax.ppermute(value, 'seq', ring)]
  transfers between devices with their start and end apart: 7 -> 23, of which waited for: 6 -> 14; matrix products, arithmetic and copies ran while one was open for 30% -> 7% of each run, Pallas kernels for 0% -> 12%
where the time goes in v2:
time: 117 us; the launch traced here: 116 us
  waiting for transfers between devices  53 us (45%)
  Pallas kernels  25.9 us (22%)
  starting transfers between devices  19.3 us (16%)
  other arithmetic  9.12 us (8%)
  local copies, waits for them, and re-layouts  4.86 us (4%)
  blocking collectives  2.5 us (2%)
  between operations  1.69 us (1%)
    ppermute x9, waiting for transfers between devices, over_ring(): return lax.ppermute(value, 'seq', ring)  30.7 us
    ppermute x6, waiting for transfers between devices, over_pair(): return lax.ppermute(value, 'dp', pair)  9.3 us
    pallas_call x1, Pallas kernels, up(): pl.pallas_call(functools.partial(up_kernel, hops, tuple(apart)), name='up...  8.44 us
    ppermute x9, starting transfers between devices, over_ring(): return lax.ppermute(value, 'seq', ring)  5.54 us
    pallas_call x1, Pallas kernels, front(): pl.pallas_call(front_kernel, name='conv_norm', out_shape=(pltpu.HBM((rows...  5.46 us
    pallas_call x1, Pallas kernels, tail(): pl.pallas_call(tail_kernel, name='norm_conv_back', out_shape=jax.ShapeDty...  5.4 us
    ppermute x3, waiting for transfers between devices, over_groups(): return lax.ppermute(value, 'groups', swap)  5.27 us
    all_to_all x1, waiting for transfers between devices, on_device(): lax.all_to_all(after(embed_grad[0], near[min(1, n_seq - 2)]), 'seq', spli...  5.23 us
  transfers between devices with their start and end apart: 23, of which 14 were waited for; matrix products, arithmetic and copies ran while one was open for 7% of the time, Pallas kernels for 12%

profile of v2, /device:TPU:0, one launch (start us, length us, event | category | flops | bytes accessed | tf_op | source)
XLA Modules:
  0.0 116.4 jit_solution(10752389421457268531)
XLA Ops:
  0.7 1.1 dynamic-slice_bitcast_fusion.2
  1.8 3.1 %collective-permute-start.3 = (bf16[2,96,640]{2,1,0:T(8,128)(2,1)S(1)}, bf16[2,96,640]{2,1,0:T(8,128)(2,1)}, u32[]{:S(2)}, u32[]{:S(2)}) collective-permute-start(bf16[2,96,640]{2,1,0:T(8,128)(2,1)S(1)} %pad_maximum_fusion), channel_id=1, source_target_pairs={{0,4},{4,8},{8,12},{12,0},{1,5},{5,9},{9,13},{13,1},{2,6},{6,10},{... | collective-permute-start | bytes 737288 | tf_op jit(solution)/shard_map/ppermute | solution.py:389
  5.7 1.1 dynamic-slice_multiply_fusion
  6.8 1.6 %collective-permute-start.7 = (bf16[5,8,8,768]{3,2,1,0:T(8,128)(2,1)S(1)}, bf16[5,8,8,768]{3,2,1,0:T(8,128)(2,1)}, u32[]{:S(2)}, u32[]{:S(2)}) collective-permute-start(bf16[5,8,8,768]{3,2,1,0:T(8,128)(2,1)S(1)} %dynamic-slice_multiply_fusion), channel_id=1, source_target_pairs={{0,2},{2,0},{1,3},{3,1},{4,6},{6,4},{5,7},{7,5},{8,10},{10,8},{9,1... | collective-permute-start | bytes 1474568 | tf_op jit(solution)/shard_map/ppermute | solution.py:392
  8.4 5.5 %conv_norm.1 = (bf16[320,768]{1,0:T(8,128)(2,1)}, f32[320,768]{1,0:T(8,128)}, f32[320,128]{1,0:T(8,128)}) custom-call(s32[1]{0:T(128)} %bitcast.base_ref, bf16[10,8,8,768]{3,2,1,0:T(8,128)(2,1)S(1)} %copy-done, f32[7,7,768]{2,1,0:T(8,128)S(1)} %copy-done.1, f32[768]{0:T(1024)S(1)} %copy-done.3, f32[768]{0:T(1024)S(1)} %copy-done.5, f32[768]{0:T(1024)S(1)} %copy-done.4), custom_call_target="tpu_custom_call" | custom-call | flops 10737418240 | bytes 4194304 | tf_op jit(solution)/shard_map/conv_norm/pallas_call | solution.py:110
  13.9 1.6 %collective-permute-start.4 = (bf16[2,96,640]{2,1,0:T(8,128)(2,1)}, bf16[2,96,640]{2,1,0:T(8,128)(2,1)S(1)}, u32[]{:S(2)}, u32[]{:S(2)}) collective-permute-start(bf16[2,96,640]{2,1,0:T(8,128)(2,1)} %collective-permute-done.3.rest_11_), channel_id=1, source_target_pairs={{0,4},{4,8},{8,12},{12,0},{1,5},{5,9},{9,13},{13,1},{2,6},{6,10},{... | collective-permute-start | bytes 737288 | tf_op jit(solution)/shard_map/ppermute | solution.py:389
  15.5 0.5 collective-permute-start.1
  16.1 1.5 %collective-permute-start.6 = (bf16[2,96,640]{2,1,0:T(8,128)(2,1)}, bf16[2,96,640]{2,1,0:T(8,128)(2,1)S(1)}, u32[]{:S(2)}, u32[]{:S(2)}) collective-permute-start(bf16[2,96,640]{2,1,0:T(8,128)(2,1)} %collective-permute-done.3.rest_11_), channel_id=1, source_target_pairs={{0,16},{16,0},{1,17},{17,1},{2,18},{18,2},{3,19},{19,3},{4,20},{20... | collective-permute-start | bytes 737288 | tf_op jit(solution)/shard_map/ppermute | solution.py:398
  17.6 5.5 %collective-permute-done.4.rest_12_ = bf16[2,96,640]{2,1,0:T(8,128)(2,1)S(1)} collective-permute-done((bf16[2,96,640]{2,1,0:T(8,128)(2,1)}, bf16[2,96,640]{2,1,0:T(8,128)(2,1)S(1)}, u32[]{:S(2)}, u32[]{:S(2)}) %collective-permute-start.4) | collective-permute-done | bytes 245792 | tf_op jit(solution)/shard_map/ppermute | solution.py:389
  23.2 0.7 reshape.77
  23.9 5.1 %all-to-all-start = ((bf16[4,2,960]{2,1,0:T(2,128)(2,1)}), bf16[4,2,960]{2,1,0:T(2,128)(2,1)S(1)}, u32[]{:S(2)}, u32[]{:S(2)}) async-start(bf16[4,2,960]{2,1,0:T(2,128)(2,1)} %reshape.77), calls=%async_computation | async-start | bytes 32768 | tf_op jit(solution)/shard_map/all_to_all | solution.py:439
  28.9 0.2 collective-permute-start.9
  29.3 5.2 %all-to-all-done = bf16[4,2,960]{2,1,0:T(2,128)(2,1)S(1)} async-done(((bf16[4,2,960]{2,1,0:T(2,128)(2,1)}), bf16[4,2,960]{2,1,0:T(2,128)(2,1)S(1)}, u32[]{:S(2)}, u32[]{:S(2)}) %all-to-all-start) | async-done | bytes 15392 | tf_op jit(solution)/shard_map/all_to_all | solution.py:439
  34.8 1.6 %collective-permute-start.10 = (bf16[2,96,640]{2,1,0:T(8,128)(2,1)S(1)}, bf16[2,96,640]{2,1,0:T(8,128)(2,1)S(1)}, u32[]{:S(2)}, u32[]{:S(2)}) collective-permute-start(bf16[2,96,640]{2,1,0:T(8,128)(2,1)S(1)} %collective-permute-done.4.rest_12_), channel_id=1, source_target_pairs={{0,16},{16,0},{1,17},{17,1},{2,18},{18,2},{3,19},{19,3},{4,20},{20... | collective-permute-start | bytes 737288 | tf_op jit(solution)/shard_map/ppermute | solution.py:398
  36.5 0.5 collective-permute-start.8
  37.0 3.3 %collective-permute-done.8 = bf16[10,768]{1,0:T(8,128)(2,1)S(1)} collective-permute-done((bf16[10,768]{1,0:T(8,128)(2,1)S(1)}, bf16[10,768]{1,0:T(8,128)(2,1)S(1)}, u32[]{:S(2)}, u32[]{:S(2)}) %collective-permute-start.8) | collective-permute-done | bytes 15392 | tf_op jit(solution)/shard_map/ppermute | solution.py:392
  40.3 0.5 collective-permute-start.11
  40.8 1.6 %multiply_convert_fusion = (bf16[5,8,8,768]{3,2,1,0:T(8,128)(2,1)S(1)}, bf16[5,8,8,768]{3,2,1,0:T(8,128)(2,1)S(1)}, bf16[5,8,8,768]{3,2,1,0:T(8,128)(2,1)S(1)}, bf16[5,8,8,768]{3,2,1,0:T(8,128)(2,1)S(1)}) fusion(bf16[5,8,8,768]{3,2,1,0:T(8,128)(2,1)S(1)} %collective-permute-done.9, f32[5,768]{1,0:T(8,128)S(1)} %get-tuple-element.51, f32[768]{0:T(1024)S(1)} %copy-done.8, ...), kind=kLoop, calls=%fused_computation.2 | loop fusion | flops 4423680 | bytes 3996700 | tf_op jit(solution)/shard_map/convert_element_type | solution.py:446
  42.5 5.3 %collective-permute-done.11.rest_16_ = bf16[2,96,640]{2,1,0:T(8,128)(2,1)S(1)} collective-permute-done((bf16[2,96,640]{2,1,0:T(8,128)(2,1)S(1)}, bf16[2,96,640]{2,1,0:T(8,128)(2,1)S(1)}, u32[]{:S(2)}, u32[]{:S(2)}) %collective-permute-start.11) | collective-permute-done | bytes 245792 | tf_op jit(solution)/shard_map/ppermute | solution.py:398
  47.8 8.4 %up_and_down_grad.1 = (f32[1280,640]{1,0:T(8,128)S(1)}, bf16[768,640]{1,0:T(8,128)(2,1)S(1)}, bf16[768,640]{1,0:T(8,128)(2,1)S(1)}, bf16[768,640]{1,0:T(8,128)(2...) custom-call(s32[7]{0:T(128)S(1)} %pad_add_fusion.place_ref, ...), custom_call_target="tpu_custom_call" | custom-call | flops 10737418240 | bytes 4194304 | tf_op jit(solution)/shard_map/up_and_down_grad/pallas_call | solution.py:199
  56.3 0.7 collective-permute-start.12
  57.0 3.2 %hidden_grad.1.grad_ref = bf16[1280,640]{1,0:T(8,128)(2,1)S(1)} custom-call(bf16[1280,768]{1,0:T(8,128)(2,1)S(1)} %get-tuple-element.32.branch_ref, f32[1280,640]{1,0:T(8,128)S(1)} %get-tuple-element.33.slope_ref, bf16[768,640]{1,0:T(8,128)(2,1)S(1)} %get-tuple-element.34.weight_ref), custom_call_target="tpu_custom_call" | custom-call | flops 10737418240 | bytes 4194304 | tf_op jit(solution)/shard_map/hidden_grad/pallas_call | solution.py:238
  60.2 4.6 %collective-permute-done.12 = bf16[192,640]{1,0:T(8,128)(2,1)S(1)} collective-permute-done((bf16[192,640]{1,0:T(8,128)(2,1)S(1)}, bf16[192,640]{1,0:T(8,128)(2,1)S(1)}, u32[]{:S(2)}, u32[]{:S(2)}) %collective-permute-start.12) | collective-permute-done | bytes 245792 | tf_op jit(solution)/shard_map/ppermute | solution.py:389
  64.7 0.8 fusion.6
  65.5 1.7 %up_grad.1 = bf16[768,640]{1,0:T(8,128)(2,1)S(1)} custom-call(bf16[1280,768]{1,0:T(8,128)(2,1)S(1)} %get-tuple-element.35.normed_ref, bf16[1280,640]{1,0:T(8,128)(2,1)S(1)} %hidden_grad.1.grad_ref), custom_call_target="tpu_custom_call" | custom-call | flops 10737418240 | bytes 4194304 | tf_op jit(solution)/shard_map/up_grad/pallas_call | solution.py:255
  67.3 0.7 dynamic-slice_bitcast_fusion
  68.0 1.7 %normed_grad.1 = (bf16[2,320,768]{2,1,0:T(8,128)(2,1)S(1)}, bf16[2,320,768]{2,1,0:T(8,128)(2,1)S(1)}) custom-call(bf16[1280,640]{1,0:T(8,128)(2,1)S(1)} %hidden_grad.1.grad_ref, bf16[768,640]{1,0:T(8,128)(2,1)S(1)} %get-tuple-element.39.weight_ref), custom_call_target="tpu_custom_call" | custom-call | flops 10737418240 | bytes 4194304 | tf_op jit(solution)/shard_map/normed_grad/pallas_call | solution.py:277
  69.9 2.5 %collective-permute-done.13 = bf16[2,320,768]{2,1,0:T(8,128)(2,1)S(1)} collective-permute-done((bf16[2,320,768]{2,1,0:T(8,128)(2,1)S(1)}, bf16[2,320,768]{2,1,0:T(8,128)(2,1)S(1)}, u32[]{:S(2)}, u32[]{:S(2)}) %collective-permute-start.13) | collective-permute-done | bytes 983072 | tf_op jit(solution)/shard_map/ppermute | solution.py:395
  72.3 1.0 fusion
  73.4 0.5 collective-permute-start.14
  73.9 6.8 %collective-permute-done.15 = bf16[192,640]{1,0:T(8,128)(2,1)} collective-permute-done((bf16[192,640]{1,0:T(8,128)(2,1)}, bf16[192,640]{1,0:T(8,128)(2,1)}, u32[]{:S(2)}, u32[]{:S(2)}) %collective-permute-start.15) | collective-permute-done | bytes 245792 | tf_op jit(solution)/shard_map/ppermute | solution.py:389
  80.7 1.0 fusion.5
  81.7 3.8 %collective-permute-done.16 = bf16[192,640]{1,0:T(8,128)(2,1)} collective-permute-done((bf16[192,640]{1,0:T(8,128)(2,1)}, bf16[192,640]{1,0:T(8,128)(2,1)}, u32[]{:S(2)}, u32[]{:S(2)}) %collective-permute-start.16) | collective-permute-done | bytes 245792 | tf_op jit(solution)/shard_map/ppermute | solution.py:389
  85.5 1.0 fusion.4
  86.5 0.3 collective-permute-done.14.far_ref
  86.9 0.9 copy-done.2
  87.8 5.4 %norm_conv_back.1 = bf16[5,8,8,768]{3,2,1,0:T(8,128)(2,1)S(1)} custom-call(s32[1]{0:T(128)} %bitcast.base_ref, s32[1]{0:T(128)} %copy.19.live_ref, f32[320,768]{1,0:T(8,128)} %get-tuple-element.25.normal_in, f32[320,128]{1,0:T(8,128)} %get-tuple-element.26.inv_in, bf16[10,8,8,768]{3,2,1,0:T(8,128)(2,1)} %token_in.1, ...), custom_call_target="tpu_custom_call" | custom-call | flops 10737418240 | bytes 4194304 | tf_op jit(solution)/shard_map/norm_conv_back/pallas_call | solution.py:339
  93.2 4.4 %collective-permute-done.17 = bf16[192,640]{1,0:T(8,128)(2,1)S(1)} collective-permute-done((bf16[192,640]{1,0:T(8,128)(2,1)S(1)}, bf16[192,640]{1,0:T(8,128)(2,1)S(1)}, u32[]{:S(2)}, u32[]{:S(2)}) %collective-permute-start.17) | collective-permute-done | bytes 245792 | tf_op jit(solution)/shard_map/ppermute | solution.py:389
  97.7 5.1 %collective-permute-done.20 = bf16[192,640]{1,0:T(8,128)(2,1)S(1)} collective-permute-done((bf16[192,640]{1,0:T(8,128)(2,1)S(1)}, bf16[192,640]{1,0:T(8,128)(2,1)S(1)}, u32[]{:S(2)}, u32[]{:S(2)}) %collective-permute-start.20) | collective-permute-done | bytes 245792 | tf_op jit(solution)/shard_map/ppermute | solution.py:389
  102.9 0.6 collective-permute-start.21
  103.5 2.5 %all_gather.3 = bf16[10,8,8,768]{3,2,1,0:T(8,128)(2,1)S(1)} all-gather(bf16[5,8,8,768]{3,2,1,0:T(8,128)(2,1)S(1)} %norm_conv_back.1), channel_id=1, replica_groups=mesh['groups'=2,'seq'=4,'dp'=2,'mp'=2] {'mp'}, dimensions={0}, use_global_device_ids=true | all-gather | bytes 1474560 | tf_op jit(solution)/shard_map/all_gather | solution.py:473
  106.0 0.5 collective-permute-done.18
  106.5 1.1 collective-permute-start.19
  107.6 1.8 %collective-permute-done.21 = bf16[192,640]{1,0:T(8,128)(2,1)S(1)} collective-permute-done((bf16[192,640]{1,0:T(8,128)(2,1)S(1)}, bf16[192,640]{1,0:T(8,128)(2,1)S(1)}, u32[]{:S(2)}, u32[]{:S(2)}) %collective-permute-start.21) | collective-permute-done | bytes 245792 | tf_op jit(solution)/shard_map/ppermute | solution.py:392
  109.4 1.0 maximum_convert_fusion.1
  110.4 4.0 %collective-permute-done.19 = bf16[192,640]{1,0:T(8,128)(2,1)S(1)} collective-permute-done((bf16[192,640]{1,0:T(8,128)(2,1)S(1)}, bf16[192,640]{1,0:T(8,128)(2,1)S(1)}, u32[]{:S(2)}, u32[]{:S(2)}) %collective-permute-start.19) | collective-permute-done | bytes 245792 | tf_op jit(solution)/shard_map/ppermute | solution.py:392
  114.5 1.0 maximum_convert_fusion
  115.5 0.9 copy.20
  (64 shorter events, 1.3 us)
Async XLA Ops:
  0.6 7.7 %copy-start.5 = (f32[768]{0:T(1024)S(1)}, f32[768]{0:T(1024)}, u32[]{:S(2)}) copy-start(f32[768]{0:T(1024)} %gain_ref.3) | copy-start | bytes 9220
  0.6 7.7 %copy-start.1 = (f32[7,7,768]{2,1,0:T(8,128)S(1)}, f32[7,7,768]{2,1,0:T(8,128)}, u32[]{:S(2)}) copy-start(f32[7,7,768]{2,1,0:T(8,128)} %taps_ref.3) | copy-start | bytes 451588
  0.7 7.7 %copy-start.4 = (f32[768]{0:T(1024)S(1)}, f32[768]{0:T(1024)}, u32[]{:S(2)}) copy-start(f32[768]{0:T(1024)} %shift_ref.1) | copy-start | bytes 9220
  0.7 7.7 %copy-start.3 = (f32[768]{0:T(1024)S(1)}, f32[768]{0:T(1024)}, u32[]{:S(2)}) copy-start(f32[768]{0:T(1024)} %bias_ref.1) | copy-start | bytes 9220
  0.7 7.7 %copy-start = (bf16[10,8,8,768]{3,2,1,0:T(8,128)(2,1)S(1)}, bf16[10,8,8,768]{3,2,1,0:T(8,128)(2,1)}, u32[]{:S(2)}) copy-start(bf16[10,8,8,768]{3,2,1,0:T(8,128)(2,1)} %tiles_ref.1) | copy-start | bytes 2949124
  1.8 12.1 %collective-permute-start.3 = (bf16[2,96,640]{2,1,0:T(8,128)(2,1)S(1)}, bf16[2,96,640]{2,1,0:T(8,128)(2,1)}, u32[]{:S(2)}, u32[]{:S(2)}) collective-permute-start(bf16[2,96,640]{2,1,0:T(8,128)(2,1)S(1)} %pad_maximum_fusion), channel_id=1, source_target_pairs={{0,4},{4,8},{8,12},{12,0},{1,5},{5,9},{9,13},{13,1},{2,6},{6,10},{... | collective-permute-start | bytes 737288 | tf_op jit(solution)/shard_map/ppermute | solution.py:389
  6.8 22.1 %collective-permute-start.7 = (bf16[5,8,8,768]{3,2,1,0:T(8,128)(2,1)S(1)}, bf16[5,8,8,768]{3,2,1,0:T(8,128)(2,1)}, u32[]{:S(2)}, u32[]{:S(2)}) collective-permute-start(bf16[5,8,8,768]{3,2,1,0:T(8,128)(2,1)S(1)} %dynamic-slice_multiply_fusion), channel_id=1, source_target_pairs={{0,2},{2,0},{1,3},{3,1},{4,6},{6,4},{5,7},{7,5},{8,10},{10,8},{9,1... | collective-permute-start | bytes 1474568 | tf_op jit(solution)/shard_map/ppermute | solution.py:392
  8.4 14.8 %copy-start.7 = (bf16[1,40,192]{2,1,0:T(8,128)(2,1)S(1)}, bf16[1,40,192]{2,1,0:T(8,128)(2,1)}, u32[]{:S(2)}) copy-start(bf16[1,40,192]{2,1,0:T(8,128)(2,1)} %param.14) | copy-start | bytes 46084
  8.4 20.9 %copy-start.9 = (f32[1280]{0:T(1024)S(1)}, f32[1280]{0:T(1024)}, u32[]{:S(2)}) copy-start(f32[1280]{0:T(1024)} %param.21) | copy-start | bytes 15364
  8.4 32.4 %copy-start.6 = (bf16[10,8,8,768]{3,2,1,0:T(8,128)(2,1)S(1)}, bf16[10,8,8,768]{3,2,1,0:T(8,128)(2,1)}, u32[]{:S(2)}) copy-start(bf16[10,8,8,768]{3,2,1,0:T(8,128)(2,1)} %token_in.1) | copy-start | bytes 2949124
  8.4 32.4 %copy-start.8 = (f32[768]{0:T(1024)S(1)}, f32[768]{0:T(1024)}, u32[]{:S(2)}) copy-start(f32[768]{0:T(1024)} %param.23) | copy-start | bytes 9220
  13.9 9.2 %collective-permute-start.4 = (bf16[2,96,640]{2,1,0:T(8,128)(2,1)}, bf16[2,96,640]{2,1,0:T(8,128)(2,1)S(1)}, u32[]{:S(2)}, u32[]{:S(2)}) collective-permute-start(bf16[2,96,640]{2,1,0:T(8,128)(2,1)} %collective-permute-done.3.rest_11_), channel_id=1, source_target_pairs={{0,4},{4,8},{8,12},{12,0},{1,5},{5,9},{9,13},{13,1},{2,6},{6,10},{... | collective-permute-start | bytes 737288 | tf_op jit(solution)/shard_map/ppermute | solution.py:389
  15.5 20.8 %collective-permute-start.1 = (bf16[320,768]{1,0:T(8,128)(2,1)}, bf16[320,768]{1,0:T(8,128)(2,1)S(1)}, u32[]{:S(2)}, u32[]{:S(2)}) collective-permute-start(bf16[320,768]{1,0:T(8,128)(2,1)} %get-tuple-element.27.rest_0_), channel_id=1, source_target_pairs={{0,2},{2,0},{1,3},{3,1},{4,6},{6,4},{5,7},{7,5},{8,10},{10,8},{9,1... | collective-permute-start | bytes 1474568 | tf_op jit(solution)/shard_map/ppermute | solution.py:392
  16.1 18.7 %collective-permute-start.6 = (bf16[2,96,640]{2,1,0:T(8,128)(2,1)}, bf16[2,96,640]{2,1,0:T(8,128)(2,1)S(1)}, u32[]{:S(2)}, u32[]{:S(2)}) collective-permute-start(bf16[2,96,640]{2,1,0:T(8,128)(2,1)} %collective-permute-done.3.rest_11_), channel_id=1, source_target_pairs={{0,16},{16,0},{1,17},{17,1},{2,18},{18,2},{3,19},{19,3},{4,20},{20... | collective-permute-start | bytes 737288 | tf_op jit(solution)/shard_map/ppermute | solution.py:398
  23.1 19.4 %copy-start.11 = (bf16[2,96,640]{2,1,0:T(8,128)(2,1)}, bf16[2,96,640]{2,1,0:T(8,128)(2,1)S(1)}, u32[]{:S(2)}) copy-start(bf16[2,96,640]{2,1,0:T(8,128)(2,1)S(1)} %collective-permute-done.4.rest_12_) | copy-start | bytes 737284
  23.1 13.3 %collective-permute-start.5 = (bf16[2,96,640]{2,1,0:T(8,128)(2,1)S(1)}, bf16[2,96,640]{2,1,0:T(8,128)(2,1)S(1)}, u32[]{:S(2)}, u32[]{:S(2)}) collective-permute-start(bf16[2,96,640]{2,1,0:T(8,128)(2,1)S(1)} %collective-permute-done.4.rest_12_), channel_id=1, source_target_pairs={{0,4},{4,8},{8,12},{12,0},{1,5},{5,9},{9,13},{13,1},{2,6},{6,10},{... | collective-permute-start | bytes 737288 | tf_op jit(solution)/shard_map/ppermute | solution.py:389
  23.1 19.4 %collective-permute-start = (bf16[320,768]{1,0:T(8,128)(2,1)}, bf16[320,768]{1,0:T(8,128)(2,1)S(1)}, u32[]{:S(2)}, u32[]{:S(2)}) collective-permute-start(bf16[320,768]{1,0:T(8,128)(2,1)} %get-tuple-element.27.rest_0_), channel_id=1, source_target_pairs={{0,1},{1,0},{2,3},{3,2},{4,5},{5,4},{6,7},{7,6},{8,9},{9,8},{10,11... | collective-permute-start | bytes 1474568 | tf_op jit(solution)/shard_map/ppermute | solution.py:395
  23.9 10.7 %all-to-all-start = ((bf16[4,2,960]{2,1,0:T(2,128)(2,1)}), bf16[4,2,960]{2,1,0:T(2,128)(2,1)S(1)}, u32[]{:S(2)}, u32[]{:S(2)}) async-start(bf16[4,2,960]{2,1,0:T(2,128)(2,1)} %reshape.77), calls=%async_computation | async-start | bytes 32768 | tf_op jit(solution)/shard_map/all_to_all | solution.py:439
  28.9 11.9 %collective-permute-start.9 = (bf16[5,8,8,768]{3,2,1,0:T(8,128)(2,1)}, bf16[5,8,8,768]{3,2,1,0:T(8,128)(2,1)S(1)}, u32[]{:S(2)}, u32[]{:S(2)}) collective-permute-start(bf16[5,8,8,768]{3,2,1,0:T(8,128)(2,1)} %collective-permute-done.7), channel_id=1, source_target_pairs={{0,1},{1,0},{2,3},{3,2},{4,5},{5,4},{6,7},{7,6},{8,9},{9,8},{10,11... | collective-permute-start | bytes 1474568 | tf_op jit(solution)/shard_map/ppermute | solution.py:395
  34.8 7.7 %copy-start.12 = (bf16[2,96,640]{2,1,0:T(8,128)(2,1)}, bf16[2,96,640]{2,1,0:T(8,128)(2,1)S(1)}, u32[]{:S(2)}) copy-start(bf16[2,96,640]{2,1,0:T(8,128)(2,1)S(1)} %collective-permute-done.6.rest_14_) | copy-start | bytes 737284
  34.8 7.7 %collective-permute-start.10 = (bf16[2,96,640]{2,1,0:T(8,128)(2,1)S(1)}, bf16[2,96,640]{2,1,0:T(8,128)(2,1)S(1)}, u32[]{:S(2)}, u32[]{:S(2)}) collective-permute-start(bf16[2,96,640]{2,1,0:T(8,128)(2,1)S(1)} %collective-permute-done.4.rest_12_), channel_id=1, source_target_pairs={{0,16},{16,0},{1,17},{17,1},{2,18},{18,2},{3,19},{19,3},{4,20},{20... | collective-permute-start | bytes 737288 | tf_op jit(solution)/shard_map/ppermute | solution.py:398
  36.4 11.4 %collective-permute-start.2 = (bf16[320,768]{1,0:T(8,128)(2,1)S(1)}, bf16[320,768]{1,0:T(8,128)(2,1)S(1)}, u32[]{:S(2)}, u32[]{:S(2)}) collective-permute-start(bf16[320,768]{1,0:T(8,128)(2,1)S(1)} %collective-permute-done.1.rest_2_), channel_id=1, source_target_pairs={{0,1},{1,0},{2,3},{3,2},{4,5},{5,4},{6,7},{7,6},{8,9},{9,8},{10,11... | collective-permute-start | bytes 1474568 | tf_op jit(solution)/shard_map/ppermute | solution.py:395
  36.5 3.8 %collective-permute-start.8 = (bf16[10,768]{1,0:T(8,128)(2,1)S(1)}, bf16[10,768]{1,0:T(8,128)(2,1)S(1)}, u32[]{:S(2)}, u32[]{:S(2)}) collective-permute-start(bf16[10,768]{1,0:T(8,128)(2,1)S(1)} %broadcast_multiply_fusion), channel_id=1, source_target_pairs={{0,2},{2,0},{1,3},{3,1},{4,6},{6,4},{5,7},{7,5},{8,10},{10,8},{9,1... | collective-permute-start | bytes 46088 | tf_op jit(solution)/shard_map/ppermute | solution.py:392
  40.3 7.5 %collective-permute-start.11 = (bf16[2,96,640]{2,1,0:T(8,128)(2,1)S(1)}, bf16[2,96,640]{2,1,0:T(8,128)(2,1)S(1)}, u32[]{:S(2)}, u32[]{:S(2)}) collective-permute-start(bf16[2,96,640]{2,1,0:T(8,128)(2,1)S(1)} %collective-permute-done.5.rest_13_), channel_id=1, source_target_pairs={{0,16},{16,0},{1,17},{17,1},{2,18},{18,2},{3,19},{19,3},{4,20},{20... | collective-permute-start | bytes 737288 | tf_op jit(solution)/shard_map/ppermute | solution.py:398
  42.5 5.3 %copy-start.10 = (bf16[320,768]{1,0:T(8,128)(2,1)}, bf16[320,768]{1,0:T(8,128)(2,1)S(1)}, u32[]{:S(2)}) copy-start(bf16[320,768]{1,0:T(8,128)(2,1)S(1)} %collective-permute-done.rest_1_) | copy-start | bytes 1474564
  56.3 8.5 %collective-permute-start.12 = (bf16[192,640]{1,0:T(8,128)(2,1)S(1)}, bf16[192,640]{1,0:T(8,128)(2,1)S(1)}, u32[]{:S(2)}, u32[]{:S(2)}) collective-permute-start(bf16[192,640]{1,0:T(8,128)(2,1)S(1)} %dynamic-slice_bitcast_fusion.1), channel_id=1, source_target_pairs={{0,4},{4,8},{8,12},{12,0},{1,5},{5,9},{9,13},{13,1},{2,6},{6,10},{... | collective-permute-start | bytes 737288 | tf_op jit(solution)/shard_map/ppermute | solution.py:389
  69.7 2.6 %collective-permute-start.13 = (bf16[2,320,768]{2,1,0:T(8,128)(2,1)S(1)}, bf16[2,320,768]{2,1,0:T(8,128)(2,1)S(1)}, u32[]{:S(2)}, u32[]{:S(2)}) collective-permute-start(bf16[2,320,768]{2,1,0:T(8,128)(2,1)S(1)} %get-tuple-element.41), channel_id=1, source_target_pairs={{0,1},{1,0},{2,3},{3,2},{4,5},{5,4},{6,7},{7,6},{8,9},{9,8},{10,11... | collective-permute-start | bytes 2949128 | tf_op jit(solution)/shard_map/ppermute | solution.py:395
  69.8 10.9 %collective-permute-start.15 = (bf16[192,640]{1,0:T(8,128)(2,1)}, bf16[192,640]{1,0:T(8,128)(2,1)}, u32[]{:S(2)}, u32[]{:S(2)}) collective-permute-start(bf16[192,640]{1,0:T(8,128)(2,1)} %dynamic-slice_bitcast_fusion), channel_id=1, source_target_pairs={{0,4},{4,8},{8,12},{12,0},{1,5},{5,9},{9,13},{13,1},{2,6},{6,10},{... | collective-permute-start | bytes 737288 | tf_op jit(solution)/shard_map/ppermute | solution.py:389
  73.4 13.5 %collective-permute-start.14 = (bf16[320,768]{1,0:T(8,128)(2,1)}, bf16[320,768]{1,0:T(8,128)(2,1)S(1)}, u32[]{:S(2)}, u32[]{:S(2)}) collective-permute-start(bf16[320,768]{1,0:T(8,128)(2,1)} %get-tuple-element.45), channel_id=1, source_target_pairs={{0,2},{2,0},{1,3},{3,1},{4,6},{6,4},{5,7},{7,5},{8,10},{10,8},{9,1... | collective-permute-start | bytes 1474568 | tf_op jit(solution)/shard_map/ppermute | solution.py:392
  73.9 11.6 %collective-permute-start.16 = (bf16[192,640]{1,0:T(8,128)(2,1)}, bf16[192,640]{1,0:T(8,128)(2,1)}, u32[]{:S(2)}, u32[]{:S(2)}) collective-permute-start(bf16[192,640]{1,0:T(8,128)(2,1)} %fusion.6), channel_id=1, source_target_pairs={{0,4},{4,8},{8,12},{12,0},{1,5},{5,9},{9,13},{13,1},{2,6},{6,10},{... | collective-permute-start | bytes 737288 | tf_op jit(solution)/shard_map/ppermute | solution.py:389
  86.8 10.7 %collective-permute-start.17 = (bf16[192,640]{1,0:T(8,128)(2,1)S(1)}, bf16[192,640]{1,0:T(8,128)(2,1)S(1)}, u32[]{:S(2)}, u32[]{:S(2)}) collective-permute-start(bf16[192,640]{1,0:T(8,128)(2,1)S(1)} %fusion.5), channel_id=1, source_target_pairs={{0,4},{4,8},{8,12},{12,0},{1,5},{5,9},{9,13},{13,1},{2,6},{6,10},{... | collective-permute-start | bytes 737288 | tf_op jit(solution)/shard_map/ppermute | solution.py:389
  86.8 16.0 %collective-permute-start.20 = (bf16[192,640]{1,0:T(8,128)(2,1)S(1)}, bf16[192,640]{1,0:T(8,128)(2,1)S(1)}, u32[]{:S(2)}, u32[]{:S(2)}) collective-permute-start(bf16[192,640]{1,0:T(8,128)(2,1)S(1)} %fusion.4), channel_id=1, source_target_pairs={{0,4},{4,8},{8,12},{12,0},{1,5},{5,9},{9,13},{13,1},{2,6},{6,10},{... | collective-permute-start | bytes 737288 | tf_op jit(solution)/shard_map/ppermute | solution.py:389
  86.8 0.9 copy-start.2
  97.6 8.9 %collective-permute-start.18 = (bf16[192,640]{1,0:T(8,128)(2,1)S(1)}, bf16[192,640]{1,0:T(8,128)(2,1)S(1)}, u32[]{:S(2)}, u32[]{:S(2)}) collective-permute-start(bf16[192,640]{1,0:T(8,128)(2,1)S(1)} %fusion.3), channel_id=1, source_target_pairs={{0,4},{4,8},{8,12},{12,0},{1,5},{5,9},{9,13},{13,1},{2,6},{6,10},{... | collective-permute-start | bytes 737288 | tf_op jit(solution)/shard_map/ppermute | solution.py:389
  102.9 6.5 %collective-permute-start.21 = (bf16[192,640]{1,0:T(8,128)(2,1)S(1)}, bf16[192,640]{1,0:T(8,128)(2,1)S(1)}, u32[]{:S(2)}, u32[]{:S(2)}) collective-permute-start(bf16[192,640]{1,0:T(8,128)(2,1)S(1)} %fusion.1), channel_id=1, source_target_pairs={{0,2},{2,0},{1,3},{3,1},{4,6},{6,4},{5,7},{7,5},{8,10},{10,8},{9,1... | collective-permute-start | bytes 737288 | tf_op jit(solution)/shard_map/ppermute | solution.py:392
  106.5 7.9 %collective-permute-start.19 = (bf16[192,640]{1,0:T(8,128)(2,1)S(1)}, bf16[192,640]{1,0:T(8,128)(2,1)S(1)}, u32[]{:S(2)}, u32[]{:S(2)}) collective-permute-start(bf16[192,640]{1,0:T(8,128)(2,1)S(1)} %fusion.2), channel_id=1, source_target_pairs={{0,2},{2,0},{1,3},{3,1},{4,6},{6,4},{5,7},{7,5},{8,10},{10,8},{9,1... | collective-permute-start | bytes 737288 | tf_op jit(solution)/shard_map/ppermute | solution.py:392

commit v3 on v2

v3 whole, which is shorter than its diff:
```python
import functools
import jax
import jax.numpy as jnp
from jax import lax
from jax.experimental import pallas as pl
from jax.experimental.pallas import tpu as pltpu
from jax.sharding import PartitionSpec as P

sqrt_two_pi = 0.7978845608028654
cubic_coef = 0.044715
LANES = 128
F32 = jnp.float32
BF16 = jnp.bfloat16
WHOLE = pl.BlockSpec(memory_space=pltpu.VMEM)
SCALARS = pl.BlockSpec(memory_space=pltpu.SMEM)
APART = pl.BlockSpec(memory_space=pltpu.HBM)


def in_vmem(*values):
    return [pltpu.with_memory_space_constraint(value, pltpu.VMEM) for value in values]


def in_hbm(*values):
    return [pltpu.with_memory_space_constraint(value, pltpu.HBM) for value in values]


ROWS = 32
VMEM_LIMIT = 16 << 20


COST = pl.CostEstimate(flops=10 << 30, transcendentals=0, bytes_accessed=4 << 20)


def depthwise_lanes(rows, taps_ref, lanes, reach, flip):
    height, width = len(rows), rows[0].shape[0]
    margin = reach // 2
    place = lax.broadcasted_iota(jnp.int32, rows[0].shape, 0)
    total = [None] * height
    for col in range(reach):
        shift = col - margin
        if shift:
            inside = (place + shift >= 0) & (place + shift < width)
            moved = [jnp.where(inside, pltpu.roll(row, (-shift) % width, 0), 0.0) for row in rows]
        else:
            moved = rows
        for line in range(reach):
            index = line * reach + col
            if flip:
                index = reach * reach - 1 - index
            tap = jnp.broadcast_to(taps_ref[index // reach, pl.ds(index % reach, 1), lanes], rows[0].shape)
            for u in range(height):
                source = u + line - margin
                if 0 <= source < height:
                    term = moved[source] * tap
                    total[u] = term if total[u] is None else total[u] + term
    return total


def front_kernel(
    base_ref, tiles_ref, taps_ref, bias_ref, gain_ref, shift_ref, normed_out, normal_out, inv_out,
    conv_ref, normed_ref, normal_ref, inv_ref, sems,
):
    height, width, channels = tiles_ref.shape[1:]
    spots = height * width
    mine = normed_ref.shape[0] // spots
    reach = taps_ref.shape[0]
    slabs = channels // LANES

    def saves(tile):
        here = pl.ds(pl.multiple_of(tile * spots, spots), spots)
        return (
            pltpu.make_async_copy(normal_ref.at[here], normal_out.at[here], sems.at[0, tile]),
            pltpu.make_async_copy(inv_ref.at[here], inv_out.at[here], sems.at[1, tile]),
            pltpu.make_async_copy(normed_ref.at[here], normed_out.at[here], sems.at[2, tile]),
        )

    def one_tile(tile, carry):
        def slab(block, carry):
            lanes = pl.ds(pl.multiple_of(block * LANES, LANES), LANES)
            rows = [tiles_ref[base_ref[0] + tile, u, :, lanes].astype(F32) for u in range(height)]
            total = depthwise_lanes(rows, taps_ref, lanes, reach, False)
            for u in range(height):
                conv_ref[u * width : (u + 1) * width, lanes] = total[u] + bias_ref[lanes][None, :]
            return carry

        lax.fori_loop(0, slabs, slab, 0)
        for part in range(spots // ROWS):
            conv = conv_ref[part * ROWS : (part + 1) * ROWS, :]
            here = pl.ds(pl.multiple_of(tile * spots + part * ROWS, ROWS), ROWS)
            center = jnp.mean(conv, axis=-1, keepdims=True)
            shifted = conv - center
            inv = lax.rsqrt(jnp.mean(shifted * shifted, axis=-1, keepdims=True) + 1e-06)
            normal = shifted * inv
            normal_ref[here, :] = normal
            inv_ref[here, :] = jnp.broadcast_to(inv, (ROWS, LANES))
            normed_ref[here, :] = (normal * gain_ref[...][None, :] + shift_ref[...][None, :]).astype(BF16)
        for copy in saves(tile):
            copy.start()
        return carry

    lax.fori_loop(0, mine, one_tile, 0)
    for tile in range(mine):
        for copy in saves(tile):
            copy.wait()


def front(base, tiles, taps, bias, gain, shift, mine):
    _, height, width, channels = tiles.shape
    rows = mine * height * width
    return pl.pallas_call(
        front_kernel,
        name="conv_norm",
        out_shape=(
            pltpu.HBM((rows, channels), BF16),
            pltpu.HBM((rows, channels), F32),
            pltpu.HBM((rows, LANES), F32),
        ),
        in_specs=[SCALARS] + [WHOLE] * 5,
        out_specs=[APART] * 3,
        scratch_shapes=[
            pltpu.VMEM((height * width, channels), F32),
            pltpu.VMEM((rows, channels), BF16),
            pltpu.VMEM((rows, channels), F32),
            pltpu.VMEM((rows, LANES), F32),
            pltpu.SemaphoreType.DMA((3, mine)),
        ],
        compiler_params=pltpu.CompilerParams(vmem_limit_bytes=VMEM_LIMIT),
        cost_estimate=COST,
    )(base, tiles, taps, bias, gain, shift)


def store_chunks(seq, total, keep_ref, send_ref):
    shard = keep_ref.shape[1]
    count = total.shape[0] // shard

    def store(place):
        for chunk in range(count):
            away = chunk ^ place
            target = send_ref if away % 2 else keep_ref
            target[away // 2] = total[chunk * shard : (chunk + 1) * shard].astype(BF16)

    for place in range(count):
        pl.when(seq == place)(functools.partial(store, place))


def across_rows(left, right):
    return lax.dot_general(left, right, (((0,), (0,)), ((), ())), preferred_element_type=F32)


def lay_weight(place_ref, local, pieces, apart, whole_ref, sems):
    shard, part = local.shape[0], whole_ref.shape[1]
    pieces = [piece.at[:shard] for piece in pieces]
    columns = pl.ds(pl.multiple_of(place_ref[0], LANES), part)
    sources = [(True, local.at[:, columns])] + list(zip(apart, pieces))
    copies = []
    for k, (outside, source) in enumerate(sources):
        target = whole_ref.at[pl.ds(pl.multiple_of(place_ref[2 + k], 16), shard)]
        if outside:
            copies.append(pltpu.make_async_copy(source, target, sems.at[k]))
            copies[-1].start()
        else:
            target[...] = source[...]
    return copies


def activate(normed, weight_ref, bias_ref, hidden_ref, act_ref, slope_ref, first):
    hidden_ref[...] = jnp.dot(normed, weight_ref[...], preferred_element_type=F32)

    def block(i, carry):
        here = pl.ds(pl.multiple_of(i * ROWS, ROWS), ROWS)
        there = pl.ds(pl.multiple_of(first + i * ROWS, ROWS), ROWS)
        value = hidden_ref[here, :] + bias_ref[...]
        square = value * value
        tangent = jnp.tanh(value * (sqrt_two_pi + (sqrt_two_pi * cubic_coef) * square))
        upper = 0.5 + 0.5 * tangent
        act_ref[there, :] = (value * upper).astype(BF16)
        bend = (0.5 * value) * (1.0 - tangent * tangent)
        slope_ref[there, :] = upper + bend * (sqrt_two_pi + (3.0 * sqrt_two_pi * cubic_coef) * square)
        return carry

    lax.fori_loop(0, hidden_ref.shape[0] // ROWS, block, 0)


def up_kernel(apart, place_ref, own_ref, core_ref, bias_ref, local, *rest):
    hops = len(apart)
    pieces, (act_ref, slope_ref, up_ref, normed_ref, hidden_ref, sems) = rest[:hops], rest[hops:]
    rows = own_ref.shape[0]
    weights = lay_weight(place_ref, local, pieces, apart, up_ref, sems)
    inputs = [
        pltpu.make_async_copy(piece, normed_ref.at[k * rows : (k + 1) * rows], sems.at[1 + hops + k])
        for k, piece in enumerate((own_ref, core_ref))
    ]
    for copy in inputs:
        copy.start()
    for copy in weights:
        copy.wait()
    for k in range(2):
        inputs[k].wait()
        activate(normed_ref[k * rows : (k + 1) * rows, :], up_ref, bias_ref, hidden_ref, act_ref, slope_ref, k * rows)


def up_next_kernel(seq_ref, *rest):
    normed, branch, (bias_ref, up_ref, own_act_ref), rest = rest[:2], rest[2:6], rest[6:9], rest[9:]
    keep_ref, send_ref, slope_ref, normed_ref, branch_ref, hidden_ref, act_ref = rest
    rows = normed[0].shape[0]
    for k in range(2):
        activate(normed[k][...], up_ref, bias_ref, hidden_ref, act_ref, slope_ref, k * rows)
        normed_ref[k * rows : (k + 1) * rows, :] = normed[k][...]
    for k in range(4):
        branch_ref[k * rows : (k + 1) * rows, :] = branch[k][...]
    act = jnp.concatenate([own_act_ref[...], act_ref[...]], axis=0)
    store_chunks(seq_ref[0], across_rows(branch_ref[...], act), keep_ref, send_ref)


def sorted_pieces(pieces):
    apart = tuple(k < len(pieces) - 1 for k in range(len(pieces)))
    pieces = [(in_hbm if outside else in_vmem)(piece)[0] for outside, piece in zip(apart, pieces)]
    return apart, pieces, [APART if outside else WHOLE for outside in apart]


def up(place, own, core, bias, local, pieces):
    rows, channels = own.shape
    columns = pieces[0].shape[1]
    apart, pieces, specs = sorted_pieces(pieces)
    return pl.pallas_call(
        functools.partial(up_kernel, apart),
        name="hidden_own",
        out_shape=(
            pltpu.VMEM((2 * rows, columns), BF16),
            pltpu.VMEM((2 * rows, columns), F32),
            pltpu.VMEM((channels, columns), BF16),
            pltpu.VMEM((2 * rows, channels), BF16),
        ),
        in_specs=[SCALARS] + [APART] * 2 + [WHOLE] + [APART] + specs,
        out_specs=[WHOLE] * 4,
        scratch_shapes=[pltpu.VMEM((rows, columns), F32), pltpu.SemaphoreType.DMA((3 + len(pieces),))],
        compiler_params=pltpu.CompilerParams(vmem_limit_bytes=VMEM_LIMIT),
        cost_estimate=COST,
    )(place, *in_hbm(own, core), bias, *in_hbm(local), *pieces)


def up_next(seq, normed, branch, bias, weight, act, shard):
    rows, channels = normed[0].shape
    columns = weight.shape[1]
    chunks = pltpu.VMEM((channels // shard // 2, shard, columns), BF16)
    return pl.pallas_call(
        up_next_kernel,
        name="hidden_next_and_down_grad",
        out_shape=(
            chunks,
            chunks,
            pltpu.VMEM((2 * rows, columns), F32),
            pltpu.VMEM((2 * rows, channels), BF16),
            pltpu.VMEM((4 * rows, channels), BF16),
        ),
        in_specs=[SCALARS] + [WHOLE] * 9,
        out_specs=[WHOLE] * 5,
        scratch_shapes=[pltpu.VMEM((rows, columns), F32), pltpu.VMEM((2 * rows, columns), BF16)],
        compiler_params=pltpu.CompilerParams(vmem_limit_bytes=VMEM_LIMIT),
        cost_estimate=COST,
    )(seq, *in_vmem(*normed, *branch), bias, *in_vmem(weight, act))


def down_kernel(apart, place_ref, branch_ref, slope_own, slope_next, local, *rest):
    hops = len(apart)
    pieces, (grad_ref, weight_ref, acted_ref, sems) = rest[:hops], rest[hops:]
    for copy in lay_weight(place_ref, local, pieces, apart, weight_ref, sems):
        copy.wait()
    rows = acted_ref.shape[0]
    for k in range(4):
        acted_ref[...] = jnp.dot(branch_ref[k * rows : (k + 1) * rows, :], weight_ref[...], preferred_element_type=F32)

        def block(i, carry):
            here = pl.ds(pl.multiple_of(i * ROWS, ROWS), ROWS)
            there = pl.ds(pl.multiple_of(k * rows + i * ROWS, ROWS), ROWS)
            slope = pl.ds(pl.multiple_of(k % 2 * rows + i * ROWS, ROWS), ROWS)
            grad_ref[there, :] = (acted_ref[here, :] * (slope_next if k > 1 else slope_own)[slope, :]).astype(BF16)
            return carry

        lax.fori_loop(0, rows // ROWS, block, 0)


def down(place, branch, slopes, local, pieces):
    rows, columns = branch.shape[0], slopes[0].shape[1]
    apart, pieces, specs = sorted_pieces(pieces)
    return pl.pallas_call(
        functools.partial(down_kernel, apart),
        name="hidden_grad",
        out_shape=pltpu.VMEM((rows, columns), BF16),
        in_specs=[SCALARS] + [WHOLE] * 3 + [APART] + specs,
        out_specs=WHOLE,
        scratch_shapes=[
            pltpu.VMEM((branch.shape[1], columns), BF16),
            pltpu.VMEM((rows // 4, columns), F32),
            pltpu.SemaphoreType.DMA((1 + len(pieces),)),
        ],
        compiler_params=pltpu.CompilerParams(vmem_limit_bytes=VMEM_LIMIT),
        cost_estimate=COST,
    )(place, *in_vmem(branch, *slopes), *in_hbm(local), *pieces)


def rise_kernel(seq_ref, own_ref, next_ref, grad_ref, keep_ref, send_ref):
    normed = jnp.concatenate([own_ref[...], next_ref[...]], axis=0)
    store_chunks(seq_ref[0], across_rows(normed, grad_ref[...]), keep_ref, send_ref)


def rise(seq, normed, grad, shard):
    chunks = pltpu.VMEM((normed[0].shape[1] // shard // 2, shard, grad.shape[1]), BF16)
    return pl.pallas_call(
        rise_kernel,
        name="up_grad",
        out_shape=(chunks, chunks),
        in_specs=[SCALARS] + [WHOLE] * 3,
        out_specs=[WHOLE] * 2,
        compiler_params=pltpu.CompilerParams(vmem_limit_bytes=VMEM_LIMIT),
        cost_estimate=COST,
    )(seq, *in_vmem(*normed, grad))


def back_kernel(grad_ref, weight_ref, keep_ref, send_ref):
    rows = keep_ref.shape[1]
    for k, (target, slot) in enumerate(((keep_ref, 0), (send_ref, 0), (keep_ref, 1), (send_ref, 1))):
        target[slot] = lax.dot_general(
            grad_ref[k * rows : (k + 1) * rows, :], weight_ref[...], (((1,), (1,)), ((), ())), preferred_element_type=F32
        ).astype(BF16)


def back(grad, weight):
    rows, columns = grad.shape
    half = pltpu.VMEM((2, rows // 4, weight.shape[0]), BF16)
    return pl.pallas_call(
        back_kernel,
        name="normed_grad",
        out_shape=(half, half),
        in_specs=[WHOLE, WHOLE],
        out_specs=[WHOLE] * 2,
        compiler_params=pltpu.CompilerParams(vmem_limit_bytes=VMEM_LIMIT),
        cost_estimate=COST,
    )(*in_vmem(grad, weight))


def tail_kernel(
    base_ref, live_ref, normal_in, inv_in, token_in, taps_in, near_ref, far_ref, pooled_ref, gain_ref, out_ref,
    normal_ref, inv_ref, token_ref, taps_ref, conv_ref, sems, taps_sem,
):
    mine, height, width, channels = out_ref.shape
    spots = height * width
    reach = taps_ref.shape[0]
    slabs = channels // LANES

    def loads(tile):
        here = pl.ds(pl.multiple_of(tile * spots, spots), spots)
        pairs = [(source.at[here], target.at[here]) for source, target in ((normal_in, normal_ref), (inv_in, inv_ref))]
        pairs.append((token_in.at[base_ref[0] + tile], token_ref.at[tile]))
        return [pltpu.make_async_copy(source, target, sems.at[k, tile]) for k, (source, target) in enumerate(pairs)]

    load_taps = pltpu.make_async_copy(taps_in, taps_ref, taps_sem)
    load_taps.start()
    for tile in range(mine):
        for copy in loads(tile):
            copy.start()
    load_taps.wait()

    def one_tile(tile, carry):
        for copy in loads(tile):
            copy.wait()
        for part in range(spots // ROWS):
            here = pl.ds(pl.multiple_of(tile * spots + part * ROWS, ROWS), ROWS)
            scaled = (near_ref[here, :] + far_ref[here, :].astype(F32)) * gain_ref[...][None, :]
            normal = normal_ref[here, :]
            center = jnp.mean(scaled, axis=-1, keepdims=True)
            along = jnp.mean(scaled * normal, axis=-1, keepdims=True)
            conv_ref[part * ROWS : (part + 1) * ROWS, :] = (scaled - center - normal * along) * inv_ref[here, :1]
        live = (base_ref[0] + tile < live_ref[0]).astype(F32)

        def slab(block, carry):
            lanes = pl.ds(pl.multiple_of(block * LANES, LANES), LANES)
            rows = [conv_ref[u * width : (u + 1) * width, lanes] for u in range(height)]
            total = depthwise_lanes(rows, taps_ref, lanes, reach, True)
            pooled = pooled_ref[tile, :, lanes]
            for u in range(height):
                out_grad = live * token_ref[tile, u, :, lanes].astype(F32) + pooled
                out_ref[tile, u, :, lanes] = (out_grad + total[u]).astype(BF16)
            return carry

        lax.fori_loop(0, slabs, slab, 0)
        return carry

    lax.fori_loop(0, mine, one_tile, 0)


def tail(base, live, near, far, normal, inv, token, pooled, taps, gain):
    _, height, width, channels = token.shape
    rows = normal.shape[0]
    mine = rows // (height * width)
    return pl.pallas_call(
        tail_kernel,
        name="norm_conv_back",
        out_shape=jax.ShapeDtypeStruct((mine, height, width, channels), BF16),
        in_specs=[SCALARS] * 2 + [APART] * 4 + [WHOLE] * 4,
        out_specs=WHOLE,
        scratch_shapes=[
            pltpu.VMEM(normal.shape, F32),
            pltpu.VMEM(inv.shape, F32),
            pltpu.VMEM((mine, height, width, channels), BF16),
            pltpu.VMEM(taps.shape, F32),
            pltpu.VMEM((height * width, channels), F32),
            pltpu.SemaphoreType.DMA((3, mine)),
            pltpu.SemaphoreType.DMA,
        ],
        compiler_params=pltpu.CompilerParams(vmem_limit_bytes=VMEM_LIMIT),
        cost_estimate=COST,
    )(base, live, *in_hbm(normal, inv, token, taps), *in_vmem(near, far), pooled, gain)


def after(value, *others):
    return lax.optimization_barrier((value,) + others)[0]


def on_device(
    sizes,
    tiles,
    token_grad,
    embed_grad,
    live_tiles,
    dw_kernel,
    dw_bias,
    ln_gain,
    ln_bias,
    w_up,
    b_up,
    w_down,
    layer_scale,
):
    n_seq, n_dp = sizes
    count, height, width, channels = tiles.shape
    mine = count // 2
    spots = height * width
    shard, columns = w_up.shape
    part = columns // 2
    seq, dp, core = (lax.axis_index(name) for name in ("seq", "dp", "mp"))
    pair = [(i, i ^ 1) for i in range(n_dp)]
    swap = [(0, 1), (1, 0)]
    side = (dp % 2) * part

    def over_pair(value):
        return lax.ppermute(value, "dp", pair)

    def over_cores(value):
        return lax.ppermute(value, "mp", swap)

    def meet(value, step):
        return lax.ppermute(value, "seq", [(i, i ^ step) for i in range(n_seq)])

    def both_sides(piece, *others):
        if n_dp == 2:
            theirs = after(over_pair(piece), *others)
            low = jnp.where(dp == 0, piece, theirs)
            high = jnp.where(dp == 0, theirs, piece)
            return jnp.concatenate([low, high], axis=1).astype(F32)
        spread = lax.dynamic_update_slice_in_dim(jnp.zeros((shard, columns), F32), piece.astype(F32), side, 1)
        return lax.psum(spread.astype(BF16), "dp").astype(F32)

    offsets = (seq ^ jnp.arange(n_seq, dtype=jnp.int32)) * shard
    my_place = seq.astype(jnp.int32)[None]
    place = jnp.concatenate([jnp.stack([side, seq]), offsets]).astype(jnp.int32)
    base = (core * mine).astype(jnp.int32)[None]

    def own_tiles(values, which):
        return lax.dynamic_slice_in_dim(values, which * mine, mine, 0)

    live = (jnp.arange(count) < live_tiles[0]).astype(BF16)
    steps = [1 << level for level in range(n_seq.bit_length() - 1)]

    def spread(own, first):
        pieces = {0: own, **first}
        for r in range(1, n_seq):
            if r not in pieces:
                pieces[r] = meet(pieces[r ^ (r & -r)], r & -r)
        return [pieces[r] for r in range(1, n_seq)]

    embed = embed_grad[0]
    slots, width_ = embed.shape
    beside = part // width_
    deep = -(-slots // (16 * beside)) * 16
    embed = jnp.pad(embed, ((0, deep * beside - slots), (0, 0)))
    embed = jnp.concatenate([embed[k * deep : (k + 1) * deep] for k in range(beside)], axis=1)
    embed = jnp.pad(embed, ((0, 0), (0, part - beside * width_)))
    up_own = jnp.concatenate([lax.dynamic_slice_in_dim(w_up, side, part, 1), embed], axis=0)
    first = {r: meet(up_own, r) for r in steps}
    own_token = own_tiles(after(token_grad, up_own), core) * own_tiles(live, core)[:, None, None, None]
    next_token = over_pair(own_token)
    base = after(base, own_token)
    own_half, normal, inv = front(base, tiles, dw_kernel, dw_bias, ln_gain, ln_bias, mine)
    first, own_half = lax.optimization_barrier((first, own_half))
    up_pieces = spread(up_own, first)
    next_half = over_pair(own_half)
    core_half = over_cores(own_half)
    down_own = lax.dynamic_slice_in_dim(after(w_down, own_half), side, part, 1)
    first = {steps[-1]: meet(down_own, steps[-1])}
    up_pieces, core_half, next_token = lax.optimization_barrier((up_pieces, core_half, next_token))
    first = {**{r: meet(after(down_own, up_pieces), r) for r in steps[:-1]}, **first}
    parts = []
    for piece in [up_own] + up_pieces:
        packed = piece[shard:]
        packed = jnp.concatenate([packed[:, k * width_ : (k + 1) * width_] for k in range(beside)], axis=0)
        parts.append(lax.dynamic_slice_in_dim(packed, seq * count, count, 0))
    pooled = []
    for place_at in range(n_seq):
        block = parts[0]
        for r in range(1, n_seq):
            block = jnp.where(seq ^ place_at == r, parts[r], block)
        pooled.append(block)
    pooled = jnp.concatenate(pooled, axis=1) * live[:, None]
    next_pooled = over_pair(pooled)
    core_token = own_tiles(token_grad, 1 - core) * own_tiles(live, 1 - core)[:, None, None, None]

    def branch_grad(tokens, pools, which):
        own_pools = own_tiles(pools, which).astype(F32) / spots
        return (layer_scale * (tokens.astype(F32) + own_pools[:, None, None, :])).astype(BF16).reshape(mine * spots, channels)

    branch = (
        branch_grad(own_token, pooled, core),
        branch_grad(core_token, pooled, 1 - core),
        branch_grad(next_token, next_pooled, core),
        branch_grad(over_cores(next_token), next_pooled, 1 - core),
    )
    bias = lax.dynamic_slice_in_dim(b_up, side, part, 0)[None, :]
    act, slope, whole_up, normed = up(place, own_half, core_half, bias, w_up, up_pieces)
    down_pieces = spread(down_own, after(first, act, pooled))
    next_half = after(next_half, act)
    fall, fall_away, next_slope, next_normed, branch = up_next(
        my_place, (next_half, over_cores(next_half)), branch, bias, whole_up, act, shard
    )
    fall_from = meet(fall_away, 1)
    hidden_grad = down(place, branch, (slope, next_slope), w_down, down_pieces)

    def joined(keep, arrived):
        values = [keep[k].astype(F32) + arrived[k].astype(F32) for k in range(n_seq // 2)]
        return values[::2], [value.astype(BF16) for value in values[1::2]]

    def settle(values, away, *others):
        step = 2
        while away:
            arrived = after([meet(value, step) for value in away], *others)
            values = [value + more.astype(F32) for value, more in zip(values, arrived)]
            values, away = values[::2], [value.astype(BF16) for value in values[1::2]]
            step *= 2
        return values[0].astype(BF16)

    fall, fall_away = joined(fall, fall_from)
    climb, climb_away = rise(my_place, (normed, next_normed), hidden_grad, shard)
    climb_from = meet(climb_away, 1)
    keep, send = back(after(hidden_grad, climb, fall_away), whole_up)
    from_core = over_cores(send)
    far_grad = (keep[1].astype(F32) + from_core[1].astype(F32)).astype(BF16)
    from_pair = over_pair(far_grad)
    fall = settle(fall, fall_away, climb, from_pair)
    near_grad = after(keep[0].astype(F32) + from_core[0].astype(F32), fall)
    own_pooled = lax.dynamic_slice_in_dim(pooled, core * mine, mine, 0).astype(F32)[:, None, :] / spots
    grad_half = tail(base, live_tiles, near_grad, from_pair, normal, inv, token_grad, own_pooled, dw_kernel, ln_gain)
    climb, climb_away = joined(climb, after(climb_from, grad_half))
    climb = settle(climb, climb_away)
    other_half = over_cores(grad_half)
    first = jnp.where(core == 0, grad_half, other_half)
    second = jnp.where(core == 0, other_half, grad_half)
    tile_grad = jnp.concatenate([first, second], axis=0)
    grad_down = both_sides(fall)
    return (tile_grad, both_sides(climb, tile_grad, grad_down), grad_down)


def solution(mesh):
    sizes = (mesh.shape["seq"], mesh.shape["dp"])
    return jax.shard_map(
        functools.partial(on_device, sizes),
        mesh=mesh,
        in_specs=(
            P(("groups", "seq", "dp"), None, None, None),
            P(("groups", "seq", "dp"), None, None, None),
            P("dp", "groups", "seq"),
            P(("groups", "seq", "dp")),
            P(),
            P(),
            P(),
            P(),
            P("seq", "mp"),
            P("mp"),
            P("seq", "mp"),
            P(),
        ),
        out_specs=(
            P(("groups", "seq", "dp"), None, None, None),
            P(("groups", "seq"), "mp"),
            P(("groups", "seq"), "mp"),
        ),
        check_vma=False,
    )
```

time: 117 us -> 108 us (0.923)
  waiting for transfers between devices: 53 us -> 43.3 us
  starting transfers between devices: 19.3 us -> 25.4 us
  other arithmetic: 9.12 us -> 5.86 us
  Pallas kernels: 25.9 us -> 28.9 us
  blocking collectives: 2.5 us -> 0 us
  local copies, waits for them, and re-layouts: 4.86 us -> 2.89 us
    ppermute x12 -> x10, starting transfers between devices: 9.15 us -> 16.9 us  [meet(): return lax.ppermute(value, 'seq', [(i, i ^ step) for i in range(n_seq)])]
    ppermute x6, waiting for transfers between devices: 9.3 us -> 3.91 us  [over_pair(): return lax.ppermute(value, 'dp', pair)]
    all_to_all x1 -> x0, waiting for transfers between devices: 5.23 us -> none  [on_device(): lax.all_to_all(after(embed_grad[0], near[min(1, n_seq - 2)]), 'seq', spli...]
    all_to_all x1 -> x0, starting transfers between devices: 5.07 us -> none  [on_device(): lax.all_to_all(after(embed_grad[0], near[min(1, n_seq - 2)]), 'seq', spli...]
    convert_element_type x7 -> x5, other arithmetic: 4.01 us -> 0.54 us  [the longest x1 0.21 us: on_device(): far_grad = (keep[1].astype(F32) + from_core[1].astype(F32)).astype(BF16)]
    ppermute x6, starting transfers between devices: 4.83 us -> 7.91 us  [over_pair(): return lax.ppermute(value, 'dp', pair)]
    unnamed x29 -> x28, local copies, waits for them, and re-layouts: 2.72 us -> 0.07 us
    all_gather x1 -> x0, blocking collectives: 2.5 us -> none  [on_device(): tile_grad = lax.all_gather(grad_half, 'mp', axis=0, tiled=True)]
  transfers between devices with their start and end apart: 23 -> 21, of which waited for: 14 -> 9; matrix products, arithmetic and copies ran while one was open for 7% -> 4% of each run, Pallas kernels for 12% -> 25%
where the time goes in v3:
time: 108 us
  waiting for transfers between devices  43.3 us (40%)
  Pallas kernels  28.9 us (27%)
  starting transfers between devices  25.4 us (24%)
  other arithmetic  5.86 us (5%)
  local copies, waits for them, and re-layouts  2.89 us (3%)
  between operations  1.65 us (2%)
    ppermute x10, waiting for transfers between devices, meet(): return lax.ppermute(value, 'seq', [(i, i ^ step) for i in range(n_seq)])  36.9 us
    ppermute x10, starting transfers between devices, meet(): return lax.ppermute(value, 'seq', [(i, i ^ step) for i in range(n_seq)])  16.9 us
    ppermute x6, starting transfers between devices, over_pair(): return lax.ppermute(value, 'dp', pair)  7.91 us
    pallas_call x1, Pallas kernels, tail(): pl.pallas_call(tail_kernel, name='norm_conv_back', out_shape=jax.ShapeDty...  5.94 us
    pallas_call x1, Pallas kernels, front(): pl.pallas_call(front_kernel, name='conv_norm', out_shape=(pltpu.HBM((rows...  5.46 us
    pallas_call x1, Pallas kernels, down(): pl.pallas_call(functools.partial(down_kernel, apart), name='hidden_grad',...  4.93 us
    pallas_call x1, Pallas kernels, up(): pl.pallas_call(functools.partial(up_kernel, apart), name='hidden_own', ou...  4.42 us
    pallas_call x1, Pallas kernels, up_next(): pl.pallas_call(up_next_kernel, name='hidden_next_and_down_grad', out_shap...  4.36 us
  transfers between devices with their start and end apart: 21, of which 9 were waited for; matrix products, arithmetic and copies ran while one was open for 4% of the time, Pallas kernels for 25%

profile of v3, /device:TPU:0, one launch (start us, length us, event | category | flops | bytes accessed | tf_op | source)
XLA Modules:
  0.0 108.0 jit_solution(3377641834020544893)
XLA Ops:
  0.7 0.8 slice_bitcast_fusion.1
  1.5 0.7 pad_slice_fusion
  2.2 1.0 constant_dynamic-slice_fusion.1
  3.2 0.1 fusion.9
  3.3 4.1 %collective-permute-start.1 = (bf16[208,640]{1,0:T(8,128)(2,1)S(1)}, bf16[208,640]{1,0:T(8,128)(2,1)S(1)}, u32[]{:S(2)}, u32[]{:S(2)}) collective-permute-start(bf16[208,640]{1,0:T(8,128)(2,1)S(1)} %pad_maximum_fusion.1), channel_id=1, source_target_pairs={{0,8},{4,12},{8,0},{12,4},{1,9},{5,13},{9,1},{13,5},{2,10},{6,14},... | collective-permute-start | bytes 798728 | tf_op jit(solution)/shard_map/ppermute | solution.py:453
  7.4 1.6 %collective-permute-start = (bf16[208,640]{1,0:T(8,128)(2,1)S(1)}, bf16[208,640]{1,0:T(8,128)(2,1)S(1)}, u32[]{:S(2)}, u32[]{:S(2)}) collective-permute-start(bf16[208,640]{1,0:T(8,128)(2,1)S(1)} %pad_maximum_fusion.1), channel_id=1, source_target_pairs={{0,4},{4,0},{8,12},{12,8},{1,5},{5,1},{9,13},{13,9},{2,6},{6,2},{1... | collective-permute-start | bytes 798728 | tf_op jit(solution)/shard_map/ppermute | solution.py:453
  9.6 0.1 fusion.25
  9.7 1.1 %dynamic-slice_multiply_fusion = bf16[5,8,8,768]{3,2,1,0:T(8,128)(2,1)S(1)} fusion(bf16[10,8,8,768]{3,2,1,0:T(8,128)(2,1)} %token_in.1, s32[]{:T(128)S(6)} %select_n.140, bf16[5]{0:T(256)(128)(2,1)S(1)} %get-tuple-element.111), kind=kLoop, calls=%fused_computation.16 | loop fusion | flops 245760 | bytes 983054 | tf_op jit(solution)/shard_map/mul | solution.py:491
  10.8 1.6 %collective-permute-start.5 = (bf16[5,8,8,768]{3,2,1,0:T(8,128)(2,1)S(1)}, bf16[5,8,8,768]{3,2,1,0:T(8,128)(2,1)S(1)}, u32[]{:S(2)}, u32[]{:S(2)}) collective-permute-start(bf16[5,8,8,768]{3,2,1,0:T(8,128)(2,1)S(1)} %dynamic-slice_multiply_fusion), channel_id=1, source_target_pairs={{0,2},{2,0},{1,3},{3,1},{4,6},{6,4},{5,7},{7,5},{8,10},{10,8},{9,1... | collective-permute-start | bytes 1474568 | tf_op jit(solution)/shard_map/ppermute | solution.py:447
  12.4 5.5 %conv_norm.1 = (bf16[320,768]{1,0:T(8,128)(2,1)}, f32[320,768]{1,0:T(8,128)}, f32[320,128]{1,0:T(8,128)}) custom-call(s32[1]{0:T(128)} %bitcast.base_ref, bf16[10,8,8,768]{3,2,1,0:T(8,128)(2,1)S(1)} %copy-done, f32[7,7,768]{2,1,0:T(8,128)S(1)} %copy-done.1, f32[768]{0:T(1024)S(1)} %copy-done.2, f32[768]{0:T(1024)S(1)} %copy-done.4, f32[768]{0:T(1024)S(1)} %copy-done.3), custom_call_target="tpu_custom_call" | custom-call | flops 10737418240 | bytes 4194304 | tf_op jit(solution)/shard_map/conv_norm/pallas_call | solution.py:110
  17.9 1.7 %collective-permute-done.1.rest_1_ = bf16[208,640]{1,0:T(8,128)(2,1)S(1)} collective-permute-done((bf16[208,640]{1,0:T(8,128)(2,1)S(1)}, bf16[208,640]{1,0:T(8,128)(2,1)S(1)}, u32[]{:S(2)}, u32[]{:S(2)}) %collective-permute-start.1) | collective-permute-done | bytes 266272 | tf_op jit(solution)/shard_map/ppermute | solution.py:453
  19.6 0.2 collective-permute-done.rest_0_
  19.8 1.5 %collective-permute-start.3 = (bf16[208,640]{1,0:T(8,128)(2,1)S(1)}, bf16[208,640]{1,0:T(8,128)(2,1)S(1)}, u32[]{:S(2)}, u32[]{:S(2)}) collective-permute-start(bf16[208,640]{1,0:T(8,128)(2,1)S(1)} %collective-permute-done.1.rest_1_), channel_id=1, source_target_pairs={{0,4},{4,0},{8,12},{12,8},{1,5},{5,1},{9,13},{13,9},{2,6},{6,2},{1... | collective-permute-start | bytes 798728 | tf_op jit(solution)/shard_map/ppermute | solution.py:453
  21.3 0.1 dynamic_slice.49
  21.4 1.5 %collective-permute-start.2 = (bf16[320,768]{1,0:T(8,128)(2,1)}, bf16[320,768]{1,0:T(8,128)(2,1)S(1)}, u32[]{:S(2)}, u32[]{:S(2)}) collective-permute-start(bf16[320,768]{1,0:T(8,128)(2,1)} %get-tuple-element.44.own_ref), channel_id=1, source_target_pairs={{0,2},{2,0},{1,3},{3,1},{4,6},{6,4},{5,7},{7,5},{8,10},{10,8},{9,1... | collective-permute-start | bytes 1474568 | tf_op jit(solution)/shard_map/ppermute | solution.py:447
  23.0 2.5 %collective-permute-start.10 = (bf16[192,640]{1,0:T(8,128)(2,1)S(1)}, bf16[192,640]{1,0:T(8,128)(2,1)S(1)}, u32[]{:S(2)}, u32[]{:S(2)}) collective-permute-start(bf16[192,640]{1,0:T(8,128)(2,1)S(1)} %constant_dynamic-slice_fusion), channel_id=1, source_target_pairs={{0,8},{4,12},{8,0},{12,4},{1,9},{5,13},{9,1},{13,5},{2,10},{6,14},... | collective-permute-start | bytes 737288 | tf_op jit(solution)/shard_map/ppermute | solution.py:453
  25.5 6.8 %collective-permute-done.3.rest_2_ = bf16[208,640]{1,0:T(8,128)(2,1)S(1)} collective-permute-done((bf16[208,640]{1,0:T(8,128)(2,1)S(1)}, bf16[208,640]{1,0:T(8,128)(2,1)S(1)}, u32[]{:S(2)}, u32[]{:S(2)}) %collective-permute-start.3) | collective-permute-done | bytes 266272 | tf_op jit(solution)/shard_map/ppermute | solution.py:453
  32.4 0.1 fusion.22
  32.6 0.1 maximum_multiply_fusion
  32.7 2.6 %collective-permute-start.7 = (bf16[10,768]{1,0:T(8,128)(2,1)S(1)}, bf16[10,768]{1,0:T(8,128)(2,1)S(1)}, u32[]{:S(2)}, u32[]{:S(2)}) collective-permute-start(bf16[10,768]{1,0:T(8,128)(2,1)S(1)} %maximum_multiply_fusion), channel_id=1, source_target_pairs={{0,2},{2,0},{1,3},{3,1},{4,6},{6,4},{5,7},{7,5},{8,10},{10,8},{9,1... | collective-permute-start | bytes 46088 | tf_op jit(solution)/shard_map/ppermute | solution.py:447
  35.3 4.4 %hidden_own.1 = (bf16[640,640]{1,0:T(8,128)(2,1)S(1)}, f32[640,640]{1,0:T(8,128)S(1)}, bf16[768,640]{1,0:T(8,128)(2,1)S(1)}, bf16[640,768]{1,0:T(8,128)(2,1)S(1)}) custom-call(s32[6]{0:T(128)S(1)} %pad_add_fusion.place_ref, bf16[320,768]{1,0:T(8,128)(2,1)} %get-tuple-element.44.own_ref, bf16[320,768]{1,0:T(8,128)(2,1)} %copy-done.11, ...), custom_call_target="tpu_custom_call" | custom-call | flops 10737418240 | bytes 4194304 | tf_op jit(solution)/shard_map/hidden_own/pallas_call | solution.py:225
  39.7 0.6 collective-permute-start.6
  40.4 2.2 %collective-permute-done.9.rest_0_ = bf16[192,640]{1,0:T(8,128)(2,1)S(1)} collective-permute-done((bf16[192,640]{1,0:T(8,128)(2,1)S(1)}, bf16[192,640]{1,0:T(8,128)(2,1)S(1)}, u32[]{:S(2)}, u32[]{:S(2)}) %collective-permute-start.9) | collective-permute-done | bytes 245792 | tf_op jit(solution)/shard_map/ppermute | solution.py:453
  42.6 0.3 collective-permute-start.11
  42.9 0.6 multiply_convert_fusion
  43.5 4.4 %hidden_next_and_down_grad.1 = (bf16[2,192,640]{2,1,0:T(8,128)(2,1)S(1)}, bf16[2,192,640]{2,1,0:T(8,128)(2,1)S(1)}, f32[640,640]{1,0:T(8,128)S(1)}, bf16[640,768]{1,0:T(8,128)(2,1)S(1)}, bf16[1280,768]{1,0:T(8,128)(2,1)S(1)}) custom-call(s32[1]{0:T(128)} %bitcast.6.seq_ref, bf16[320,768]{1,0:T(8,128)(2,1)S(1)} %collective-permute-done.2.rest_0_, ...), custom_call_target="tpu_custom_call" | custom-call | flops 10737418240 | bytes 4194304 | tf_op jit(solution)/shard_map/hidden_next_and_down_grad/pallas_call | solution.py:246
  47.8 1.8 %collective-permute-start.12 = (bf16[2,192,640]{2,1,0:T(8,128)(2,1)S(1)}, bf16[2,192,640]{2,1,0:T(8,128)(2,1)S(1)}, u32[]{:S(2)}, u32[]{:S(2)}) collective-permute-start(bf16[2,192,640]{2,1,0:T(8,128)(2,1)S(1)} %get-tuple-element.66), channel_id=1, source_target_pairs={{0,4},{4,0},{8,12},{12,8},{1,5},{5,1},{9,13},{13,9},{2,6},{6,2},{1... | collective-permute-start | bytes 1474568 | tf_op jit(solution)/shard_map/ppermute | solution.py:453
  49.6 4.9 %hidden_grad.1.grad_ref = bf16[1280,640]{1,0:T(8,128)(2,1)S(1)} custom-call(s32[6]{0:T(128)S(1)} %pad_add_fusion.place_ref, bf16[1280,768]{1,0:T(8,128)(2,1)S(1)} %get-tuple-element.55.branch_ref, f32[640,640]{1,0:T(8,128)S(1)} %get-tuple-element.56.slope_own, f32[640,640]{1,0:T(8,128)S(1)} %get-tuple-element.57.slope_next, bf16[192,1280]{1,0:T(8,128)(2,1)} %local.3, ...), custom_call_target="tpu_custom_call" | custom-call | flops 10737418240 | bytes 4194304 | tf_op jit(solution)/shard_map/hidden_grad/pallas_call | solution.py:286
  54.6 2.0 %up_grad.1 = (bf16[2,192,640]{2,1,0:T(8,128)(2,1)S(1)}, bf16[2,192,640]{2,1,0:T(8,128)(2,1)S(1)}) custom-call(s32[1]{0:T(128)} %bitcast.6.seq_ref, bf16[640,768]{1,0:T(8,128)(2,1)S(1)} %get-tuple-element.62.own_ref, bf16[640,768]{1,0:T(8,128)(2,1)S(1)} %get-tuple-element.63.next_ref, bf16[1280,640]{1,0:T(8,128)(2,1)S(1)} %hidden_grad.1.grad_ref), custom_call_target="tpu_custom_call" | custom-call | flops 10737418240 | bytes 4194304 | tf_op jit(solution)/shard_map/up_grad/pallas_call | solution.py:309
  56.6 3.8 %collective-permute-done.12 = bf16[2,192,640]{2,1,0:T(8,128)(2,1)S(1)} collective-permute-done((bf16[2,192,640]{2,1,0:T(8,128)(2,1)S(1)}, bf16[2,192,640]{2,1,0:T(8,128)(2,1)S(1)}, u32[]{:S(2)}, u32[]{:S(2)}) %collective-permute-start.12) | collective-permute-done | bytes 491552 | tf_op jit(solution)/shard_map/ppermute | solution.py:453
  60.5 1.7 %normed_grad.1 = (bf16[2,320,768]{2,1,0:T(8,128)(2,1)S(1)}, bf16[2,320,768]{2,1,0:T(8,128)(2,1)S(1)}) custom-call(bf16[1280,640]{1,0:T(8,128)(2,1)S(1)} %hidden_grad.1.grad_ref, bf16[768,640]{1,0:T(8,128)(2,1)S(1)} %get-tuple-element.54.rest_7_.weight_ref), custom_call_target="tpu_custom_call" | custom-call | flops 10737418240 | bytes 4194304 | tf_op jit(solution)/shard_map/normed_grad/pallas_call | solution.py:331
  62.3 2.6 %collective-permute-done.13 = bf16[2,320,768]{2,1,0:T(8,128)(2,1)S(1)} collective-permute-done((bf16[2,320,768]{2,1,0:T(8,128)(2,1)S(1)}, bf16[2,320,768]{2,1,0:T(8,128)(2,1)S(1)}, u32[]{:S(2)}, u32[]{:S(2)}) %collective-permute-start.13) | collective-permute-done | bytes 983072 | tf_op jit(solution)/shard_map/ppermute | solution.py:450
  64.8 0.2 fusion
  65.0 0.1 collective-permute-start.15
  65.2 2.7 %collective-permute-start.14 = (bf16[192,640]{1,0:T(8,128)(2,1)S(1)}, bf16[192,640]{1,0:T(8,128)(2,1)S(1)}, u32[]{:S(2)}, u32[]{:S(2)}) collective-permute-start(bf16[192,640]{1,0:T(8,128)(2,1)S(1)} %fusion.3), channel_id=1, source_target_pairs={{0,8},{4,12},{8,0},{12,4},{1,9},{5,13},{9,1},{13,5},{2,10},{6,14},... | collective-permute-start | bytes 737288 | tf_op jit(solution)/shard_map/ppermute | solution.py:453
  67.9 0.8 collective-permute-start.17
  68.7 10.8 %collective-permute-done.14 = bf16[192,640]{1,0:T(8,128)(2,1)S(1)} collective-permute-done((bf16[192,640]{1,0:T(8,128)(2,1)S(1)}, bf16[192,640]{1,0:T(8,128)(2,1)S(1)}, u32[]{:S(2)}, u32[]{:S(2)}) %collective-permute-start.14) | collective-permute-done | bytes 245792 | tf_op jit(solution)/shard_map/ppermute | solution.py:453
  79.6 0.1 fusion.2
  79.7 5.9 %norm_conv_back.1 = bf16[5,8,8,768]{3,2,1,0:T(8,128)(2,1)S(1)} custom-call(s32[1]{0:T(128)} %bitcast.base_ref, s32[1]{0:T(128)} %copy.15.live_ref, f32[320,768]{1,0:T(8,128)} %get-tuple-element.41.normal_in, f32[320,128]{1,0:T(8,128)} %get-tuple-element.42.inv_in, bf16[10,8,8,768]{3,2,1,0:T(8,128)(2,1)} %token_in.1, f32[7,7,768]{2,1,0:T(8,128)} %taps_in.1, ...), custom_call_target="tpu_custom_call" | custom-call | flops 10737418240 | bytes 4194304 | tf_op jit(solution)/shard_map/norm_conv_back/pallas_call | solution.py:396
  85.7 1.6 %collective-permute-start.18 = (bf16[192,640]{1,0:T(8,128)(2,1)S(1)}, bf16[192,640]{1,0:T(8,128)(2,1)S(1)}, u32[]{:S(2)}, u32[]{:S(2)}) collective-permute-start(bf16[192,640]{1,0:T(8,128)(2,1)S(1)} %fusion.4), channel_id=1, source_target_pairs={{0,8},{4,12},{8,0},{12,4},{1,9},{5,13},{9,1},{13,5},{2,10},{6,14},... | collective-permute-start | bytes 737288 | tf_op jit(solution)/shard_map/ppermute | solution.py:453
  87.3 0.5 collective-permute-start.20
  87.8 11.3 %collective-permute-done.18 = bf16[192,640]{1,0:T(8,128)(2,1)S(1)} collective-permute-done((bf16[192,640]{1,0:T(8,128)(2,1)S(1)}, bf16[192,640]{1,0:T(8,128)(2,1)S(1)}, u32[]{:S(2)}, u32[]{:S(2)}) %collective-permute-start.18) | collective-permute-done | bytes 245792 | tf_op jit(solution)/shard_map/ppermute | solution.py:453
  99.1 0.1 fusion.1
  99.2 1.7 %collective-permute-start.19 = (bf16[192,640]{1,0:T(8,128)(2,1)S(1)}, bf16[192,640]{1,0:T(8,128)(2,1)S(1)}, u32[]{:S(2)}, u32[]{:S(2)}) collective-permute-start(bf16[192,640]{1,0:T(8,128)(2,1)S(1)} %fusion.1), channel_id=1, source_target_pairs={{0,2},{2,0},{1,3},{3,1},{4,6},{6,4},{5,7},{7,5},{8,10},{10,8},{9,1... | collective-permute-start | bytes 737288 | tf_op jit(solution)/shard_map/ppermute | solution.py:447
  101.0 1.0 maximum_convert_fusion
  102.0 1.0 pad_maximum_fusion
  103.1 3.9 %collective-permute-done.19 = bf16[192,640]{1,0:T(8,128)(2,1)S(1)} collective-permute-done((bf16[192,640]{1,0:T(8,128)(2,1)S(1)}, bf16[192,640]{1,0:T(8,128)(2,1)S(1)}, u32[]{:S(2)}, u32[]{:S(2)}) %collective-permute-start.19) | collective-permute-done | bytes 245792 | tf_op jit(solution)/shard_map/ppermute | solution.py:447
  107.0 1.0 maximum_convert_fusion.1
  (62 shorter events, 0.8 us)
Async XLA Ops:
  0.6 11.8 %copy-start.4 = (f32[768]{0:T(1024)S(1)}, f32[768]{0:T(1024)}, u32[]{:S(2)}) copy-start(f32[768]{0:T(1024)} %gain_ref.3) | copy-start | bytes 9220
  0.6 11.8 %copy-start.1 = (f32[7,7,768]{2,1,0:T(8,128)S(1)}, f32[7,7,768]{2,1,0:T(8,128)}, u32[]{:S(2)}) copy-start(f32[7,7,768]{2,1,0:T(8,128)} %taps_in.1) | copy-start | bytes 451588
  0.7 11.8 %copy-start.3 = (f32[768]{0:T(1024)S(1)}, f32[768]{0:T(1024)}, u32[]{:S(2)}) copy-start(f32[768]{0:T(1024)} %shift_ref.1) | copy-start | bytes 9220
  0.7 11.7 %copy-start.2 = (f32[768]{0:T(1024)S(1)}, f32[768]{0:T(1024)}, u32[]{:S(2)}) copy-start(f32[768]{0:T(1024)} %bias_ref.1) | copy-start | bytes 9220
  0.7 11.7 %copy-start = (bf16[10,8,8,768]{3,2,1,0:T(8,128)(2,1)S(1)}, bf16[10,8,8,768]{3,2,1,0:T(8,128)(2,1)}, u32[]{:S(2)}) copy-start(bf16[10,8,8,768]{3,2,1,0:T(8,128)(2,1)} %tiles_ref.1) | copy-start | bytes 2949124
  3.3 16.3 %collective-permute-start.1 = (bf16[208,640]{1,0:T(8,128)(2,1)S(1)}, bf16[208,640]{1,0:T(8,128)(2,1)S(1)}, u32[]{:S(2)}, u32[]{:S(2)}) collective-permute-start(bf16[208,640]{1,0:T(8,128)(2,1)S(1)} %pad_maximum_fusion.1), channel_id=1, source_target_pairs={{0,8},{4,12},{8,0},{12,4},{1,9},{5,13},{9,1},{13,5},{2,10},{6,14},... | collective-permute-start | bytes 798728 | tf_op jit(solution)/shard_map/ppermute | solution.py:453
  7.4 12.4 %collective-permute-start = (bf16[208,640]{1,0:T(8,128)(2,1)S(1)}, bf16[208,640]{1,0:T(8,128)(2,1)S(1)}, u32[]{:S(2)}, u32[]{:S(2)}) collective-permute-start(bf16[208,640]{1,0:T(8,128)(2,1)S(1)} %pad_maximum_fusion.1), channel_id=1, source_target_pairs={{0,4},{4,0},{8,12},{12,8},{1,5},{5,1},{9,13},{13,9},{2,6},{6,2},{1... | collective-permute-start | bytes 798728 | tf_op jit(solution)/shard_map/ppermute | solution.py:453
  10.8 14.6 %collective-permute-start.5 = (bf16[5,8,8,768]{3,2,1,0:T(8,128)(2,1)S(1)}, bf16[5,8,8,768]{3,2,1,0:T(8,128)(2,1)S(1)}, u32[]{:S(2)}, u32[]{:S(2)}) collective-permute-start(bf16[5,8,8,768]{3,2,1,0:T(8,128)(2,1)S(1)} %dynamic-slice_multiply_fusion), channel_id=1, source_target_pairs={{0,2},{2,0},{1,3},{3,1},{4,6},{6,4},{5,7},{7,5},{8,10},{10,8},{9,1... | collective-permute-start | bytes 1474568 | tf_op jit(solution)/shard_map/ppermute | solution.py:447
  12.4 8.9 %copy-start.10 = (f32[1280]{0:T(1024)S(1)}, f32[1280]{0:T(1024)}, u32[]{:S(2)}) copy-start(f32[1280]{0:T(1024)} %param.21) | copy-start | bytes 15364
  12.4 10.5 %copy-start.6 = (bf16[192,1280]{1,0:T(8,128)(2,1)S(1)}, bf16[192,1280]{1,0:T(8,128)(2,1)}, u32[]{:S(2)}) copy-start(bf16[192,1280]{1,0:T(8,128)(2,1)} %local.3) | copy-start | bytes 1474564
  19.6 15.7 %copy-start.9 = (bf16[208,640]{1,0:T(8,128)(2,1)}, bf16[208,640]{1,0:T(8,128)(2,1)S(1)}, u32[]{:S(2)}) copy-start(bf16[208,640]{1,0:T(8,128)(2,1)S(1)} %collective-permute-done.1.rest_1_) | copy-start | bytes 798724
  19.8 15.5 %copy-start.8 = (bf16[208,640]{1,0:T(8,128)(2,1)}, bf16[208,640]{1,0:T(8,128)(2,1)S(1)}, u32[]{:S(2)}) copy-start(bf16[208,640]{1,0:T(8,128)(2,1)S(1)} %collective-permute-done.rest_0_) | copy-start | bytes 798724
  19.8 12.6 %collective-permute-start.4 = (bf16[320,768]{1,0:T(8,128)(2,1)}, bf16[320,768]{1,0:T(8,128)(2,1)S(1)}, u32[]{:S(2)}, u32[]{:S(2)}) collective-permute-start(bf16[320,768]{1,0:T(8,128)(2,1)} %get-tuple-element.44.own_ref), channel_id=1, source_target_pairs={{0,1},{1,0},{2,3},{3,2},{4,5},{5,4},{6,7},{7,6},{8,9},{9,8},{10,11... | collective-permute-start | bytes 1474568 | tf_op jit(solution)/shard_map/ppermute | solution.py:450
  19.8 12.5 %collective-permute-start.3 = (bf16[208,640]{1,0:T(8,128)(2,1)S(1)}, bf16[208,640]{1,0:T(8,128)(2,1)S(1)}, u32[]{:S(2)}, u32[]{:S(2)}) collective-permute-start(bf16[208,640]{1,0:T(8,128)(2,1)S(1)} %collective-permute-done.1.rest_1_), channel_id=1, source_target_pairs={{0,4},{4,0},{8,12},{12,8},{1,5},{5,1},{9,13},{13,9},{2,6},{6,2},{1... | collective-permute-start | bytes 798728 | tf_op jit(solution)/shard_map/ppermute | solution.py:453
  21.4 18.3 %collective-permute-start.2 = (bf16[320,768]{1,0:T(8,128)(2,1)}, bf16[320,768]{1,0:T(8,128)(2,1)S(1)}, u32[]{:S(2)}, u32[]{:S(2)}) collective-permute-start(bf16[320,768]{1,0:T(8,128)(2,1)} %get-tuple-element.44.own_ref), channel_id=1, source_target_pairs={{0,2},{2,0},{1,3},{3,1},{4,6},{6,4},{5,7},{7,5},{8,10},{10,8},{9,1... | collective-permute-start | bytes 1474568 | tf_op jit(solution)/shard_map/ppermute | solution.py:447
  23.0 17.4 %collective-permute-start.10 = (bf16[192,640]{1,0:T(8,128)(2,1)S(1)}, bf16[192,640]{1,0:T(8,128)(2,1)S(1)}, u32[]{:S(2)}, u32[]{:S(2)}) collective-permute-start(bf16[192,640]{1,0:T(8,128)(2,1)S(1)} %constant_dynamic-slice_fusion), channel_id=1, source_target_pairs={{0,8},{4,12},{8,0},{12,4},{1,9},{5,13},{9,1},{13,5},{2,10},{6,14},... | collective-permute-start | bytes 737288 | tf_op jit(solution)/shard_map/ppermute | solution.py:453
  32.3 2.9 %copy-start.11 = (bf16[320,768]{1,0:T(8,128)(2,1)}, bf16[320,768]{1,0:T(8,128)(2,1)S(1)}, u32[]{:S(2)}) copy-start(bf16[320,768]{1,0:T(8,128)(2,1)S(1)} %collective-permute-done.4.core_ref) | copy-start | bytes 1474564
  32.7 10.2 %copy-start.5 = (bf16[10,8,8,768]{3,2,1,0:T(8,128)(2,1)S(1)}, bf16[10,8,8,768]{3,2,1,0:T(8,128)(2,1)}, u32[]{:S(2)}) copy-start(bf16[10,8,8,768]{3,2,1,0:T(8,128)(2,1)} %token_in.1) | copy-start | bytes 2949124
  32.7 10.2 %copy-start.7 = (f32[768]{0:T(1024)S(1)}, f32[768]{0:T(1024)}, u32[]{:S(2)}) copy-start(f32[768]{0:T(1024)} %param.23) | copy-start | bytes 9220
  32.7 7.6 %collective-permute-start.7 = (bf16[10,768]{1,0:T(8,128)(2,1)S(1)}, bf16[10,768]{1,0:T(8,128)(2,1)S(1)}, u32[]{:S(2)}, u32[]{:S(2)}) collective-permute-start(bf16[10,768]{1,0:T(8,128)(2,1)S(1)} %maximum_multiply_fusion), channel_id=1, source_target_pairs={{0,2},{2,0},{1,3},{3,1},{4,6},{6,4},{5,7},{7,5},{8,10},{10,8},{9,1... | collective-permute-start | bytes 46088 | tf_op jit(solution)/shard_map/ppermute | solution.py:447
  35.3 7.3 %collective-permute-start.9 = (bf16[192,640]{1,0:T(8,128)(2,1)S(1)}, bf16[192,640]{1,0:T(8,128)(2,1)S(1)}, u32[]{:S(2)}, u32[]{:S(2)}) collective-permute-start(bf16[192,640]{1,0:T(8,128)(2,1)S(1)} %constant_dynamic-slice_fusion), channel_id=1, source_target_pairs={{0,4},{4,0},{8,12},{12,8},{1,5},{5,1},{9,13},{13,9},{2,6},{6,2},{1... | collective-permute-start | bytes 737288 | tf_op jit(solution)/shard_map/ppermute | solution.py:453
  35.3 7.6 %collective-permute-start.8 = (bf16[5,8,8,768]{3,2,1,0:T(8,128)(2,1)S(1)}, bf16[5,8,8,768]{3,2,1,0:T(8,128)(2,1)S(1)}, u32[]{:S(2)}, u32[]{:S(2)}) collective-permute-start(bf16[5,8,8,768]{3,2,1,0:T(8,128)(2,1)S(1)} %collective-permute-done.5), channel_id=1, source_target_pairs={{0,1},{1,0},{2,3},{3,2},{4,5},{5,4},{6,7},{7,6},{8,9},{9,8},{10,11... | collective-permute-start | bytes 1474568 | tf_op jit(solution)/shard_map/ppermute | solution.py:450
  39.7 3.7 %collective-permute-start.6 = (bf16[320,768]{1,0:T(8,128)(2,1)S(1)}, bf16[320,768]{1,0:T(8,128)(2,1)S(1)}, u32[]{:S(2)}, u32[]{:S(2)}) collective-permute-start(bf16[320,768]{1,0:T(8,128)(2,1)S(1)} %collective-permute-done.2.rest_0_), channel_id=1, source_target_pairs={{0,1},{1,0},{2,3},{3,2},{4,5},{5,4},{6,7},{7,6},{8,9},{9,8},{10,11... | collective-permute-start | bytes 1474568 | tf_op jit(solution)/shard_map/ppermute | solution.py:450
  40.4 3.1 %copy-start.12 = (bf16[192,640]{1,0:T(8,128)(2,1)}, bf16[192,640]{1,0:T(8,128)(2,1)S(1)}, u32[]{:S(2)}) copy-start(bf16[192,640]{1,0:T(8,128)(2,1)S(1)} %collective-permute-done.10.rest_1_) | copy-start | bytes 737284
  42.6 0.9 copy-start.13
  42.6 7.1 %collective-permute-start.11 = (bf16[192,640]{1,0:T(8,128)(2,1)S(1)}, bf16[192,640]{1,0:T(8,128)(2,1)S(1)}, u32[]{:S(2)}, u32[]{:S(2)}) collective-permute-start(bf16[192,640]{1,0:T(8,128)(2,1)S(1)} %collective-permute-done.10.rest_1_), channel_id=1, source_target_pairs={{0,4},{4,0},{8,12},{12,8},{1,5},{5,1},{9,13},{13,9},{2,6},{6,2},{1... | collective-permute-start | bytes 737288 | tf_op jit(solution)/shard_map/ppermute | solution.py:453
  47.8 12.6 %collective-permute-start.12 = (bf16[2,192,640]{2,1,0:T(8,128)(2,1)S(1)}, bf16[2,192,640]{2,1,0:T(8,128)(2,1)S(1)}, u32[]{:S(2)}, u32[]{:S(2)}) collective-permute-start(bf16[2,192,640]{2,1,0:T(8,128)(2,1)S(1)} %get-tuple-element.66), channel_id=1, source_target_pairs={{0,4},{4,0},{8,12},{12,8},{1,5},{5,1},{9,13},{13,9},{2,6},{6,2},{1... | collective-permute-start | bytes 1474568 | tf_op jit(solution)/shard_map/ppermute | solution.py:453
  62.2 2.6 %collective-permute-start.13 = (bf16[2,320,768]{2,1,0:T(8,128)(2,1)S(1)}, bf16[2,320,768]{2,1,0:T(8,128)(2,1)S(1)}, u32[]{:S(2)}, u32[]{:S(2)}) collective-permute-start(bf16[2,320,768]{2,1,0:T(8,128)(2,1)S(1)} %get-tuple-element.69), channel_id=1, source_target_pairs={{0,1},{1,0},{2,3},{3,2},{4,5},{5,4},{6,7},{7,6},{8,9},{9,8},{10,11... | collective-permute-start | bytes 2949128 | tf_op jit(solution)/shard_map/ppermute | solution.py:450
  65.0 14.5 %collective-permute-start.15 = (bf16[320,768]{1,0:T(8,128)(2,1)S(1)}, bf16[320,768]{1,0:T(8,128)(2,1)S(1)}, u32[]{:S(2)}, u32[]{:S(2)}) collective-permute-start(bf16[320,768]{1,0:T(8,128)(2,1)S(1)} %get-tuple-element.80), channel_id=1, source_target_pairs={{0,2},{2,0},{1,3},{3,1},{4,6},{6,4},{5,7},{7,5},{8,10},{10,8},{9,1... | collective-permute-start | bytes 1474568 | tf_op jit(solution)/shard_map/ppermute | solution.py:447
  65.2 14.4 %collective-permute-start.14 = (bf16[192,640]{1,0:T(8,128)(2,1)S(1)}, bf16[192,640]{1,0:T(8,128)(2,1)S(1)}, u32[]{:S(2)}, u32[]{:S(2)}) collective-permute-start(bf16[192,640]{1,0:T(8,128)(2,1)S(1)} %fusion.3), channel_id=1, source_target_pairs={{0,8},{4,12},{8,0},{12,4},{1,9},{5,13},{9,1},{13,5},{2,10},{6,14},... | collective-permute-start | bytes 737288 | tf_op jit(solution)/shard_map/ppermute | solution.py:453
  67.9 17.7 %collective-permute-start.17 = (bf16[2,192,640]{2,1,0:T(8,128)(2,1)S(1)}, bf16[2,192,640]{2,1,0:T(8,128)(2,1)S(1)}, u32[]{:S(2)}, u32[]{:S(2)}) collective-permute-start(bf16[2,192,640]{2,1,0:T(8,128)(2,1)S(1)} %get-tuple-element.72), channel_id=1, source_target_pairs={{0,4},{4,0},{8,12},{12,8},{1,5},{5,1},{9,13},{13,9},{2,6},{6,2},{1... | collective-permute-start | bytes 1474568 | tf_op jit(solution)/shard_map/ppermute | solution.py:453
  85.7 13.4 %collective-permute-start.18 = (bf16[192,640]{1,0:T(8,128)(2,1)S(1)}, bf16[192,640]{1,0:T(8,128)(2,1)S(1)}, u32[]{:S(2)}, u32[]{:S(2)}) collective-permute-start(bf16[192,640]{1,0:T(8,128)(2,1)S(1)} %fusion.4), channel_id=1, source_target_pairs={{0,8},{4,12},{8,0},{12,4},{1,9},{5,13},{9,1},{13,5},{2,10},{6,14},... | collective-permute-start | bytes 737288 | tf_op jit(solution)/shard_map/ppermute | solution.py:453
  87.3 13.6 %collective-permute-start.20 = (bf16[192,640]{1,0:T(8,128)(2,1)S(1)}, bf16[192,640]{1,0:T(8,128)(2,1)S(1)}, u32[]{:S(2)}, u32[]{:S(2)}) collective-permute-start(bf16[192,640]{1,0:T(8,128)(2,1)S(1)} %fusion.2), channel_id=1, source_target_pairs={{0,2},{2,0},{1,3},{3,1},{4,6},{6,4},{5,7},{7,5},{8,10},{10,8},{9,1... | collective-permute-start | bytes 737288 | tf_op jit(solution)/shard_map/ppermute | solution.py:447
  87.8 14.2 %collective-permute-start.16 = (bf16[5,8,8,768]{3,2,1,0:T(8,128)(2,1)S(1)}, bf16[5,8,8,768]{3,2,1,0:T(8,128)(2,1)S(1)}, u32[]{:S(2)}, u32[]{:S(2)}) collective-permute-start(bf16[5,8,8,768]{3,2,1,0:T(8,128)(2,1)S(1)} %norm_conv_back.1), channel_id=1, source_target_pairs={{0,1},{1,0},{2,3},{3,2},{4,5},{5,4},{6,7},{7,6},{8,9},{9,8},{10,11... | collective-permute-start | bytes 1474568 | tf_op jit(solution)/shard_map/ppermute | solution.py:450
  99.2 7.7 %collective-permute-start.19 = (bf16[192,640]{1,0:T(8,128)(2,1)S(1)}, bf16[192,640]{1,0:T(8,128)(2,1)S(1)}, u32[]{:S(2)}, u32[]{:S(2)}) collective-permute-start(bf16[192,640]{1,0:T(8,128)(2,1)S(1)} %fusion.1), channel_id=1, source_target_pairs={{0,2},{2,0},{1,3},{3,1},{4,6},{6,4},{5,7},{7,5},{8,10},{10,8},{9,1... | collective-permute-start | bytes 737288 | tf_op jit(solution)/shard_map/ppermute | solution.py:447

commit v4 on v3

--- a/solution.py
+++ b/solution.py
@@ -551,21 +551,21 @@
     fall, fall_away = joined(fall, fall_from)
     climb, climb_away = rise(my_place, (normed, next_normed), hidden_grad, shard)
     climb_from = meet(climb_away, 1)
-    keep, send = back(after(hidden_grad, climb, fall_away), whole_up)
+    climb, climb_away = joined(climb, climb_from)
+    fall = settle(fall, fall_away)
+    keep, send = back(after(hidden_grad, climb_away, fall), whole_up)
     from_core = over_cores(send)
     far_grad = (keep[1].astype(F32) + from_core[1].astype(F32)).astype(BF16)
     from_pair = over_pair(far_grad)
-    fall = settle(fall, fall_away, climb, from_pair)
-    near_grad = after(keep[0].astype(F32) + from_core[0].astype(F32), fall)
+    climb = settle(climb, climb_away)
+    near_grad = after(keep[0].astype(F32) + from_core[0].astype(F32), climb)
     own_pooled = lax.dynamic_slice_in_dim(pooled, core * mine, mine, 0).astype(F32)[:, None, :] / spots
     grad_half = tail(base, live_tiles, near_grad, from_pair, normal, inv, token_grad, own_pooled, dw_kernel, ln_gain)
-    climb, climb_away = joined(climb, after(climb_from, grad_half))
-    climb = settle(climb, climb_away)
     other_half = over_cores(grad_half)
     first = jnp.where(core == 0, grad_half, other_half)
     second = jnp.where(core == 0, other_half, grad_half)
     tile_grad = jnp.concatenate([first, second], axis=0)
-    grad_down = both_sides(fall)
+    grad_down = both_sides(fall, grad_half)
     return (tile_grad, both_sides(climb, tile_grad, grad_down), grad_down)
 
 

time: 108 us -> 106 us (0.981)
  waiting for transfers between devices: 43.3 us -> 39.1 us
  starting transfers between devices: 25.4 us -> 26.5 us
    ppermute x6, waiting for transfers between devices: 3.91 us -> 1.81 us  [over_pair(): return lax.ppermute(value, 'dp', pair)]
    ppermute x5, waiting for transfers between devices: 2.56 us -> 1.13 us  [over_cores(): return lax.ppermute(value, 'mp', swap)]
  transfers between devices with their start and end apart: 21 -> 21, of which waited for: 9 -> 11; matrix products, arithmetic and copies ran while one was open for 4% -> 6% of each run, Pallas kernels for 25% -> 26%
where the time goes in v4:
time: 106 us
  waiting for transfers between devices  39.1 us (37%)
  Pallas kernels  28.9 us (27%)
  starting transfers between devices  26.5 us (25%)
  other arithmetic  6.91 us (7%)
  local copies, waits for them, and re-layouts  2.89 us (3%)
  between operations  1.66 us (2%)
    ppermute x10, waiting for transfers between devices, meet(): return lax.ppermute(value, 'seq', [(i, i ^ step) for i in range(n_seq)])  36.2 us
    ppermute x10, starting transfers between devices, meet(): return lax.ppermute(value, 'seq', [(i, i ^ step) for i in range(n_seq)])  17.9 us
    ppermute x6, starting transfers between devices, over_pair(): return lax.ppermute(value, 'dp', pair)  7.92 us
    pallas_call x1, Pallas kernels, tail(): pl.pallas_call(tail_kernel, name='norm_conv_back', out_shape=jax.ShapeDty...  5.93 us
    pallas_call x1, Pallas kernels, front(): pl.pallas_call(front_kernel, name='conv_norm', out_shape=(pltpu.HBM((rows...  5.46 us
    pallas_call x1, Pallas kernels, down(): pl.pallas_call(functools.partial(down_kernel, apart), name='hidden_grad',...  4.93 us
    pallas_call x1, Pallas kernels, up(): pl.pallas_call(functools.partial(up_kernel, apart), name='hidden_own', ou...  4.42 us
    pallas_call x1, Pallas kernels, up_next(): pl.pallas_call(up_next_kernel, name='hidden_next_and_down_grad', out_shap...  4.36 us
  transfers between devices with their start and end apart: 21, of which 11 were waited for; matrix products, arithmetic and copies ran while one was open for 6% of the time, Pallas kernels for 26%

profile of v4, /device:TPU:0, one launch (start us, length us, event | category | flops | bytes accessed | tf_op | source)
XLA Modules:
  0.0 106.0 jit_solution(16462096368880468330)
XLA Ops:
  0.7 0.8 slice_bitcast_fusion.1
  1.5 0.7 pad_slice_fusion
  2.2 1.0 constant_dynamic-slice_fusion.1
  3.3 4.1 %collective-permute-start.1 = (bf16[208,640]{1,0:T(8,128)(2,1)S(1)}, bf16[208,640]{1,0:T(8,128)(2,1)S(1)}, u32[]{:S(2)}, u32[]{:S(2)}) collective-permute-start(bf16[208,640]{1,0:T(8,128)(2,1)S(1)} %pad_maximum_fusion.1), channel_id=1, source_target_pairs={{0,8},{4,12},{8,0},{12,4},{1,9},{5,13},{9,1},{13,5},{2,10},{6,14},... | collective-permute-start | bytes 798728 | tf_op jit(solution)/shard_map/ppermute | solution.py:453
  7.4 1.6 %collective-permute-start = (bf16[208,640]{1,0:T(8,128)(2,1)S(1)}, bf16[208,640]{1,0:T(8,128)(2,1)S(1)}, u32[]{:S(2)}, u32[]{:S(2)}) collective-permute-start(bf16[208,640]{1,0:T(8,128)(2,1)S(1)} %pad_maximum_fusion.1), channel_id=1, source_target_pairs={{0,4},{4,0},{8,12},{12,8},{1,5},{5,1},{9,13},{13,9},{2,6},{6,2},{1... | collective-permute-start | bytes 798728 | tf_op jit(solution)/shard_map/ppermute | solution.py:453
  9.6 0.1 fusion.25
  9.7 1.1 %dynamic-slice_multiply_fusion = bf16[5,8,8,768]{3,2,1,0:T(8,128)(2,1)S(1)} fusion(bf16[10,8,8,768]{3,2,1,0:T(8,128)(2,1)} %token_in.1, s32[]{:T(128)S(6)} %select_n.140, bf16[5]{0:T(256)(128)(2,1)S(1)} %get-tuple-element.109), kind=kLoop, calls=%fused_computation.16 | loop fusion | flops 245760 | bytes 983054 | tf_op jit(solution)/shard_map/mul | solution.py:491
  10.8 1.6 %collective-permute-start.5 = (bf16[5,8,8,768]{3,2,1,0:T(8,128)(2,1)S(1)}, bf16[5,8,8,768]{3,2,1,0:T(8,128)(2,1)S(1)}, u32[]{:S(2)}, u32[]{:S(2)}) collective-permute-start(bf16[5,8,8,768]{3,2,1,0:T(8,128)(2,1)S(1)} %dynamic-slice_multiply_fusion), channel_id=1, source_target_pairs={{0,2},{2,0},{1,3},{3,1},{4,6},{6,4},{5,7},{7,5},{8,10},{10,8},{9,1... | collective-permute-start | bytes 1474568 | tf_op jit(solution)/shard_map/ppermute | solution.py:447
  12.4 5.5 %conv_norm.1 = (bf16[320,768]{1,0:T(8,128)(2,1)}, f32[320,768]{1,0:T(8,128)}, f32[320,128]{1,0:T(8,128)}) custom-call(s32[1]{0:T(128)} %bitcast.base_ref, bf16[10,8,8,768]{3,2,1,0:T(8,128)(2,1)S(1)} %copy-done, f32[7,7,768]{2,1,0:T(8,128)S(1)} %copy-done.1, f32[768]{0:T(1024)S(1)} %copy-done.2, f32[768]{0:T(1024)S(1)} %copy-done.4, f32[768]{0:T(1024)S(1)} %copy-done.3), custom_call_target="tpu_custom_call" | custom-call | flops 10737418240 | bytes 4194304 | tf_op jit(solution)/shard_map/conv_norm/pallas_call | solution.py:110
  17.9 1.7 %collective-permute-done.1.rest_1_ = bf16[208,640]{1,0:T(8,128)(2,1)S(1)} collective-permute-done((bf16[208,640]{1,0:T(8,128)(2,1)S(1)}, bf16[208,640]{1,0:T(8,128)(2,1)S(1)}, u32[]{:S(2)}, u32[]{:S(2)}) %collective-permute-start.1) | collective-permute-done | bytes 266272 | tf_op jit(solution)/shard_map/ppermute | solution.py:453
  19.6 0.2 collective-permute-done.rest_0_
  19.8 1.5 %collective-permute-start.3 = (bf16[208,640]{1,0:T(8,128)(2,1)S(1)}, bf16[208,640]{1,0:T(8,128)(2,1)S(1)}, u32[]{:S(2)}, u32[]{:S(2)}) collective-permute-start(bf16[208,640]{1,0:T(8,128)(2,1)S(1)} %collective-permute-done.1.rest_1_), channel_id=1, source_target_pairs={{0,4},{4,0},{8,12},{12,8},{1,5},{5,1},{9,13},{13,9},{2,6},{6,2},{1... | collective-permute-start | bytes 798728 | tf_op jit(solution)/shard_map/ppermute | solution.py:453
  21.4 1.5 %collective-permute-start.2 = (bf16[320,768]{1,0:T(8,128)(2,1)}, bf16[320,768]{1,0:T(8,128)(2,1)S(1)}, u32[]{:S(2)}, u32[]{:S(2)}) collective-permute-start(bf16[320,768]{1,0:T(8,128)(2,1)} %get-tuple-element.43.own_ref), channel_id=1, source_target_pairs={{0,2},{2,0},{1,3},{3,1},{4,6},{6,4},{5,7},{7,5},{8,10},{10,8},{9,1... | collective-permute-start | bytes 1474568 | tf_op jit(solution)/shard_map/ppermute | solution.py:447
  23.0 2.5 %collective-permute-start.10 = (bf16[192,640]{1,0:T(8,128)(2,1)S(1)}, bf16[192,640]{1,0:T(8,128)(2,1)S(1)}, u32[]{:S(2)}, u32[]{:S(2)}) collective-permute-start(bf16[192,640]{1,0:T(8,128)(2,1)S(1)} %constant_dynamic-slice_fusion), channel_id=1, source_target_pairs={{0,8},{4,12},{8,0},{12,4},{1,9},{5,13},{9,1},{13,5},{2,10},{6,14},... | collective-permute-start | bytes 737288 | tf_op jit(solution)/shard_map/ppermute | solution.py:453
  25.5 6.8 %collective-permute-done.3.rest_2_ = bf16[208,640]{1,0:T(8,128)(2,1)S(1)} collective-permute-done((bf16[208,640]{1,0:T(8,128)(2,1)S(1)}, bf16[208,640]{1,0:T(8,128)(2,1)S(1)}, u32[]{:S(2)}, u32[]{:S(2)}) %collective-permute-start.3) | collective-permute-done | bytes 266272 | tf_op jit(solution)/shard_map/ppermute | solution.py:453
  32.6 0.1 maximum_multiply_fusion
  32.7 2.6 %collective-permute-start.7 = (bf16[10,768]{1,0:T(8,128)(2,1)S(1)}, bf16[10,768]{1,0:T(8,128)(2,1)S(1)}, u32[]{:S(2)}, u32[]{:S(2)}) collective-permute-start(bf16[10,768]{1,0:T(8,128)(2,1)S(1)} %maximum_multiply_fusion), channel_id=1, source_target_pairs={{0,2},{2,0},{1,3},{3,1},{4,6},{6,4},{5,7},{7,5},{8,10},{10,8},{9,1... | collective-permute-start | bytes 46088 | tf_op jit(solution)/shard_map/ppermute | solution.py:447
  35.3 4.4 %hidden_own.1 = (bf16[640,640]{1,0:T(8,128)(2,1)S(1)}, f32[640,640]{1,0:T(8,128)S(1)}, bf16[768,640]{1,0:T(8,128)(2,1)S(1)}, bf16[640,768]{1,0:T(8,128)(2,1)S(1)}) custom-call(s32[6]{0:T(128)S(1)} %pad_add_fusion.place_ref, bf16[320,768]{1,0:T(8,128)(2,1)} %get-tuple-element.43.own_ref, bf16[320,768]{1,0:T(8,128)(2,1)} %copy-done.11, ...), custom_call_target="tpu_custom_call" | custom-call | flops 10737418240 | bytes 4194304 | tf_op jit(solution)/shard_map/hidden_own/pallas_call | solution.py:225
  39.7 0.6 collective-permute-start.6
  40.4 2.2 %collective-permute-done.9.rest_0_ = bf16[192,640]{1,0:T(8,128)(2,1)S(1)} collective-permute-done((bf16[192,640]{1,0:T(8,128)(2,1)S(1)}, bf16[192,640]{1,0:T(8,128)(2,1)S(1)}, u32[]{:S(2)}, u32[]{:S(2)}) %collective-permute-start.9) | collective-permute-done | bytes 245792 | tf_op jit(solution)/shard_map/ppermute | solution.py:453
  42.6 0.3 collective-permute-start.11
  42.9 0.6 multiply_convert_fusion
  43.5 4.4 %hidden_next_and_down_grad.1 = (bf16[2,192,640]{2,1,0:T(8,128)(2,1)S(1)}, bf16[2,192,640]{2,1,0:T(8,128)(2,1)S(1)}, f32[640,640]{1,0:T(8,128)S(1)}, bf16[640,768]{1,0:T(8,128)(2,1)S(1)}, bf16[1280,768]{1,0:T(8,128)(2,1)S(1)}) custom-call(s32[1]{0:T(128)} %bitcast.6.seq_ref, bf16[320,768]{1,0:T(8,128)(2,1)S(1)} %collective-permute-done.2.rest_0_, ...), custom_call_target="tpu_custom_call" | custom-call | flops 10737418240 | bytes 4194304 | tf_op jit(solution)/shard_map/hidden_next_and_down_grad/pallas_call | solution.py:246
  47.8 1.8 %collective-permute-start.13 = (bf16[2,192,640]{2,1,0:T(8,128)(2,1)S(1)}, bf16[2,192,640]{2,1,0:T(8,128)(2,1)S(1)}, u32[]{:S(2)}, u32[]{:S(2)}) collective-permute-start(bf16[2,192,640]{2,1,0:T(8,128)(2,1)S(1)} %get-tuple-element.66), channel_id=1, source_target_pairs={{0,4},{4,0},{8,12},{12,8},{1,5},{5,1},{9,13},{13,9},{2,6},{6,2},{1... | collective-permute-start | bytes 1474568 | tf_op jit(solution)/shard_map/ppermute | solution.py:453
  49.6 4.9 %hidden_grad.1.grad_ref = bf16[1280,640]{1,0:T(8,128)(2,1)S(1)} custom-call(s32[6]{0:T(128)S(1)} %pad_add_fusion.place_ref, bf16[1280,768]{1,0:T(8,128)(2,1)S(1)} %get-tuple-element.54.branch_ref, f32[640,640]{1,0:T(8,128)S(1)} %get-tuple-element.55.slope_own, f32[640,640]{1,0:T(8,128)S(1)} %get-tuple-element.56.slope_next, bf16[192,1280]{1,0:T(8,128)(2,1)} %local.3, ...), custom_call_target="tpu_custom_call" | custom-call | flops 10737418240 | bytes 4194304 | tf_op jit(solution)/shard_map/hidden_grad/pallas_call | solution.py:286
  54.6 2.0 %up_grad.1 = (bf16[2,192,640]{2,1,0:T(8,128)(2,1)S(1)}, bf16[2,192,640]{2,1,0:T(8,128)(2,1)S(1)}) custom-call(s32[1]{0:T(128)} %bitcast.6.seq_ref, bf16[640,768]{1,0:T(8,128)(2,1)S(1)} %get-tuple-element.61.own_ref, bf16[640,768]{1,0:T(8,128)(2,1)S(1)} %get-tuple-element.62.next_ref, bf16[1280,640]{1,0:T(8,128)(2,1)S(1)} %hidden_grad.1.grad_ref), custom_call_target="tpu_custom_call" | custom-call | flops 10737418240 | bytes 4194304 | tf_op jit(solution)/shard_map/up_grad/pallas_call | solution.py:309
  56.6 0.8 collective-permute-start.12
  57.4 4.7 %collective-permute-done.13 = bf16[2,192,640]{2,1,0:T(8,128)(2,1)S(1)} collective-permute-done((bf16[2,192,640]{2,1,0:T(8,128)(2,1)S(1)}, bf16[2,192,640]{2,1,0:T(8,128)(2,1)S(1)}, u32[]{:S(2)}, u32[]{:S(2)}) %collective-permute-start.13) | collective-permute-done | bytes 491552 | tf_op jit(solution)/shard_map/ppermute | solution.py:453
  62.1 3.1 %collective-permute-start.14 = (bf16[192,640]{1,0:T(8,128)(2,1)S(1)}, bf16[192,640]{1,0:T(8,128)(2,1)S(1)}, u32[]{:S(2)}, u32[]{:S(2)}) collective-permute-start(bf16[192,640]{1,0:T(8,128)(2,1)S(1)} %fusion.4), channel_id=1, source_target_pairs={{0,8},{4,12},{8,0},{12,4},{1,9},{5,13},{9,1},{13,5},{2,10},{6,14},... | collective-permute-start | bytes 737288 | tf_op jit(solution)/shard_map/ppermute | solution.py:453
  65.3 10.9 %collective-permute-done.12 = bf16[2,192,640]{2,1,0:T(8,128)(2,1)S(1)} collective-permute-done((bf16[2,192,640]{2,1,0:T(8,128)(2,1)S(1)}, bf16[2,192,640]{2,1,0:T(8,128)(2,1)S(1)}, u32[]{:S(2)}, u32[]{:S(2)}) %collective-permute-start.12) | collective-permute-done | bytes 491552 | tf_op jit(solution)/shard_map/ppermute | solution.py:453
  76.3 0.1 fusion.2
  76.4 1.8 %normed_grad.1 = (bf16[2,320,768]{2,1,0:T(8,128)(2,1)S(1)}, bf16[2,320,768]{2,1,0:T(8,128)(2,1)S(1)}) custom-call(bf16[1280,640]{1,0:T(8,128)(2,1)S(1)} %hidden_grad.1.grad_ref, bf16[768,640]{1,0:T(8,128)(2,1)S(1)} %get-tuple-element.53.rest_7_.weight_ref), custom_call_target="tpu_custom_call" | custom-call | flops 10737418240 | bytes 4194304 | tf_op jit(solution)/shard_map/normed_grad/pallas_call | solution.py:331
  78.2 2.2 %collective-permute-start.16 = (bf16[192,640]{1,0:T(8,128)(2,1)S(1)}, bf16[192,640]{1,0:T(8,128)(2,1)}, u32[]{:S(2)}, u32[]{:S(2)}) collective-permute-start(bf16[192,640]{1,0:T(8,128)(2,1)S(1)} %fusion.3), channel_id=1, source_target_pairs={{0,8},{4,12},{8,0},{12,4},{1,9},{5,13},{9,1},{13,5},{2,10},{6,14},... | collective-permute-start | bytes 737288 | tf_op jit(solution)/shard_map/ppermute | solution.py:453
  80.4 0.4 collective-permute-done.15
  80.8 0.2 fusion
  81.0 0.1 collective-permute-start.17
  81.2 2.0 %collective-permute-start.20 = (bf16[192,640]{1,0:T(8,128)(2,1)S(1)}, bf16[192,640]{1,0:T(8,128)(2,1)S(1)}, u32[]{:S(2)}, u32[]{:S(2)}) collective-permute-start(bf16[192,640]{1,0:T(8,128)(2,1)S(1)} %fusion.2), channel_id=1, source_target_pairs={{0,2},{2,0},{1,3},{3,1},{4,6},{6,4},{5,7},{7,5},{8,10},{10,8},{9,1... | collective-permute-start | bytes 737288 | tf_op jit(solution)/shard_map/ppermute | solution.py:447
  83.2 9.7 %collective-permute-done.16 = bf16[192,640]{1,0:T(8,128)(2,1)} collective-permute-done((bf16[192,640]{1,0:T(8,128)(2,1)S(1)}, bf16[192,640]{1,0:T(8,128)(2,1)}, u32[]{:S(2)}, u32[]{:S(2)}) %collective-permute-start.16) | collective-permute-done | bytes 245792 | tf_op jit(solution)/shard_map/ppermute | solution.py:453
  92.9 1.1 fusion.1
  93.9 0.1 collective-permute-start.19
  94.1 1.1 %collective-permute-done.17.far_ref = bf16[320,768]{1,0:T(8,128)(2,1)S(1)} collective-permute-done((bf16[320,768]{1,0:T(8,128)(2,1)S(1)}, bf16[320,768]{1,0:T(8,128)(2,1)S(1)}, u32[]{:S(2)}, u32[]{:S(2)}) %collective-permute-start.17) | collective-permute-done | bytes 491552 | tf_op jit(solution)/shard_map/ppermute | solution.py:447
  95.2 5.9 %norm_conv_back.1 = bf16[5,8,8,768]{3,2,1,0:T(8,128)(2,1)S(1)} custom-call(s32[1]{0:T(128)} %bitcast.base_ref, s32[1]{0:T(128)} %copy.15.live_ref, f32[320,768]{1,0:T(8,128)} %get-tuple-element.40.normal_in, f32[320,128]{1,0:T(8,128)} %get-tuple-element.41.inv_in, bf16[10,8,8,768]{3,2,1,0:T(8,128)(2,1)} %token_in.1, f32[7,7,768]{2,1,0:T(8,128)} %taps_in.1, ...), custom_call_target="tpu_custom_call" | custom-call | flops 10737418240 | bytes 4194304 | tf_op jit(solution)/shard_map/norm_conv_back/pallas_call | solution.py:396
  101.2 1.0 maximum_convert_fusion
  102.3 0.8 collective-permute-done.18
  103.0 0.1 broadcast_select_fusion.1
  103.1 1.0 pad_maximum_fusion
  104.2 0.7 collective-permute-done.19
  104.9 1.0 maximum_convert_fusion.1
  (62 shorter events, 1.1 us)
Async XLA Ops:
  0.6 11.8 %copy-start.4 = (f32[768]{0:T(1024)S(1)}, f32[768]{0:T(1024)}, u32[]{:S(2)}) copy-start(f32[768]{0:T(1024)} %gain_ref.3) | copy-start | bytes 9220
  0.6 11.8 %copy-start.1 = (f32[7,7,768]{2,1,0:T(8,128)S(1)}, f32[7,7,768]{2,1,0:T(8,128)}, u32[]{:S(2)}) copy-start(f32[7,7,768]{2,1,0:T(8,128)} %taps_in.1) | copy-start | bytes 451588
  0.7 11.8 %copy-start.3 = (f32[768]{0:T(1024)S(1)}, f32[768]{0:T(1024)}, u32[]{:S(2)}) copy-start(f32[768]{0:T(1024)} %shift_ref.1) | copy-start | bytes 9220
  0.7 11.7 %copy-start.2 = (f32[768]{0:T(1024)S(1)}, f32[768]{0:T(1024)}, u32[]{:S(2)}) copy-start(f32[768]{0:T(1024)} %bias_ref.1) | copy-start | bytes 9220
  0.7 11.7 %copy-start = (bf16[10,8,8,768]{3,2,1,0:T(8,128)(2,1)S(1)}, bf16[10,8,8,768]{3,2,1,0:T(8,128)(2,1)}, u32[]{:S(2)}) copy-start(bf16[10,8,8,768]{3,2,1,0:T(8,128)(2,1)} %tiles_ref.1) | copy-start | bytes 2949124
  3.3 16.3 %collective-permute-start.1 = (bf16[208,640]{1,0:T(8,128)(2,1)S(1)}, bf16[208,640]{1,0:T(8,128)(2,1)S(1)}, u32[]{:S(2)}, u32[]{:S(2)}) collective-permute-start(bf16[208,640]{1,0:T(8,128)(2,1)S(1)} %pad_maximum_fusion.1), channel_id=1, source_target_pairs={{0,8},{4,12},{8,0},{12,4},{1,9},{5,13},{9,1},{13,5},{2,10},{6,14},... | collective-permute-start | bytes 798728 | tf_op jit(solution)/shard_map/ppermute | solution.py:453
  7.4 12.4 %collective-permute-start = (bf16[208,640]{1,0:T(8,128)(2,1)S(1)}, bf16[208,640]{1,0:T(8,128)(2,1)S(1)}, u32[]{:S(2)}, u32[]{:S(2)}) collective-permute-start(bf16[208,640]{1,0:T(8,128)(2,1)S(1)} %pad_maximum_fusion.1), channel_id=1, source_target_pairs={{0,4},{4,0},{8,12},{12,8},{1,5},{5,1},{9,13},{13,9},{2,6},{6,2},{1... | collective-permute-start | bytes 798728 | tf_op jit(solution)/shard_map/ppermute | solution.py:453
  10.8 14.6 %collective-permute-start.5 = (bf16[5,8,8,768]{3,2,1,0:T(8,128)(2,1)S(1)}, bf16[5,8,8,768]{3,2,1,0:T(8,128)(2,1)S(1)}, u32[]{:S(2)}, u32[]{:S(2)}) collective-permute-start(bf16[5,8,8,768]{3,2,1,0:T(8,128)(2,1)S(1)} %dynamic-slice_multiply_fusion), channel_id=1, source_target_pairs={{0,2},{2,0},{1,3},{3,1},{4,6},{6,4},{5,7},{7,5},{8,10},{10,8},{9,1... | collective-permute-start | bytes 1474568 | tf_op jit(solution)/shard_map/ppermute | solution.py:447
  12.4 8.9 %copy-start.10 = (f32[1280]{0:T(1024)S(1)}, f32[1280]{0:T(1024)}, u32[]{:S(2)}) copy-start(f32[1280]{0:T(1024)} %param.21) | copy-start | bytes 15364
  12.4 10.5 %copy-start.6 = (bf16[192,1280]{1,0:T(8,128)(2,1)S(1)}, bf16[192,1280]{1,0:T(8,128)(2,1)}, u32[]{:S(2)}) copy-start(bf16[192,1280]{1,0:T(8,128)(2,1)} %local.3) | copy-start | bytes 1474564
  19.6 15.7 %copy-start.9 = (bf16[208,640]{1,0:T(8,128)(2,1)}, bf16[208,640]{1,0:T(8,128)(2,1)S(1)}, u32[]{:S(2)}) copy-start(bf16[208,640]{1,0:T(8,128)(2,1)S(1)} %collective-permute-done.1.rest_1_) | copy-start | bytes 798724
  19.8 15.5 %copy-start.8 = (bf16[208,640]{1,0:T(8,128)(2,1)}, bf16[208,640]{1,0:T(8,128)(2,1)S(1)}, u32[]{:S(2)}) copy-start(bf16[208,640]{1,0:T(8,128)(2,1)S(1)} %collective-permute-done.rest_0_) | copy-start | bytes 798724
  19.8 12.6 %collective-permute-start.4 = (bf16[320,768]{1,0:T(8,128)(2,1)}, bf16[320,768]{1,0:T(8,128)(2,1)S(1)}, u32[]{:S(2)}, u32[]{:S(2)}) collective-permute-start(bf16[320,768]{1,0:T(8,128)(2,1)} %get-tuple-element.43.own_ref), channel_id=1, source_target_pairs={{0,1},{1,0},{2,3},{3,2},{4,5},{5,4},{6,7},{7,6},{8,9},{9,8},{10,11... | collective-permute-start | bytes 1474568 | tf_op jit(solution)/shard_map/ppermute | solution.py:450
  19.8 12.5 %collective-permute-start.3 = (bf16[208,640]{1,0:T(8,128)(2,1)S(1)}, bf16[208,640]{1,0:T(8,128)(2,1)S(1)}, u32[]{:S(2)}, u32[]{:S(2)}) collective-permute-start(bf16[208,640]{1,0:T(8,128)(2,1)S(1)} %collective-permute-done.1.rest_1_), channel_id=1, source_target_pairs={{0,4},{4,0},{8,12},{12,8},{1,5},{5,1},{9,13},{13,9},{2,6},{6,2},{1... | collective-permute-start | bytes 798728 | tf_op jit(solution)/shard_map/ppermute | solution.py:453
  21.4 18.3 %collective-permute-start.2 = (bf16[320,768]{1,0:T(8,128)(2,1)}, bf16[320,768]{1,0:T(8,128)(2,1)S(1)}, u32[]{:S(2)}, u32[]{:S(2)}) collective-permute-start(bf16[320,768]{1,0:T(8,128)(2,1)} %get-tuple-element.43.own_ref), channel_id=1, source_target_pairs={{0,2},{2,0},{1,3},{3,1},{4,6},{6,4},{5,7},{7,5},{8,10},{10,8},{9,1... | collective-permute-start | bytes 1474568 | tf_op jit(solution)/shard_map/ppermute | solution.py:447
  23.0 17.4 %collective-permute-start.10 = (bf16[192,640]{1,0:T(8,128)(2,1)S(1)}, bf16[192,640]{1,0:T(8,128)(2,1)S(1)}, u32[]{:S(2)}, u32[]{:S(2)}) collective-permute-start(bf16[192,640]{1,0:T(8,128)(2,1)S(1)} %constant_dynamic-slice_fusion), channel_id=1, source_target_pairs={{0,8},{4,12},{8,0},{12,4},{1,9},{5,13},{9,1},{13,5},{2,10},{6,14},... | collective-permute-start | bytes 737288 | tf_op jit(solution)/shard_map/ppermute | solution.py:453
  32.3 2.9 %copy-start.11 = (bf16[320,768]{1,0:T(8,128)(2,1)}, bf16[320,768]{1,0:T(8,128)(2,1)S(1)}, u32[]{:S(2)}) copy-start(bf16[320,768]{1,0:T(8,128)(2,1)S(1)} %collective-permute-done.4.core_ref) | copy-start | bytes 1474564
  32.7 10.2 %copy-start.5 = (bf16[10,8,8,768]{3,2,1,0:T(8,128)(2,1)S(1)}, bf16[10,8,8,768]{3,2,1,0:T(8,128)(2,1)}, u32[]{:S(2)}) copy-start(bf16[10,8,8,768]{3,2,1,0:T(8,128)(2,1)} %token_in.1) | copy-start | bytes 2949124
  32.7 10.2 %copy-start.7 = (f32[768]{0:T(1024)S(1)}, f32[768]{0:T(1024)}, u32[]{:S(2)}) copy-start(f32[768]{0:T(1024)} %param.23) | copy-start | bytes 9220
  32.7 7.6 %collective-permute-start.7 = (bf16[10,768]{1,0:T(8,128)(2,1)S(1)}, bf16[10,768]{1,0:T(8,128)(2,1)S(1)}, u32[]{:S(2)}, u32[]{:S(2)}) collective-permute-start(bf16[10,768]{1,0:T(8,128)(2,1)S(1)} %maximum_multiply_fusion), channel_id=1, source_target_pairs={{0,2},{2,0},{1,3},{3,1},{4,6},{6,4},{5,7},{7,5},{8,10},{10,8},{9,1... | collective-permute-start | bytes 46088 | tf_op jit(solution)/shard_map/ppermute | solution.py:447
  35.3 7.3 %collective-permute-start.9 = (bf16[192,640]{1,0:T(8,128)(2,1)S(1)}, bf16[192,640]{1,0:T(8,128)(2,1)S(1)}, u32[]{:S(2)}, u32[]{:S(2)}) collective-permute-start(bf16[192,640]{1,0:T(8,128)(2,1)S(1)} %constant_dynamic-slice_fusion), channel_id=1, source_target_pairs={{0,4},{4,0},{8,12},{12,8},{1,5},{5,1},{9,13},{13,9},{2,6},{6,2},{1... | collective-permute-start | bytes 737288 | tf_op jit(solution)/shard_map/ppermute | solution.py:453
  35.3 7.6 %collective-permute-start.8 = (bf16[5,8,8,768]{3,2,1,0:T(8,128)(2,1)S(1)}, bf16[5,8,8,768]{3,2,1,0:T(8,128)(2,1)S(1)}, u32[]{:S(2)}, u32[]{:S(2)}) collective-permute-start(bf16[5,8,8,768]{3,2,1,0:T(8,128)(2,1)S(1)} %collective-permute-done.5), channel_id=1, source_target_pairs={{0,1},{1,0},{2,3},{3,2},{4,5},{5,4},{6,7},{7,6},{8,9},{9,8},{10,11... | collective-permute-start | bytes 1474568 | tf_op jit(solution)/shard_map/ppermute | solution.py:450
  39.7 3.7 %collective-permute-start.6 = (bf16[320,768]{1,0:T(8,128)(2,1)S(1)}, bf16[320,768]{1,0:T(8,128)(2,1)S(1)}, u32[]{:S(2)}, u32[]{:S(2)}) collective-permute-start(bf16[320,768]{1,0:T(8,128)(2,1)S(1)} %collective-permute-done.2.rest_0_), channel_id=1, source_target_pairs={{0,1},{1,0},{2,3},{3,2},{4,5},{5,4},{6,7},{7,6},{8,9},{9,8},{10,11... | collective-permute-start | bytes 1474568 | tf_op jit(solution)/shard_map/ppermute | solution.py:450
  40.4 3.1 %copy-start.12 = (bf16[192,640]{1,0:T(8,128)(2,1)}, bf16[192,640]{1,0:T(8,128)(2,1)S(1)}, u32[]{:S(2)}) copy-start(bf16[192,640]{1,0:T(8,128)(2,1)S(1)} %collective-permute-done.10.rest_1_) | copy-start | bytes 737284
  42.6 0.9 copy-start.13
  42.6 7.1 %collective-permute-start.11 = (bf16[192,640]{1,0:T(8,128)(2,1)S(1)}, bf16[192,640]{1,0:T(8,128)(2,1)S(1)}, u32[]{:S(2)}, u32[]{:S(2)}) collective-permute-start(bf16[192,640]{1,0:T(8,128)(2,1)S(1)} %collective-permute-done.10.rest_1_), channel_id=1, source_target_pairs={{0,4},{4,0},{8,12},{12,8},{1,5},{5,1},{9,13},{13,9},{2,6},{6,2},{1... | collective-permute-start | bytes 737288 | tf_op jit(solution)/shard_map/ppermute | solution.py:453
  47.8 14.2 %collective-permute-start.13 = (bf16[2,192,640]{2,1,0:T(8,128)(2,1)S(1)}, bf16[2,192,640]{2,1,0:T(8,128)(2,1)S(1)}, u32[]{:S(2)}, u32[]{:S(2)}) collective-permute-start(bf16[2,192,640]{2,1,0:T(8,128)(2,1)S(1)} %get-tuple-element.66), channel_id=1, source_target_pairs={{0,4},{4,0},{8,12},{12,8},{1,5},{5,1},{9,13},{13,9},{2,6},{6,2},{1... | collective-permute-start | bytes 1474568 | tf_op jit(solution)/shard_map/ppermute | solution.py:453
  56.6 19.6 %collective-permute-start.12 = (bf16[2,192,640]{2,1,0:T(8,128)(2,1)S(1)}, bf16[2,192,640]{2,1,0:T(8,128)(2,1)S(1)}, u32[]{:S(2)}, u32[]{:S(2)}) collective-permute-start(bf16[2,192,640]{2,1,0:T(8,128)(2,1)S(1)} %get-tuple-element.64), channel_id=1, source_target_pairs={{0,4},{4,0},{8,12},{12,8},{1,5},{5,1},{9,13},{13,9},{2,6},{6,2},{1... | collective-permute-start | bytes 1474568 | tf_op jit(solution)/shard_map/ppermute | solution.py:453
  62.1 14.1 %collective-permute-start.14 = (bf16[192,640]{1,0:T(8,128)(2,1)S(1)}, bf16[192,640]{1,0:T(8,128)(2,1)S(1)}, u32[]{:S(2)}, u32[]{:S(2)}) collective-permute-start(bf16[192,640]{1,0:T(8,128)(2,1)S(1)} %fusion.4), channel_id=1, source_target_pairs={{0,8},{4,12},{8,0},{12,4},{1,9},{5,13},{9,1},{13,5},{2,10},{6,14},... | collective-permute-start | bytes 737288 | tf_op jit(solution)/shard_map/ppermute | solution.py:453
  78.2 2.6 %collective-permute-start.15 = (bf16[2,320,768]{2,1,0:T(8,128)(2,1)S(1)}, bf16[2,320,768]{2,1,0:T(8,128)(2,1)S(1)}, u32[]{:S(2)}, u32[]{:S(2)}) collective-permute-start(bf16[2,320,768]{2,1,0:T(8,128)(2,1)S(1)} %get-tuple-element.69), channel_id=1, source_target_pairs={{0,1},{1,0},{2,3},{3,2},{4,5},{5,4},{6,7},{7,6},{8,9},{9,8},{10,11... | collective-permute-start | bytes 2949128 | tf_op jit(solution)/shard_map/ppermute | solution.py:450
  78.2 14.6 %collective-permute-start.16 = (bf16[192,640]{1,0:T(8,128)(2,1)S(1)}, bf16[192,640]{1,0:T(8,128)(2,1)}, u32[]{:S(2)}, u32[]{:S(2)}) collective-permute-start(bf16[192,640]{1,0:T(8,128)(2,1)S(1)} %fusion.3), channel_id=1, source_target_pairs={{0,8},{4,12},{8,0},{12,4},{1,9},{5,13},{9,1},{13,5},{2,10},{6,14},... | collective-permute-start | bytes 737288 | tf_op jit(solution)/shard_map/ppermute | solution.py:453
  81.0 14.1 %collective-permute-start.17 = (bf16[320,768]{1,0:T(8,128)(2,1)S(1)}, bf16[320,768]{1,0:T(8,128)(2,1)S(1)}, u32[]{:S(2)}, u32[]{:S(2)}) collective-permute-start(bf16[320,768]{1,0:T(8,128)(2,1)S(1)} %get-tuple-element.78), channel_id=1, source_target_pairs={{0,2},{2,0},{1,3},{3,1},{4,6},{6,4},{5,7},{7,5},{8,10},{10,8},{9,1... | collective-permute-start | bytes 1474568 | tf_op jit(solution)/shard_map/ppermute | solution.py:447
  81.2 20.0 %collective-permute-start.20 = (bf16[192,640]{1,0:T(8,128)(2,1)S(1)}, bf16[192,640]{1,0:T(8,128)(2,1)S(1)}, u32[]{:S(2)}, u32[]{:S(2)}) collective-permute-start(bf16[192,640]{1,0:T(8,128)(2,1)S(1)} %fusion.2), channel_id=1, source_target_pairs={{0,2},{2,0},{1,3},{3,1},{4,6},{6,4},{5,7},{7,5},{8,10},{10,8},{9,1... | collective-permute-start | bytes 737288 | tf_op jit(solution)/shard_map/ppermute | solution.py:447
  93.9 11.0 %collective-permute-start.19 = (bf16[192,640]{1,0:T(8,128)(2,1)S(1)}, bf16[192,640]{1,0:T(8,128)(2,1)S(1)}, u32[]{:S(2)}, u32[]{:S(2)}) collective-permute-start(bf16[192,640]{1,0:T(8,128)(2,1)S(1)} %fusion.1), channel_id=1, source_target_pairs={{0,2},{2,0},{1,3},{3,1},{4,6},{6,4},{5,7},{7,5},{8,10},{10,8},{9,1... | collective-permute-start | bytes 737288 | tf_op jit(solution)/shard_map/ppermute | solution.py:447
  101.1 1.9 %collective-permute-start.18 = (bf16[5,8,8,768]{3,2,1,0:T(8,128)(2,1)S(1)}, bf16[5,8,8,768]{3,2,1,0:T(8,128)(2,1)S(1)}, u32[]{:S(2)}, u32[]{:S(2)}) collective-permute-start(bf16[5,8,8,768]{3,2,1,0:T(8,128)(2,1)S(1)} %norm_conv_back.1), channel_id=1, source_target_pairs={{0,1},{1,0},{2,3},{3,2},{4,5},{5,4},{6,7},{7,6},{8,9},{9,8},{10,11... | collective-permute-start | bytes 1474568 | tf_op jit(solution)/shard_map/ppermute | solution.py:450

commit v5 on v4

--- a/solution.py
+++ b/solution.py
@@ -213,7 +213,7 @@
 
 
 def sorted_pieces(pieces):
-    apart = tuple(k < len(pieces) - 1 for k in range(len(pieces)))
+    apart = tuple(False for _ in pieces)
     pieces = [(in_hbm if outside else in_vmem)(piece)[0] for outside, piece in zip(apart, pieces)]
     return apart, pieces, [APART if outside else WHOLE for outside in apart]
 

time: 106 us -> 106 us (level)
  waiting for transfers between devices: 39.1 us -> 42.1 us
  starting transfers between devices: 26.5 us -> 23.7 us
    ppermute x10, waiting for transfers between devices: 36.2 us -> 39.2 us  [meet(): return lax.ppermute(value, 'seq', [(i, i ^ step) for i in range(n_seq)])]
    ppermute x10, starting transfers between devices: 17.9 us -> 15 us  [meet(): return lax.ppermute(value, 'seq', [(i, i ^ step) for i in range(n_seq)])]
  transfers between devices with their start and end apart: 21 -> 21, of which waited for: 11 -> 11; matrix products, arithmetic and copies ran while one was open for 6% -> 6% of each run, Pallas kernels for 26% -> 25%
where the time goes in v5:
time: 106 us
  waiting for transfers between devices  42.1 us (40%)
  Pallas kernels  28.4 us (27%)
  starting transfers between devices  23.7 us (22%)
  other arithmetic  6.91 us (7%)
  local copies, waits for them, and re-layouts  2.87 us (3%)
  between operations  1.61 us (2%)
    ppermute x10, waiting for transfers between devices, meet(): return lax.ppermute(value, 'seq', [(i, i ^ step) for i in range(n_seq)])  39.2 us
    ppermute x10, starting transfers between devices, meet(): return lax.ppermute(value, 'seq', [(i, i ^ step) for i in range(n_seq)])  15 us
    ppermute x6, starting transfers between devices, over_pair(): return lax.ppermute(value, 'dp', pair)  7.96 us
    pallas_call x1, Pallas kernels, tail(): pl.pallas_call(tail_kernel, name='norm_conv_back', out_shape=jax.ShapeDty...  5.93 us
    pallas_call x1, Pallas kernels, front(): pl.pallas_call(front_kernel, name='conv_norm', out_shape=(pltpu.HBM((rows...  5.46 us
    pallas_call x1, Pallas kernels, down(): pl.pallas_call(functools.partial(down_kernel, apart), name='hidden_grad',...  4.69 us
    pallas_call x1, Pallas kernels, up_next(): pl.pallas_call(up_next_kernel, name='hidden_next_and_down_grad', out_shap...  4.36 us
    pallas_call x1, Pallas kernels, up(): pl.pallas_call(functools.partial(up_kernel, apart), name='hidden_own', ou...  4.17 us
  transfers between devices with their start and end apart: 21, of which 11 were waited for; matrix products, arithmetic and copies ran while one was open for 6% of the time, Pallas kernels for 25%

profile of v5, /device:TPU:0, one launch (start us, length us, event | category | flops | bytes accessed | tf_op | source)
XLA Modules:
  0.0 105.6 jit_solution(13884570734962974907)
XLA Ops:
  0.7 0.8 slice_bitcast_fusion.1
  1.5 0.7 pad_slice_fusion
  2.2 1.0 constant_dynamic-slice_fusion.1
  3.3 4.1 %collective-permute-start.1 = (bf16[208,640]{1,0:T(8,128)(2,1)S(1)}, bf16[208,640]{1,0:T(8,128)(2,1)S(1)}, u32[]{:S(2)}, u32[]{:S(2)}) collective-permute-start(bf16[208,640]{1,0:T(8,128)(2,1)S(1)} %pad_maximum_fusion.1), channel_id=1, source_target_pairs={{0,8},{4,12},{8,0},{12,4},{1,9},{5,13},{9,1},{13,5},{2,10},{6,14},... | collective-permute-start | bytes 798728 | tf_op jit(solution)/shard_map/ppermute | solution.py:453
  7.4 1.6 %collective-permute-start = (bf16[208,640]{1,0:T(8,128)(2,1)S(1)}, bf16[208,640]{1,0:T(8,128)(2,1)S(1)}, u32[]{:S(2)}, u32[]{:S(2)}) collective-permute-start(bf16[208,640]{1,0:T(8,128)(2,1)S(1)} %pad_maximum_fusion.1), channel_id=1, source_target_pairs={{0,4},{4,0},{8,12},{12,8},{1,5},{5,1},{9,13},{13,9},{2,6},{6,2},{1... | collective-permute-start | bytes 798728 | tf_op jit(solution)/shard_map/ppermute | solution.py:453
  9.6 0.1 fusion.25
  9.7 1.1 %dynamic-slice_multiply_fusion = bf16[5,8,8,768]{3,2,1,0:T(8,128)(2,1)S(1)} fusion(bf16[10,8,8,768]{3,2,1,0:T(8,128)(2,1)} %token_in.1, s32[]{:T(128)S(6)} %select_n.140, bf16[5]{0:T(256)(128)(2,1)S(1)} %get-tuple-element.109), kind=kLoop, calls=%fused_computation.16 | loop fusion | flops 245760 | bytes 983054 | tf_op jit(solution)/shard_map/mul | solution.py:491
  10.8 1.6 %collective-permute-start.5 = (bf16[5,8,8,768]{3,2,1,0:T(8,128)(2,1)S(1)}, bf16[5,8,8,768]{3,2,1,0:T(8,128)(2,1)S(1)}, u32[]{:S(2)}, u32[]{:S(2)}) collective-permute-start(bf16[5,8,8,768]{3,2,1,0:T(8,128)(2,1)S(1)} %dynamic-slice_multiply_fusion), channel_id=1, source_target_pairs={{0,2},{2,0},{1,3},{3,1},{4,6},{6,4},{5,7},{7,5},{8,10},{10,8},{9,1... | collective-permute-start | bytes 1474568 | tf_op jit(solution)/shard_map/ppermute | solution.py:447
  12.4 5.5 %conv_norm.1 = (bf16[320,768]{1,0:T(8,128)(2,1)}, f32[320,768]{1,0:T(8,128)}, f32[320,128]{1,0:T(8,128)}) custom-call(s32[1]{0:T(128)} %bitcast.base_ref, bf16[10,8,8,768]{3,2,1,0:T(8,128)(2,1)S(1)} %copy-done, f32[7,7,768]{2,1,0:T(8,128)S(1)} %copy-done.1, f32[768]{0:T(1024)S(1)} %copy-done.2, f32[768]{0:T(1024)S(1)} %copy-done.4, f32[768]{0:T(1024)S(1)} %copy-done.3), custom_call_target="tpu_custom_call" | custom-call | flops 10737418240 | bytes 4194304 | tf_op jit(solution)/shard_map/conv_norm/pallas_call | solution.py:110
  17.9 1.7 %collective-permute-done.1.rest_1_ = bf16[208,640]{1,0:T(8,128)(2,1)S(1)} collective-permute-done((bf16[208,640]{1,0:T(8,128)(2,1)S(1)}, bf16[208,640]{1,0:T(8,128)(2,1)S(1)}, u32[]{:S(2)}, u32[]{:S(2)}) %collective-permute-start.1) | collective-permute-done | bytes 266272 | tf_op jit(solution)/shard_map/ppermute | solution.py:453
  19.6 0.2 collective-permute-done.rest_0_
  19.8 1.5 %collective-permute-start.3 = (bf16[208,640]{1,0:T(8,128)(2,1)S(1)}, bf16[208,640]{1,0:T(8,128)(2,1)S(1)}, u32[]{:S(2)}, u32[]{:S(2)}) collective-permute-start(bf16[208,640]{1,0:T(8,128)(2,1)S(1)} %collective-permute-done.1.rest_1_), channel_id=1, source_target_pairs={{0,4},{4,0},{8,12},{12,8},{1,5},{5,1},{9,13},{13,9},{2,6},{6,2},{1... | collective-permute-start | bytes 798728 | tf_op jit(solution)/shard_map/ppermute | solution.py:453
  21.4 1.5 %collective-permute-start.2 = (bf16[320,768]{1,0:T(8,128)(2,1)}, bf16[320,768]{1,0:T(8,128)(2,1)S(1)}, u32[]{:S(2)}, u32[]{:S(2)}) collective-permute-start(bf16[320,768]{1,0:T(8,128)(2,1)} %get-tuple-element.43.own_ref), channel_id=1, source_target_pairs={{0,2},{2,0},{1,3},{3,1},{4,6},{6,4},{5,7},{7,5},{8,10},{10,8},{9,1... | collective-permute-start | bytes 1474568 | tf_op jit(solution)/shard_map/ppermute | solution.py:447
  23.0 2.4 %collective-permute-start.10 = (bf16[192,640]{1,0:T(8,128)(2,1)S(1)}, bf16[192,640]{1,0:T(8,128)(2,1)S(1)}, u32[]{:S(2)}, u32[]{:S(2)}) collective-permute-start(bf16[192,640]{1,0:T(8,128)(2,1)S(1)} %constant_dynamic-slice_fusion), channel_id=1, source_target_pairs={{0,8},{4,12},{8,0},{12,4},{1,9},{5,13},{9,1},{13,5},{2,10},{6,14},... | collective-permute-start | bytes 737288 | tf_op jit(solution)/shard_map/ppermute | solution.py:453
  25.4 6.9 %collective-permute-done.3.rest_2_ = bf16[208,640]{1,0:T(8,128)(2,1)S(1)} collective-permute-done((bf16[208,640]{1,0:T(8,128)(2,1)S(1)}, bf16[208,640]{1,0:T(8,128)(2,1)S(1)}, u32[]{:S(2)}, u32[]{:S(2)}) %collective-permute-start.3) | collective-permute-done | bytes 266272 | tf_op jit(solution)/shard_map/ppermute | solution.py:453
  32.5 0.1 maximum_multiply_fusion
  32.6 2.6 %collective-permute-start.7 = (bf16[10,768]{1,0:T(8,128)(2,1)S(1)}, bf16[10,768]{1,0:T(8,128)(2,1)S(1)}, u32[]{:S(2)}, u32[]{:S(2)}) collective-permute-start(bf16[10,768]{1,0:T(8,128)(2,1)S(1)} %maximum_multiply_fusion), channel_id=1, source_target_pairs={{0,2},{2,0},{1,3},{3,1},{4,6},{6,4},{5,7},{7,5},{8,10},{10,8},{9,1... | collective-permute-start | bytes 46088 | tf_op jit(solution)/shard_map/ppermute | solution.py:447
  35.2 4.2 %hidden_own.1 = (bf16[640,640]{1,0:T(8,128)(2,1)S(1)}, f32[640,640]{1,0:T(8,128)S(1)}, bf16[768,640]{1,0:T(8,128)(2,1)S(1)}, bf16[640,768]{1,0:T(8,128)(2,1)S(1)}) custom-call(s32[6]{0:T(128)S(1)} %pad_add_fusion.place_ref, bf16[320,768]{1,0:T(8,128)(2,1)} %get-tuple-element.43.own_ref, bf16[320,768]{1,0:T(8,128)(2,1)} %copy-done.9, ...), custom_call_target="tpu_custom_call" | custom-call | flops 10737418240 | bytes 4194304 | tf_op jit(solution)/shard_map/hidden_own/pallas_call | solution.py:225
  39.4 0.6 collective-permute-start.6
  40.0 2.5 %collective-permute-done.9.rest_0_ = bf16[192,640]{1,0:T(8,128)(2,1)S(1)} collective-permute-done((bf16[192,640]{1,0:T(8,128)(2,1)S(1)}, bf16[192,640]{1,0:T(8,128)(2,1)S(1)}, u32[]{:S(2)}, u32[]{:S(2)}) %collective-permute-start.9) | collective-permute-done | bytes 245792 | tf_op jit(solution)/shard_map/ppermute | solution.py:453
  42.5 0.3 collective-permute-start.11
  42.8 0.6 multiply_convert_fusion
  43.4 4.4 %hidden_next_and_down_grad.1 = (bf16[2,192,640]{2,1,0:T(8,128)(2,1)S(1)}, bf16[2,192,640]{2,1,0:T(8,128)(2,1)S(1)}, f32[640,640]{1,0:T(8,128)S(1)}, bf16[640,768]{1,0:T(8,128)(2,1)S(1)}, bf16[1280,768]{1,0:T(8,128)(2,1)S(1)}) custom-call(s32[1]{0:T(128)} %bitcast.6.seq_ref, bf16[320,768]{1,0:T(8,128)(2,1)S(1)} %collective-permute-done.2.rest_0_, ...), custom_call_target="tpu_custom_call" | custom-call | flops 10737418240 | bytes 4194304 | tf_op jit(solution)/shard_map/hidden_next_and_down_grad/pallas_call | solution.py:246
  47.7 1.8 %collective-permute-start.13 = (bf16[2,192,640]{2,1,0:T(8,128)(2,1)S(1)}, bf16[2,192,640]{2,1,0:T(8,128)(2,1)S(1)}, u32[]{:S(2)}, u32[]{:S(2)}) collective-permute-start(bf16[2,192,640]{2,1,0:T(8,128)(2,1)S(1)} %get-tuple-element.66), channel_id=1, source_target_pairs={{0,4},{4,0},{8,12},{12,8},{1,5},{5,1},{9,13},{13,9},{2,6},{6,2},{1... | collective-permute-start | bytes 1474568 | tf_op jit(solution)/shard_map/ppermute | solution.py:453
  49.6 4.7 %hidden_grad.1.grad_ref = bf16[1280,640]{1,0:T(8,128)(2,1)S(1)} custom-call(s32[6]{0:T(128)S(1)} %pad_add_fusion.place_ref, bf16[1280,768]{1,0:T(8,128)(2,1)S(1)} %get-tuple-element.54.branch_ref, f32[640,640]{1,0:T(8,128)S(1)} %get-tuple-element.55.slope_own, f32[640,640]{1,0:T(8,128)S(1)} %get-tuple-element.56.slope_next, bf16[192,1280]{1,0:T(8,128)(2,1)} %local.3, ...), custom_call_target="tpu_custom_call" | custom-call | flops 10737418240 | bytes 4194304 | tf_op jit(solution)/shard_map/hidden_grad/pallas_call | solution.py:286
  54.3 2.0 %up_grad.1 = (bf16[2,192,640]{2,1,0:T(8,128)(2,1)S(1)}, bf16[2,192,640]{2,1,0:T(8,128)(2,1)S(1)}) custom-call(s32[1]{0:T(128)} %bitcast.6.seq_ref, bf16[640,768]{1,0:T(8,128)(2,1)S(1)} %get-tuple-element.61.own_ref, bf16[640,768]{1,0:T(8,128)(2,1)S(1)} %get-tuple-element.62.next_ref, bf16[1280,640]{1,0:T(8,128)(2,1)S(1)} %hidden_grad.1.grad_ref), custom_call_target="tpu_custom_call" | custom-call | flops 10737418240 | bytes 4194304 | tf_op jit(solution)/shard_map/up_grad/pallas_call | solution.py:309
  56.3 0.5 collective-permute-start.12
  56.8 7.8 %collective-permute-done.13 = bf16[2,192,640]{2,1,0:T(8,128)(2,1)S(1)} collective-permute-done((bf16[2,192,640]{2,1,0:T(8,128)(2,1)S(1)}, bf16[2,192,640]{2,1,0:T(8,128)(2,1)S(1)}, u32[]{:S(2)}, u32[]{:S(2)}) %collective-permute-start.13) | collective-permute-done | bytes 491552 | tf_op jit(solution)/shard_map/ppermute | solution.py:453
  64.7 0.6 collective-permute-start.14
  65.3 10.5 %collective-permute-done.12 = bf16[2,192,640]{2,1,0:T(8,128)(2,1)S(1)} collective-permute-done((bf16[2,192,640]{2,1,0:T(8,128)(2,1)S(1)}, bf16[2,192,640]{2,1,0:T(8,128)(2,1)S(1)}, u32[]{:S(2)}, u32[]{:S(2)}) %collective-permute-start.12) | collective-permute-done | bytes 491552 | tf_op jit(solution)/shard_map/ppermute | solution.py:453
  75.9 0.1 fusion.2
  76.0 1.8 %normed_grad.1 = (bf16[2,320,768]{2,1,0:T(8,128)(2,1)S(1)}, bf16[2,320,768]{2,1,0:T(8,128)(2,1)S(1)}) custom-call(bf16[1280,640]{1,0:T(8,128)(2,1)S(1)} %hidden_grad.1.grad_ref, bf16[768,640]{1,0:T(8,128)(2,1)S(1)} %get-tuple-element.53.rest_7_.weight_ref), custom_call_target="tpu_custom_call" | custom-call | flops 10737418240 | bytes 4194304 | tf_op jit(solution)/shard_map/normed_grad/pallas_call | solution.py:331
  77.9 2.2 %collective-permute-start.16 = (bf16[192,640]{1,0:T(8,128)(2,1)S(1)}, bf16[192,640]{1,0:T(8,128)(2,1)}, u32[]{:S(2)}, u32[]{:S(2)}) collective-permute-start(bf16[192,640]{1,0:T(8,128)(2,1)S(1)} %fusion.3), channel_id=1, source_target_pairs={{0,8},{4,12},{8,0},{12,4},{1,9},{5,13},{9,1},{13,5},{2,10},{6,14},... | collective-permute-start | bytes 737288 | tf_op jit(solution)/shard_map/ppermute | solution.py:453
  80.1 0.3 collective-permute-done.15
  80.4 0.2 fusion
  80.7 0.2 collective-permute-start.17
  80.9 2.0 %collective-permute-start.20 = (bf16[192,640]{1,0:T(8,128)(2,1)S(1)}, bf16[192,640]{1,0:T(8,128)(2,1)S(1)}, u32[]{:S(2)}, u32[]{:S(2)}) collective-permute-start(bf16[192,640]{1,0:T(8,128)(2,1)S(1)} %fusion.2), channel_id=1, source_target_pairs={{0,2},{2,0},{1,3},{3,1},{4,6},{6,4},{5,7},{7,5},{8,10},{10,8},{9,1... | collective-permute-start | bytes 737288 | tf_op jit(solution)/shard_map/ppermute | solution.py:447
  82.8 9.7 %collective-permute-done.16 = bf16[192,640]{1,0:T(8,128)(2,1)} collective-permute-done((bf16[192,640]{1,0:T(8,128)(2,1)S(1)}, bf16[192,640]{1,0:T(8,128)(2,1)}, u32[]{:S(2)}, u32[]{:S(2)}) %collective-permute-start.16) | collective-permute-done | bytes 245792 | tf_op jit(solution)/shard_map/ppermute | solution.py:453
  92.5 1.1 %fusion.1 = bf16[192,640]{1,0:T(8,128)(2,1)S(1)} fusion(bf16[192,640]{1,0:T(8,128)(2,1)} %collective-permute-done.16, bf16[2,192,640]{2,1,0:T(8,128)(2,1)S(1)} %collective-permute-done.12, bf16[2,192,640]{2,1,0:T(8,128)(2,1)S(1)} %get-tuple-element.63), kind=kLoop, calls=%fused_computation.11 | loop fusion | flops 737280 | bytes 983040 | tf_op jit(solution)/shard_map/convert_element_type | solution.py:549
  93.6 0.2 collective-permute-start.19
  93.8 1.0 collective-permute-done.17.far_ref
  94.8 5.9 %norm_conv_back.1 = bf16[5,8,8,768]{3,2,1,0:T(8,128)(2,1)S(1)} custom-call(s32[1]{0:T(128)} %bitcast.base_ref, s32[1]{0:T(128)} %copy.15.live_ref, f32[320,768]{1,0:T(8,128)} %get-tuple-element.40.normal_in, f32[320,128]{1,0:T(8,128)} %get-tuple-element.41.inv_in, bf16[10,8,8,768]{3,2,1,0:T(8,128)(2,1)} %token_in.1, f32[7,7,768]{2,1,0:T(8,128)} %taps_in.1, ...), custom_call_target="tpu_custom_call" | custom-call | flops 10737418240 | bytes 4194304 | tf_op jit(solution)/shard_map/norm_conv_back/pallas_call | solution.py:396
  100.9 1.0 maximum_convert_fusion
  101.9 0.8 collective-permute-done.18
  102.7 0.1 broadcast_select_fusion.1
  102.8 1.0 pad_maximum_fusion
  103.8 0.7 collective-permute-done.19
  104.6 1.0 maximum_convert_fusion.1
  (54 shorter events, 1.0 us)
Async XLA Ops:
  0.6 11.8 %copy-start.4 = (f32[768]{0:T(1024)S(1)}, f32[768]{0:T(1024)}, u32[]{:S(2)}) copy-start(f32[768]{0:T(1024)} %gain_ref.3) | copy-start | bytes 9220
  0.6 11.8 %copy-start.1 = (f32[7,7,768]{2,1,0:T(8,128)S(1)}, f32[7,7,768]{2,1,0:T(8,128)}, u32[]{:S(2)}) copy-start(f32[7,7,768]{2,1,0:T(8,128)} %taps_in.1) | copy-start | bytes 451588
  0.7 11.8 %copy-start.3 = (f32[768]{0:T(1024)S(1)}, f32[768]{0:T(1024)}, u32[]{:S(2)}) copy-start(f32[768]{0:T(1024)} %shift_ref.1) | copy-start | bytes 9220
  0.7 11.7 %copy-start.2 = (f32[768]{0:T(1024)S(1)}, f32[768]{0:T(1024)}, u32[]{:S(2)}) copy-start(f32[768]{0:T(1024)} %bias_ref.1) | copy-start | bytes 9220
  0.7 11.7 %copy-start = (bf16[10,8,8,768]{3,2,1,0:T(8,128)(2,1)S(1)}, bf16[10,8,8,768]{3,2,1,0:T(8,128)(2,1)}, u32[]{:S(2)}) copy-start(bf16[10,8,8,768]{3,2,1,0:T(8,128)(2,1)} %tiles_ref.1) | copy-start | bytes 2949124
  3.3 16.3 %collective-permute-start.1 = (bf16[208,640]{1,0:T(8,128)(2,1)S(1)}, bf16[208,640]{1,0:T(8,128)(2,1)S(1)}, u32[]{:S(2)}, u32[]{:S(2)}) collective-permute-start(bf16[208,640]{1,0:T(8,128)(2,1)S(1)} %pad_maximum_fusion.1), channel_id=1, source_target_pairs={{0,8},{4,12},{8,0},{12,4},{1,9},{5,13},{9,1},{13,5},{2,10},{6,14},... | collective-permute-start | bytes 798728 | tf_op jit(solution)/shard_map/ppermute | solution.py:453
  7.4 12.4 %collective-permute-start = (bf16[208,640]{1,0:T(8,128)(2,1)S(1)}, bf16[208,640]{1,0:T(8,128)(2,1)S(1)}, u32[]{:S(2)}, u32[]{:S(2)}) collective-permute-start(bf16[208,640]{1,0:T(8,128)(2,1)S(1)} %pad_maximum_fusion.1), channel_id=1, source_target_pairs={{0,4},{4,0},{8,12},{12,8},{1,5},{5,1},{9,13},{13,9},{2,6},{6,2},{1... | collective-permute-start | bytes 798728 | tf_op jit(solution)/shard_map/ppermute | solution.py:453
  10.8 14.5 %collective-permute-start.5 = (bf16[5,8,8,768]{3,2,1,0:T(8,128)(2,1)S(1)}, bf16[5,8,8,768]{3,2,1,0:T(8,128)(2,1)S(1)}, u32[]{:S(2)}, u32[]{:S(2)}) collective-permute-start(bf16[5,8,8,768]{3,2,1,0:T(8,128)(2,1)S(1)} %dynamic-slice_multiply_fusion), channel_id=1, source_target_pairs={{0,2},{2,0},{1,3},{3,1},{4,6},{6,4},{5,7},{7,5},{8,10},{10,8},{9,1... | collective-permute-start | bytes 1474568 | tf_op jit(solution)/shard_map/ppermute | solution.py:447
  12.4 8.9 %copy-start.8 = (f32[1280]{0:T(1024)S(1)}, f32[1280]{0:T(1024)}, u32[]{:S(2)}) copy-start(f32[1280]{0:T(1024)} %param.21) | copy-start | bytes 15364
  12.4 10.5 %copy-start.6 = (bf16[192,1280]{1,0:T(8,128)(2,1)S(1)}, bf16[192,1280]{1,0:T(8,128)(2,1)}, u32[]{:S(2)}) copy-start(bf16[192,1280]{1,0:T(8,128)(2,1)} %local.3) | copy-start | bytes 1474564
  19.8 12.5 %collective-permute-start.4 = (bf16[320,768]{1,0:T(8,128)(2,1)}, bf16[320,768]{1,0:T(8,128)(2,1)S(1)}, u32[]{:S(2)}, u32[]{:S(2)}) collective-permute-start(bf16[320,768]{1,0:T(8,128)(2,1)} %get-tuple-element.43.own_ref), channel_id=1, source_target_pairs={{0,1},{1,0},{2,3},{3,2},{4,5},{5,4},{6,7},{7,6},{8,9},{9,8},{10,11... | collective-permute-start | bytes 1474568 | tf_op jit(solution)/shard_map/ppermute | solution.py:450
  19.8 12.5 %collective-permute-start.3 = (bf16[208,640]{1,0:T(8,128)(2,1)S(1)}, bf16[208,640]{1,0:T(8,128)(2,1)S(1)}, u32[]{:S(2)}, u32[]{:S(2)}) collective-permute-start(bf16[208,640]{1,0:T(8,128)(2,1)S(1)} %collective-permute-done.1.rest_1_), channel_id=1, source_target_pairs={{0,4},{4,0},{8,12},{12,8},{1,5},{5,1},{9,13},{13,9},{2,6},{6,2},{1... | collective-permute-start | bytes 798728 | tf_op jit(solution)/shard_map/ppermute | solution.py:453
  21.4 18.0 %collective-permute-start.2 = (bf16[320,768]{1,0:T(8,128)(2,1)}, bf16[320,768]{1,0:T(8,128)(2,1)S(1)}, u32[]{:S(2)}, u32[]{:S(2)}) collective-permute-start(bf16[320,768]{1,0:T(8,128)(2,1)} %get-tuple-element.43.own_ref), channel_id=1, source_target_pairs={{0,2},{2,0},{1,3},{3,1},{4,6},{6,4},{5,7},{7,5},{8,10},{10,8},{9,1... | collective-permute-start | bytes 1474568 | tf_op jit(solution)/shard_map/ppermute | solution.py:447
  23.0 17.1 %collective-permute-start.10 = (bf16[192,640]{1,0:T(8,128)(2,1)S(1)}, bf16[192,640]{1,0:T(8,128)(2,1)S(1)}, u32[]{:S(2)}, u32[]{:S(2)}) collective-permute-start(bf16[192,640]{1,0:T(8,128)(2,1)S(1)} %constant_dynamic-slice_fusion), channel_id=1, source_target_pairs={{0,8},{4,12},{8,0},{12,4},{1,9},{5,13},{9,1},{13,5},{2,10},{6,14},... | collective-permute-start | bytes 737288 | tf_op jit(solution)/shard_map/ppermute | solution.py:453
  32.3 2.9 %copy-start.9 = (bf16[320,768]{1,0:T(8,128)(2,1)}, bf16[320,768]{1,0:T(8,128)(2,1)S(1)}, u32[]{:S(2)}) copy-start(bf16[320,768]{1,0:T(8,128)(2,1)S(1)} %collective-permute-done.4.core_ref) | copy-start | bytes 1474564
  32.6 10.2 %copy-start.5 = (bf16[10,8,8,768]{3,2,1,0:T(8,128)(2,1)S(1)}, bf16[10,8,8,768]{3,2,1,0:T(8,128)(2,1)}, u32[]{:S(2)}) copy-start(bf16[10,8,8,768]{3,2,1,0:T(8,128)(2,1)} %token_in.1) | copy-start | bytes 2949124
  32.6 10.2 %copy-start.7 = (f32[768]{0:T(1024)S(1)}, f32[768]{0:T(1024)}, u32[]{:S(2)}) copy-start(f32[768]{0:T(1024)} %param.23) | copy-start | bytes 9220
  32.6 7.4 %collective-permute-start.7 = (bf16[10,768]{1,0:T(8,128)(2,1)S(1)}, bf16[10,768]{1,0:T(8,128)(2,1)S(1)}, u32[]{:S(2)}, u32[]{:S(2)}) collective-permute-start(bf16[10,768]{1,0:T(8,128)(2,1)S(1)} %maximum_multiply_fusion), channel_id=1, source_target_pairs={{0,2},{2,0},{1,3},{3,1},{4,6},{6,4},{5,7},{7,5},{8,10},{10,8},{9,1... | collective-permute-start | bytes 46088 | tf_op jit(solution)/shard_map/ppermute | solution.py:447
  35.2 7.3 %collective-permute-start.9 = (bf16[192,640]{1,0:T(8,128)(2,1)S(1)}, bf16[192,640]{1,0:T(8,128)(2,1)S(1)}, u32[]{:S(2)}, u32[]{:S(2)}) collective-permute-start(bf16[192,640]{1,0:T(8,128)(2,1)S(1)} %constant_dynamic-slice_fusion), channel_id=1, source_target_pairs={{0,4},{4,0},{8,12},{12,8},{1,5},{5,1},{9,13},{13,9},{2,6},{6,2},{1... | collective-permute-start | bytes 737288 | tf_op jit(solution)/shard_map/ppermute | solution.py:453
  35.2 7.6 %collective-permute-start.8 = (bf16[5,8,8,768]{3,2,1,0:T(8,128)(2,1)S(1)}, bf16[5,8,8,768]{3,2,1,0:T(8,128)(2,1)S(1)}, u32[]{:S(2)}, u32[]{:S(2)}) collective-permute-start(bf16[5,8,8,768]{3,2,1,0:T(8,128)(2,1)S(1)} %collective-permute-done.5), channel_id=1, source_target_pairs={{0,1},{1,0},{2,3},{3,2},{4,5},{5,4},{6,7},{7,6},{8,9},{9,8},{10,11... | collective-permute-start | bytes 1474568 | tf_op jit(solution)/shard_map/ppermute | solution.py:450
  39.4 4.0 %collective-permute-start.6 = (bf16[320,768]{1,0:T(8,128)(2,1)S(1)}, bf16[320,768]{1,0:T(8,128)(2,1)S(1)}, u32[]{:S(2)}, u32[]{:S(2)}) collective-permute-start(bf16[320,768]{1,0:T(8,128)(2,1)S(1)} %collective-permute-done.2.rest_0_), channel_id=1, source_target_pairs={{0,1},{1,0},{2,3},{3,2},{4,5},{5,4},{6,7},{7,6},{8,9},{9,8},{10,11... | collective-permute-start | bytes 1474568 | tf_op jit(solution)/shard_map/ppermute | solution.py:450
  42.5 7.1 %collective-permute-start.11 = (bf16[192,640]{1,0:T(8,128)(2,1)S(1)}, bf16[192,640]{1,0:T(8,128)(2,1)S(1)}, u32[]{:S(2)}, u32[]{:S(2)}) collective-permute-start(bf16[192,640]{1,0:T(8,128)(2,1)S(1)} %collective-permute-done.10.rest_1_), channel_id=1, source_target_pairs={{0,4},{4,0},{8,12},{12,8},{1,5},{5,1},{9,13},{13,9},{2,6},{6,2},{1... | collective-permute-start | bytes 737288 | tf_op jit(solution)/shard_map/ppermute | solution.py:453
  47.7 16.9 %collective-permute-start.13 = (bf16[2,192,640]{2,1,0:T(8,128)(2,1)S(1)}, bf16[2,192,640]{2,1,0:T(8,128)(2,1)S(1)}, u32[]{:S(2)}, u32[]{:S(2)}) collective-permute-start(bf16[2,192,640]{2,1,0:T(8,128)(2,1)S(1)} %get-tuple-element.66), channel_id=1, source_target_pairs={{0,4},{4,0},{8,12},{12,8},{1,5},{5,1},{9,13},{13,9},{2,6},{6,2},{1... | collective-permute-start | bytes 1474568 | tf_op jit(solution)/shard_map/ppermute | solution.py:453
  56.3 19.5 %collective-permute-start.12 = (bf16[2,192,640]{2,1,0:T(8,128)(2,1)S(1)}, bf16[2,192,640]{2,1,0:T(8,128)(2,1)S(1)}, u32[]{:S(2)}, u32[]{:S(2)}) collective-permute-start(bf16[2,192,640]{2,1,0:T(8,128)(2,1)S(1)} %get-tuple-element.64), channel_id=1, source_target_pairs={{0,4},{4,0},{8,12},{12,8},{1,5},{5,1},{9,13},{13,9},{2,6},{6,2},{1... | collective-permute-start | bytes 1474568 | tf_op jit(solution)/shard_map/ppermute | solution.py:453
  64.7 11.2 %collective-permute-start.14 = (bf16[192,640]{1,0:T(8,128)(2,1)S(1)}, bf16[192,640]{1,0:T(8,128)(2,1)S(1)}, u32[]{:S(2)}, u32[]{:S(2)}) collective-permute-start(bf16[192,640]{1,0:T(8,128)(2,1)S(1)} %fusion.4), channel_id=1, source_target_pairs={{0,8},{4,12},{8,0},{12,4},{1,9},{5,13},{9,1},{13,5},{2,10},{6,14},... | collective-permute-start | bytes 737288 | tf_op jit(solution)/shard_map/ppermute | solution.py:453
  77.8 2.6 %collective-permute-start.15 = (bf16[2,320,768]{2,1,0:T(8,128)(2,1)S(1)}, bf16[2,320,768]{2,1,0:T(8,128)(2,1)S(1)}, u32[]{:S(2)}, u32[]{:S(2)}) collective-permute-start(bf16[2,320,768]{2,1,0:T(8,128)(2,1)S(1)} %get-tuple-element.69), channel_id=1, source_target_pairs={{0,1},{1,0},{2,3},{3,2},{4,5},{5,4},{6,7},{7,6},{8,9},{9,8},{10,11... | collective-permute-start | bytes 2949128 | tf_op jit(solution)/shard_map/ppermute | solution.py:450
  77.9 14.6 %collective-permute-start.16 = (bf16[192,640]{1,0:T(8,128)(2,1)S(1)}, bf16[192,640]{1,0:T(8,128)(2,1)}, u32[]{:S(2)}, u32[]{:S(2)}) collective-permute-start(bf16[192,640]{1,0:T(8,128)(2,1)S(1)} %fusion.3), channel_id=1, source_target_pairs={{0,8},{4,12},{8,0},{12,4},{1,9},{5,13},{9,1},{13,5},{2,10},{6,14},... | collective-permute-start | bytes 737288 | tf_op jit(solution)/shard_map/ppermute | solution.py:453
  80.7 14.1 %collective-permute-start.17 = (bf16[320,768]{1,0:T(8,128)(2,1)S(1)}, bf16[320,768]{1,0:T(8,128)(2,1)S(1)}, u32[]{:S(2)}, u32[]{:S(2)}) collective-permute-start(bf16[320,768]{1,0:T(8,128)(2,1)S(1)} %get-tuple-element.78), channel_id=1, source_target_pairs={{0,2},{2,0},{1,3},{3,1},{4,6},{6,4},{5,7},{7,5},{8,10},{10,8},{9,1... | collective-permute-start | bytes 1474568 | tf_op jit(solution)/shard_map/ppermute | solution.py:447
  80.9 19.9 %collective-permute-start.20 = (bf16[192,640]{1,0:T(8,128)(2,1)S(1)}, bf16[192,640]{1,0:T(8,128)(2,1)S(1)}, u32[]{:S(2)}, u32[]{:S(2)}) collective-permute-start(bf16[192,640]{1,0:T(8,128)(2,1)S(1)} %fusion.2), channel_id=1, source_target_pairs={{0,2},{2,0},{1,3},{3,1},{4,6},{6,4},{5,7},{7,5},{8,10},{10,8},{9,1... | collective-permute-start | bytes 737288 | tf_op jit(solution)/shard_map/ppermute | solution.py:447
  93.6 11.0 %collective-permute-start.19 = (bf16[192,640]{1,0:T(8,128)(2,1)S(1)}, bf16[192,640]{1,0:T(8,128)(2,1)S(1)}, u32[]{:S(2)}, u32[]{:S(2)}) collective-permute-start(bf16[192,640]{1,0:T(8,128)(2,1)S(1)} %fusion.1), channel_id=1, source_target_pairs={{0,2},{2,0},{1,3},{3,1},{4,6},{6,4},{5,7},{7,5},{8,10},{10,8},{9,1... | collective-permute-start | bytes 737288 | tf_op jit(solution)/shard_map/ppermute | solution.py:447
  100.7 1.9 %collective-permute-start.18 = (bf16[5,8,8,768]{3,2,1,0:T(8,128)(2,1)S(1)}, bf16[5,8,8,768]{3,2,1,0:T(8,128)(2,1)S(1)}, u32[]{:S(2)}, u32[]{:S(2)}) collective-permute-start(bf16[5,8,8,768]{3,2,1,0:T(8,128)(2,1)S(1)} %norm_conv_back.1), channel_id=1, source_target_pairs={{0,1},{1,0},{2,3},{3,2},{4,5},{5,4},{6,7},{7,6},{8,9},{9,8},{10,11... | collective-permute-start | bytes 1474568 | tf_op jit(solution)/shard_map/ppermute | solution.py:450
